TPU v7x, 512 devices: a whole 4x8x8 slice. The times are simulated.
512 devices in a mesh: px: 32 (over z, y_lo, core), pz: 16 (over x, y_hi).
Axes of the slice: x: 4, y: 8 (y_hi: 4, y_lo: 2; y = y_hi * 2 + y_lo), z: 8, core: 2. Of those that a mesh axis runs over, the one named last changes fastest.
Arguments:
- velocity: float32 [3, 64, 512, 256], P(None, 'pz', 'px'), may hold values from -6 to 6
- first_deriv: bfloat16 [512, 512], replicated, may hold values from -0.25 to 0.25
- second_deriv: bfloat16 [512, 512], replicated, may hold values from -0.25 to 0.25
- bubble_vel: float32 [3, 12288, 128], P(None, ('px', 'pz')), may hold values from -6 to 6
- owner: int32 [2, 12288, 128], P(None, ('px', 'pz')), may hold values from 0 to 16383
- dest: int32 [2, 12288], P(None, ('px', 'pz')), may hold values from -1 to 1, as said below
Outputs:
- velocity_next: float32 [3, 64, 512, 256], P(None, 'pz', 'px')
- bubble_next: float32 [3, 12288, 128], P(None, ('px', 'pz'))
Inputs may be any that keep to these rules, and one draw needn't show every extreme that they name: `dest`: in each substep at most 8 rows of one device have 1 and at most 8 have -1; some device has exactly 8 rows with 1 and some device exactly 8 rows with -1. `owner`: the cell counts streamwise cells fastest, then the wall-normal rows of the owning device's block, then its spanwise cells.
All inputs are finite; a program needn't handle non-finite values.
Results may differ from a plain program's by a relative error of at most 0.0018.
Values may be sent and summed in bfloat16 or wider, within the bound.
No kernel may reach another device: no remote copies, remote signals or barrier semaphores. Data moves between devices by JAX's collectives and lax.ppermute only.
A program may use at most 64 MiB of HBM per device.

v0:
```python
import functools

import jax
import jax.numpy as jnp
from jax import lax
from jax.experimental import pallas as pl
from jax.experimental.pallas import tpu as pltpu
from jax.sharding import PartitionSpec as P

step_size = 0.5
viscosity = 0.4
relax_time = 0.5
coupling = 2.0
buoyancy = 0.5
forcing = 1.0
gammas = (8.0 / 15.0, 5.0 / 12.0)
zetas = (0.0, -17.0 / 60.0)

F32 = jnp.float32
BF16 = jnp.bfloat16
C1 = step_size * gammas[0]
C2 = step_size * gammas[1]
E2 = step_size * zetas[1]

ROWS_A = 64
FIELD_ROWS = 192
SEND_ROWS = 240
LAST_ROWS = 96


def iota(shape, dim):
    return lax.broadcasted_iota(jnp.int32, shape, dim)


def call(body, outs, scratch=()):
    return pl.pallas_call(
        body,
        out_shape=tuple(jax.ShapeDtypeStruct(s, d) for s, d in outs),
        scratch_shapes=list(scratch),
        compiler_params=pltpu.CompilerParams(vmem_limit_bytes=48 * 1024 * 1024),
    )


def exact_dot(a, b):
    return jnp.dot(a, b, precision=lax.Precision.HIGHEST, preferred_element_type=F32)


def hi_lo(x):
    hi = x.astype(BF16).astype(F32)
    return hi, x - hi


def pick_matrix(dest_row):
    up = jnp.where(dest_row == 1, 1.0, 0.0).astype(F32)
    down = jnp.where(dest_row == -1, 1.0, 0.0).astype(F32)
    slot = iota((16, 24), 0)
    marks = jnp.where(slot < 8, jnp.broadcast_to(up, (16, 24)), jnp.broadcast_to(down, (16, 24)))
    before = jnp.where(iota((24, 24), 0) < iota((24, 24), 1), 1.0, 0.0).astype(F32)
    rank = exact_dot(marks, before)
    wanted = jnp.where(slot < 8, slot, slot - 8).astype(F32)
    return jnp.where((rank == wanted) & (marks > 0.5), 1.0, 0.0).astype(F32)


def put_matrix(dest_row):
    r, c = iota((24, 24), 0), iota((24, 24), 1)
    wide = jnp.broadcast_to(dest_row, (24, 24))
    own = jnp.sum(jnp.where(r == c, wide, 0).astype(F32), axis=1, keepdims=True)
    rank_up = jnp.sum(jnp.where((c < r) & (wide == 1), 1.0, 0.0), axis=1, keepdims=True)
    rank_down = jnp.sum(jnp.where((c < r) & (wide == -1), 1.0, 0.0), axis=1, keepdims=True)
    slot = iota((24, 16), 1).astype(F32)
    hit_up = (own == 1.0) & (rank_up == slot)
    hit_down = (own == -1.0) & (rank_down + 8.0 == slot)
    return jnp.where(hit_up | hit_down, 1.0, 0.0).astype(F32)


def home_cells(cells, dest_row):
    r, c = iota((24, 24), 0), iota((24, 24), 1)
    wide = jnp.broadcast_to(dest_row, (24, 24))
    away = jnp.sum(jnp.where((r == c) & (wide != 0), 1.0, 0.0), axis=1, keepdims=True)
    row = jnp.where(away > 0.5, -1, cells >> 8)
    return row, cells & 255


def fill_columns(col, hot_ref):
    at = iota((256, 128), 0)
    for k in range(8):
        hot = jnp.where(at == jnp.broadcast_to(col[k : k + 1], (256, 128)), 1.0, 0.0)
        hot_ref[:, k * 128 : (k + 1) * 128] = hot.astype(BF16)


def fill_values(row, highs, lows, load_ref):
    at = iota((ROWS_A, 128), 0)
    for k in range(8):
        mask = at == jnp.broadcast_to(row[k : k + 1], (ROWS_A, 128))
        lanes = slice(k * 128, (k + 1) * 128)
        for part, values in enumerate((highs, lows)):
            for a in range(3):
                base = (part * 3 + a) * ROWS_A
                value = jnp.broadcast_to(values[a][k : k + 1], (ROWS_A, 128))
                load_ref[base : base + ROWS_A, lanes] = jnp.where(mask, value, 0.0).astype(BF16)
        load_ref[384:448, lanes] = jnp.where(mask, 1.0, 0.0).astype(BF16)


def scatter(load_ref, hot_ref):
    return lax.dot_general(
        load_ref[...], hot_ref[...], (((1,), (1,)), ((), ())), preferred_element_type=F32
    )


def gather(table, row, hot_ref):
    found = jnp.dot(table, hot_ref[...], preferred_element_type=F32)
    parts = found.shape[0] // FIELD_ROWS
    at = iota((ROWS_A, 128), 0)
    lines = [[], [], []]
    for k in range(8):
        mask = at == jnp.broadcast_to(row[k : k + 1], (ROWS_A, 128))
        for a in range(3):
            block = found[a * ROWS_A : (a + 1) * ROWS_A, k * 128 : (k + 1) * 128]
            for part in range(1, parts):
                base = part * FIELD_ROWS + a * ROWS_A
                block = block + found[base : base + ROWS_A, k * 128 : (k + 1) * 128]
            lines[a].append(jnp.sum(jnp.where(mask, block, 0.0), axis=0, keepdims=True))
    return [jnp.concatenate(line, axis=0) for line in lines]


def split_table(field, table_ref):
    hi, lo = hi_lo(field)
    table_ref[0:FIELD_ROWS] = hi.astype(BF16)
    table_ref[FIELD_ROWS : 2 * FIELD_ROWS] = lo.astype(BF16)


def push_of(sums, field):
    loads = sums[0:192] + sums[192:384]
    count = sums[384:448]
    return coupling * (loads - jnp.concatenate([count, count, count], axis=0) * field)


def plane(ref, a, z):
    base = (a * 4 + z) * 16
    return ref[base : base + 16, :].astype(F32)


def inner_tendency(f_ref, a, z):
    here = plane(f_ref, a, z)
    next_x = pltpu.roll(here, 255, 1)
    prev_x = pltpu.roll(here, 1, 1)
    across = next_x + prev_x - 4.0 * here
    slope_z = None
    if z < 3:
        next_z = plane(f_ref, a, z + 1)
        across = across + next_z
        slope_z = next_z
    if z > 0:
        prev_z = plane(f_ref, a, z - 1)
        across = across + prev_z
        slope_z = -prev_z if slope_z is None else slope_z - prev_z
    flow = plane(f_ref, 0, z) * (0.5 * (next_x - prev_x)) + plane(f_ref, 2, z) * (0.5 * slope_z)
    total = viscosity * across - flow
    return total + forcing if a == 0 else total


def halo_term(f_ref, below, above, a, z):
    if z == 0:
        return (viscosity + 0.5 * plane(f_ref, 2, 0)) * below
    return (viscosity - 0.5 * plane(f_ref, 2, 3)) * above


def lane_group(shape):
    return iota(shape, len(shape) - 1) // 32


def first_send(field_ref, bubble_ref, owner_ref, dest_ref, up_ref, down_ref, moved_ref):
    block = field_ref[...].astype(BF16)
    up_ref[0:FIELD_ROWS] = block
    down_ref[0:FIELD_ROWS] = block
    first, second = owner_ref[0], owner_ref[1]
    columns = [bubble_ref[a] for a in range(3)]
    columns += [((first >> 8) + 1).astype(F32), (first & 255).astype(F32)]
    picked = exact_dot(pick_matrix(dest_ref[0:1]), jnp.concatenate(columns, axis=1))
    later = jnp.concatenate([((second >> 8) + 1).astype(F32), (second & 255).astype(F32)], axis=1)
    later = exact_dot(pick_matrix(dest_ref[1:2]), later)
    moved_ref[...] = picked[:, 384:640]
    for ref, at in ((up_ref, 0), (down_ref, 8)):
        lines = []
        for a in range(3):
            lines.append(jnp.concatenate(hi_lo(picked[at : at + 8, a * 128 : (a + 1) * 128]), axis=1))
        lines += [picked[at : at + 8, 384:640], later[at : at + 8], jnp.zeros((8, 256), F32)]
        ref[FIELD_ROWS:SEND_ROWS] = jnp.concatenate(lines, axis=0).astype(BF16)


def home_first(field_ref, bubble_ref, owner_ref, dest_ref, part_ref, seen_ref,
               table_ref, row_ref, col_ref, hot_ref, load_ref, sum_ref):
    field = field_ref[...]
    split_table(field, table_ref)
    row, col = home_cells(owner_ref[0], dest_ref[0:1])
    row_ref[...] = row
    col_ref[...] = col
    sum_ref[...] = jnp.zeros_like(sum_ref)

    def step(i, carry):
        rows = pl.ds(pl.multiple_of(i * 8, 8), 8)
        row8, col8 = row_ref[rows], col_ref[rows]
        fill_columns(col8, hot_ref)
        pairs = [hi_lo(bubble_ref[a, rows]) for a in range(3)]
        fill_values(row8, [p[0] for p in pairs], [p[1] for p in pairs], load_ref)
        seen = gather(table_ref[...], row8, hot_ref)
        for a in range(3):
            seen_ref[a, rows] = seen[a]
        sum_ref[...] += scatter(load_ref, hot_ref)
        return carry

    lax.fori_loop(0, 3, step, 0)
    push = push_of(sum_ref[...], field)
    for a in range(3):
        for z in range(4):
            base = (a * 4 + z) * 16
            part_ref[base : base + 16] = inner_tendency(field_ref, a, z) + push[base : base + 16]


def tail_of(ref, line):
    base = FIELD_ROWS + line * 8
    return ref[base : base + 8, :].astype(F32)


def tail_cells(tail, line):
    at = tail[line * 8 : line * 8 + 8].astype(jnp.int32)
    return at[:, 0:128] - 1, at[:, 128:256]


def pack_pair(six, out_ref):
    group = lane_group((16, 128))
    group8 = lane_group((8, 128))
    for z in range(4):
        for half in range(2):
            tiles = [six[i][z][:, half * 128 : (half + 1) * 128] for i in range(6)]
            for o in range(4):
                def moved(x, target):
                    shift = ((target - o) % 4) * 32
                    return x if shift == 0 else pltpu.roll(x, shift, 1)
                main = moved(tiles[3], 3)
                for i in range(3):
                    main = jnp.where(group == i, moved(tiles[i], i), main)
                rest = moved(tiles[5][8:16], 3)
                rest = jnp.where(group8 == 2, moved(tiles[4][8:16], 2), rest)
                rest = jnp.where(group8 == 1, moved(tiles[5][0:8], 1), rest)
                rest = jnp.where(group8 == 0, moved(tiles[4][0:8], 0), rest)
                peer = z * 8 + half * 4 + o
                out_ref[peer] = jnp.concatenate([main, rest], axis=0).astype(BF16)


def unpack(ref, second, a, z):
    halves = []
    group = lane_group((16, 128))
    for half in range(2):
        total = None
        for o in range(4):
            chunk = ref[z * 8 + half * 4 + o].astype(F32)
            if not second:
                piece, at = chunk[0:16], a
            elif a == 0:
                piece, at = chunk[0:16], 3
            else:
                rest = chunk[16:24]
                piece, at = jnp.concatenate([rest, pltpu.roll(rest, 64, 1)], axis=0), a - 1
            shift = ((o - at) % 4) * 32
            piece = piece if shift == 0 else pltpu.roll(piece, shift, 1)
            total = piece if total is None else jnp.where(group == o, piece, total)
        halves.append(total)
    return jnp.concatenate(halves, axis=1)


def arrivals_first(field_ref, part_ref, low_ref, high_ref, tend_ref, send_ref, hot_ref, load_ref):
    field = field_ref[...]
    sums = None
    for ref in (low_ref, high_ref):
        tail = ref[FIELD_ROWS:SEND_ROWS, :].astype(F32)
        row, col = tail_cells(tail, 3)
        fill_columns(col, hot_ref)
        highs = [tail[a * 8 : a * 8 + 8, 0:128] for a in range(3)]
        lows = [tail[a * 8 : a * 8 + 8, 128:256] for a in range(3)]
        fill_values(row, highs, lows, load_ref)
        got = scatter(load_ref, hot_ref)
        sums = got if sums is None else sums + got
    push = push_of(sums, field)
    six = [[None] * 4 for _ in range(6)]
    for a in range(3):
        for z in range(4):
            base = (a * 4 + z) * 16
            total = part_ref[base : base + 16] + push[base : base + 16]
            if z == 0 or z == 3:
                total = total + halo_term(field_ref, plane(low_ref, a, 3), plane(high_ref, a, 0), a, z)
            tend_ref[base : base + 16] = total
            here = field_ref[base : base + 16]
            six[a][z] = here
            six[3 + a][z] = here + C1 * total
    pack_pair(six, send_ref)


def bubbles_first(low_ref, high_ref, moved_ref, seen_ref, bubble_ref, owner_ref, dest_ref,
                  rate_ref, next_ref, slots_ref, sum_ref, row_ref, col_ref, hot_ref, load_ref):
    found = [[], [], []]
    for at, ref in ((0, high_ref), (8, low_ref)):
        cells = moved_ref[at : at + 8].astype(jnp.int32)
        fill_columns(cells[:, 128:256], hot_ref)
        seen = gather(ref[0:FIELD_ROWS], cells[:, 0:128] - 1, hot_ref)
        for a in range(3):
            found[a].append(seen[a])
    found = jnp.concatenate([jnp.concatenate(f, axis=0) for f in found], axis=1)
    back = exact_dot(put_matrix(dest_ref[0:1]), found)
    after = []
    for a in range(3):
        here = bubble_ref[a]
        rate = (seen_ref[a] + back[:, a * 128 : (a + 1) * 128] - here) / relax_time
        if a == 1:
            rate = rate + buoyancy
        rate_ref[a] = rate
        after.append(here + C1 * rate)
        next_ref[a] = after[a]
    picked = exact_dot(pick_matrix(dest_ref[1:2]), jnp.concatenate(after, axis=1))
    for at in (0, 8):
        for a in range(3):
            line = at * 3 + a * 8
            slots_ref[line : line + 8] = jnp.concatenate(
                hi_lo(picked[at : at + 8, a * 128 : (a + 1) * 128]), axis=1
            )
    row, col = home_cells(owner_ref[1], dest_ref[1:2])
    row_ref[...] = row
    col_ref[...] = col
    sum_ref[...] = jnp.zeros_like(sum_ref)

    def step(i, carry):
        rows = pl.ds(pl.multiple_of(i * 8, 8), 8)
        fill_columns(col_ref[rows], hot_ref)
        pairs = [hi_lo(next_ref[a, rows]) for a in range(3)]
        fill_values(row_ref[rows], [p[0] for p in pairs], [p[1] for p in pairs], load_ref)
        sum_ref[...] += scatter(load_ref, hot_ref)
        return carry

    lax.fori_loop(0, 3, step, 0)


def columns_body(got_ref, first_ref, second_ref, send_ref):
    got = got_ref[...].astype(F32)
    main = got[:, 0:16].reshape(512, 128)
    rest = got[:, 16:24].reshape(256, 128)
    other = pltpu.roll(rest, 64, 1)
    rest = jnp.concatenate([rest.reshape(32, 8, 128), other.reshape(32, 8, 128)], axis=1).reshape(512, 128)
    group = lane_group((512, 128))
    guess = jnp.where(group == 0, pltpu.roll(main, 32, 1), pltpu.roll(rest, 32, 1))

    def wall(x):
        field = x.astype(BF16)
        wide = field.astype(F32)
        normal = jnp.where(group == 0, pltpu.roll(wide, 96, 1), jnp.where(group == 2, pltpu.roll(wide, 32, 1), wide))
        slopes = jnp.dot(first_ref[...], field, preferred_element_type=F32).astype(BF16).astype(F32)
        curves = jnp.dot(second_ref[...], field, preferred_element_type=F32).astype(BF16).astype(F32)
        return (viscosity * curves - normal * slopes).astype(BF16).astype(F32)

    wall_1 = wall(main)
    wall_2 = wall(guess + C1 * wall_1)
    back = pltpu.roll(wall_2, 96, 1)
    ahead = pltpu.roll(wall_2, 32, 1)
    out = jnp.where(group == 3, back, wall_1).reshape(32, 16, 128)
    group8 = lane_group((32, 8, 128))
    tail = jnp.where(group8 < 2, back.reshape(32, 16, 128)[:, 0:8], ahead.reshape(32, 16, 128)[:, 8:16])
    send_ref[...] = jnp.concatenate([out, tail], axis=1).astype(BF16)


def middle_body(wall_ref, field_ref, part_ref, low_ref, high_ref, slots_ref,
                next_ref, tend_ref, up_ref, down_ref, table_ref, hot_ref):
    for a in range(3):
        for z in range(4):
            base = (a * 4 + z) * 16
            total = part_ref[base : base + 16] + unpack(wall_ref, False, a, z)
            tend_ref[base : base + 16] = total
            next_ref[base : base + 16] = field_ref[base : base + 16] + C1 * total
    split_table(next_ref[...], table_ref)
    for ref, out_ref, z, at in ((low_ref, down_ref, 0, 24), (high_ref, up_ref, 3, 0)):
        tail = ref[FIELD_ROWS:SEND_ROWS, :].astype(F32)
        row, col = tail_cells(tail, 4)
        fill_columns(col, hot_ref)
        seen = gather(table_ref[...], row, hot_ref)
        lines = [plane(next_ref, a, z) for a in range(3)]
        lines.append(slots_ref[at : at + 24])
        lines += [jnp.concatenate(hi_lo(seen[a]), axis=1) for a in range(3)]
        out_ref[...] = jnp.concatenate(lines, axis=0).astype(BF16)


def home_second(wall_ref, field_ref, tend_ref, sum_ref, bubble_ref, rate_ref, owner_ref, dest_ref,
                base_ref, late_ref, table_ref, row_ref, col_ref, hot_ref):
    field = field_ref[...]
    push = push_of(sum_ref[...], field)
    for a in range(3):
        for z in range(4):
            base = (a * 4 + z) * 16
            total = inner_tendency(field_ref, a, z) + push[base : base + 16] + unpack(wall_ref, True, a, z)
            earlier = tend_ref[base : base + 16]
            base_ref[base : base + 16] = field_ref[base : base + 16] + (C2 * total + E2 * earlier)
    split_table(field, table_ref)
    row, col = home_cells(owner_ref[1], dest_ref[1:2])
    row_ref[...] = row
    col_ref[...] = col

    def step(i, carry):
        rows = pl.ds(pl.multiple_of(i * 8, 8), 8)
        fill_columns(col_ref[rows], hot_ref)
        seen = gather(table_ref[...], row_ref[rows], hot_ref)
        for a in range(3):
            here = bubble_ref[a, rows]
            rate = (seen[a] - here) / relax_time
            if a == 1:
                rate = rate + buoyancy
            late_ref[a, rows] = here + (C2 * rate + E2 * rate_ref[a, rows])
        return carry

    lax.fori_loop(0, 3, step, 0)


def arrivals_second(base_ref, field_ref, low_ref, high_ref, low2_ref, high2_ref, late_ref, dest_ref,
                    out_ref, bubble_ref, hot_ref, load_ref):
    field = field_ref[...]
    sums = None
    for ref, ref2 in ((low_ref, low2_ref), (high_ref, high2_ref)):
        tail = ref[FIELD_ROWS:SEND_ROWS, :].astype(F32)
        row, col = tail_cells(tail, 4)
        fill_columns(col, hot_ref)
        extra = ref2[48:96, :].astype(F32)
        highs = [extra[a * 8 : a * 8 + 8, 0:128] for a in range(3)]
        lows = [extra[a * 8 : a * 8 + 8, 128:256] for a in range(3)]
        fill_values(row, highs, lows, load_ref)
        got = scatter(load_ref, hot_ref)
        sums = got if sums is None else sums + got
    push = push_of(sums, field)
    for a in range(3):
        for z in range(4):
            base = (a * 4 + z) * 16
            total = push[base : base + 16]
            if z == 0 or z == 3:
                below = low2_ref[a * 16 : a * 16 + 16, :].astype(F32)
                above = high2_ref[a * 16 : a * 16 + 16, :].astype(F32)
                total = total + halo_term(field_ref, below, above, a, z)
            out_ref[base : base + 16] = base_ref[base : base + 16] + C2 * total
    from_high = high2_ref[48:96, :].astype(F32)
    from_low = low2_ref[48:96, :].astype(F32)
    found = []
    for a in range(3):
        line = 24 + a * 8
        high = from_high[line : line + 8, 0:128] + from_high[line : line + 8, 128:256]
        low = from_low[line : line + 8, 0:128] + from_low[line : line + 8, 128:256]
        found.append(jnp.concatenate([high, low], axis=0))
    back = exact_dot(put_matrix(dest_ref[1:2]), jnp.concatenate(found, axis=1))
    for a in range(3):
        bubble_ref[a] = late_ref[a] + (C2 / relax_time) * back[:, a * 128 : (a + 1) * 128]


def shifted(x, by):
    length = lax.axis_size("pz")
    return lax.ppermute(x, "pz", [(i, (i + by) % length) for i in range(length)])


def exchange(x):
    return lax.all_to_all(x, "px", split_axis=0, concat_axis=0, tiled=True)


def on_device(velocity, first_deriv, second_deriv, bubble_vel, owner, dest):
    field = velocity.reshape(FIELD_ROWS, 256)
    block = ((FIELD_ROWS, 256), F32)
    rows = ((3, 24, 128), F32)
    hot = pltpu.VMEM((256, 1024), BF16)
    load = pltpu.VMEM((448, 1024), BF16)
    table = pltpu.VMEM((384, 256), BF16)
    ids = pltpu.VMEM((24, 128), jnp.int32)
    packed = ((32, 24, 128), BF16)

    sends = ((SEND_ROWS, 256), BF16)
    up, down, moved = call(first_send, (sends, sends, ((16, 256), F32)))(field, bubble_vel, owner, dest)
    low, high = shifted(up, 1), shifted(down, -1)
    part, seen = call(
        home_first, (block, rows), (table, ids, ids, hot, load, pltpu.VMEM((448, 256), F32))
    )(field, bubble_vel, owner, dest)
    part, to_columns = call(arrivals_first, (block, packed), (hot, load))(field, part, low, high)
    columns = exchange(to_columns)
    rate, bubbles, slots, sums = call(
        bubbles_first, (rows, rows, ((48, 256), F32), ((448, 256), F32)), (ids, ids, hot, load)
    )(low, high, moved, seen, bubble_vel, owner, dest)
    (walls,) = call(columns_body, (packed,))(columns, first_deriv, second_deriv)
    walls = exchange(walls)
    lasts = ((LAST_ROWS, 256), BF16)
    middle, tend, up, down = call(middle_body, (block, block, lasts, lasts), (table, hot))(
        walls, field, part, low, high, slots
    )
    low2, high2 = shifted(up, 1), shifted(down, -1)
    base, late = call(home_second, (block, rows), (table, ids, ids, hot))(
        walls, middle, tend, sums, bubbles, rate, owner, dest
    )
    field, bubbles = call(arrivals_second, (block, rows), (hot, load))(
        base, middle, low, high, low2, high2, late, dest
    )
    return (field.reshape(velocity.shape), bubbles)


def solution(mesh):
    return jax.shard_map(
        on_device,
        mesh=mesh,
        in_specs=(
            P(None, "pz", "px", None),
            P(),
            P(),
            P(None, ("px", "pz"), None),
            P(None, ("px", "pz"), None),
            P(None, ("px", "pz")),
        ),
        out_specs=(P(None, "pz", "px", None), P(None, ("px", "pz"), None)),
        check_vma=False,
    )
```

profile of v0, /device:TPU:54, one launch (start us, length us, event | category | flops | bytes accessed | tf_op | source)
XLA Modules:
  0.0 75.8 jit_solution(884594112794509560)
XLA Ops:
  0.6 0.0 copy-start.8
  0.6 0.7 copy-done.8
  1.3 0.9 %copy-done = f32[3,4,16,256]{3,2,1,0:T(8,128)S(1)} copy-done((f32[3,4,16,256]{3,2,1,0:T(8,128)S(1)}, f32[3,4,16,256]{3,2,1,0:T(8,128)}, u32[]{:S(2)}) %copy-start) | copy-done | bytes 196632
  2.2 0.7 copy-done.4
  3.0 0.8 %copy-done.6 = f32[3,24,128]{2,1,0:T(8,128)S(1)} copy-done((f32[3,24,128]{2,1,0:T(8,128)S(1)}, f32[3,24,128]{2,1,0:T(8,128)}, u32[]{:S(2)}) %copy-start.6) | copy-done | bytes 36888
  3.7 0.5 shard_map.78
  4.2 7.1 %collective-permute-start = (bf16[240,256]{1,0:T(8,128)(2,1)S(1)}, bf16[240,256]{1,0:T(8,128)(2,1)S(1)}, u32[]{:S(2)}, u32[]{:S(2)}) collective-permute-start(bf16[240,256]{1,0:T(8,128)(2,1)S(1)} %get-tuple-element.22), channel_id=1, source_target_pairs={{0,1},{1,2},{2,3},{3,4},{4,5},{5,6},{6,7},{7,8},{8,9},{9,10},{10,1... | collective-permute-start | bytes 368648 | tf_op jit(solution)/shard_map/ppermute | solution.py:458
  11.3 1.9 %collective-permute-start.1 = (bf16[240,256]{1,0:T(8,128)(2,1)S(1)}, bf16[240,256]{1,0:T(8,128)(2,1)S(1)}, u32[]{:S(2)}, u32[]{:S(2)}) collective-permute-start(bf16[240,256]{1,0:T(8,128)(2,1)S(1)} %get-tuple-element.23), channel_id=1, source_target_pairs={{0,15},{1,0},{2,1},{3,2},{4,3},{5,4},{6,5},{7,6},{8,7},{9,8},{10,9... | collective-permute-start | bytes 368648 | tf_op jit(solution)/shard_map/ppermute | solution.py:458
  13.3 0.0 copy-start.3
  13.3 2.5 %shard_map.77 = (f32[192,256]{1,0:T(8,128)S(1)}, f32[3,24,128]{2,1,0:T(8,128)S(1)}) custom-call(f32[192,256]{1,0:T(8,128)S(1)} %bitcast.3, f32[3,24,128]{2,1,0:T(8,128)S(1)} %copy-done.6, s32[2,24,128]{2,1,0:T(8,128)S(1)} %copy-done.4, s32[2,24]{1,0:T(2,128)S(1)} %copy-done.8), custom_call_target="tpu_custom_call" | custom-call | tf_op jit(solution)/shard_map/pallas_call | solution.py:478
  15.8 0.0 copy-start.2
  15.8 0.0 collective-permute-done.low_ref
  15.8 6.5 %collective-permute-done.1.high_ref = bf16[240,256]{1,0:T(8,128)(2,1)S(1)} collective-permute-done((bf16[240,256]{1,0:T(8,128)(2,1)S(1)}, bf16[240,256]{1,0:T(8,128)(2,1)S(1)}, u32[]{:S(2)}, u32[]{:S(2)}) %collective-permute-start.1) | collective-permute-done | bytes 122912 | tf_op jit(solution)/shard_map/ppermute | solution.py:458
  22.3 1.4 %shard_map.79 = (f32[192,256]{1,0:T(8,128)S(1)}, bf16[32,24,128]{2,1,0:T(8,128)(2,1)S(1)}) custom-call(f32[192,256]{1,0:T(8,128)S(1)} %bitcast.4, f32[192,256]{1,0:T(8,128)S(1)} %get-tuple-element.21.part_ref, bf16[240,256]{1,0:T(8,128)(2,1)S(1)} %collective-permute-done.low_ref, bf16[240,256]{1,0:T(8,128)(2,1)S(1)} %collective-permute-done.1.high_ref), custom_call_target="tpu_custom_call" | custom-call | tf_op jit(solution)/shard_map/pallas_call | solution.py:481
  23.7 19.5 %all_to_all.10.got_ref = bf16[32,24,128]{2,1,0:T(8,128)(2,1)S(1)} all-to-all(bf16[32,24,128]{2,1,0:T(8,128)(2,1)S(1)} %get-tuple-element.24), channel_id=1, replica_groups=mesh['px'=32,'pz'=16] {'px'}, dimensions={0} | all-to-all | bytes 393216 | tf_op jit(solution)/shard_map/all_to_all | solution.py:462
  43.2 0.0 copy-done.3
  43.2 0.0 copy-done.2
  43.2 1.5 %shard_map.80 = bf16[32,24,128]{2,1,0:T(8,128)(2,1)} custom-call(bf16[32,24,128]{2,1,0:T(8,128)(2,1)S(1)} %all_to_all.10.got_ref, bf16[512,512]{1,0:T(8,128)(2,1)S(1)} %copy-done.2, bf16[512,512]{1,0:T(8,128)(2,1)S(1)} %copy-done.3), custom_call_target="tpu_custom_call" | custom-call | tf_op jit(solution)/shard_map/pallas_call | solution.py:486
  44.7 4.0 %all-to-all-start.1 = ((bf16[32,24,128]{2,1,0:T(8,128)(2,1)}), bf16[32,24,128]{2,1,0:T(8,128)(2,1)S(1)}, u32[]{:S(2)}, u32[]{:S(2)}) async-start(bf16[32,24,128]{2,1,0:T(8,128)(2,1)} %shard_map.80), calls=%async_computation.1 | async-start | bytes 393216 | tf_op jit(solution)/shard_map/all_to_all | solution.py:462
  48.7 0.0 copy-start.1
  48.7 0.0 copy-done.5
  48.7 0.0 copy-done.7
  48.7 2.9 %shard_map.81 = (f32[3,24,128]{2,1,0:T(8,128)S(1)}, f32[3,24,128]{2,1,0:T(8,128)S(1)}, f32[48,256]{1,0:T(8,128)S(1)}, f32[448,256]{1,0:T(8,128)S(1)}) custom-call(bf16[240,256]{1,0:T(8,128)(2,1)S(1)} %collective-permute-done.low_ref, bf16[240,256]{1,0:T(8,128)(2,1)S(1)} %collective-permute-done.1.high_ref, f32[16,256]{1,0:T(8,128)S(1)} %get-tuple-element.26.moved_ref, ...), custom_call_target="tpu_custom_call" | custom-call | tf_op jit(solution)/shard_map/pallas_call | solution.py:483
  51.7 8.0 %all-to-all-done.1.wall_ref = bf16[32,24,128]{2,1,0:T(8,128)(2,1)S(1)} async-done(((bf16[32,24,128]{2,1,0:T(8,128)(2,1)}), bf16[32,24,128]{2,1,0:T(8,128)(2,1)S(1)}, u32[]{:S(2)}, u32[]{:S(2)}) %all-to-all-start.1) | async-done | bytes 196640 | tf_op jit(solution)/shard_map/all_to_all | solution.py:462
  59.7 0.0 copy-done.1
  59.7 1.0 %shard_map.82 = (f32[192,256]{1,0:T(8,128)S(1)}, f32[192,256]{1,0:T(8,128)S(1)}, bf16[96,256]{1,0:T(8,128)(2,1)S(1)}, bf16[96,256]{1,0:T(8,128)(2,1)S(1)}) custom-call(bf16[32,24,128]{2,1,0:T(8,128)(2,1)S(1)} %all-to-all-done.1.wall_ref, f32[192,256]{1,0:T(8,128)S(1)} %bitcast.5, f32[192,256]{1,0:T(8,128)S(1)} %get-tuple-element.25.part_ref, ...), custom_call_target="tpu_custom_call" | custom-call | tf_op jit(solution)/shard_map/pallas_call | solution.py:489
  60.6 1.9 %collective-permute-start.2 = (bf16[96,256]{1,0:T(8,128)(2,1)S(1)}, bf16[96,256]{1,0:T(8,128)(2,1)S(1)}, u32[]{:S(2)}, u32[]{:S(2)}) collective-permute-start(bf16[96,256]{1,0:T(8,128)(2,1)S(1)} %get-tuple-element.35), channel_id=1, source_target_pairs={{0,1},{1,2},{2,3},{3,4},{4,5},{5,6},{6,7},{7,8},{8,9},{9,10},{10,1... | collective-permute-start | bytes 147464 | tf_op jit(solution)/shard_map/ppermute | solution.py:458
  62.6 4.8 %collective-permute-start.3 = (bf16[96,256]{1,0:T(8,128)(2,1)S(1)}, bf16[96,256]{1,0:T(8,128)(2,1)S(1)}, u32[]{:S(2)}, u32[]{:S(2)}) collective-permute-start(bf16[96,256]{1,0:T(8,128)(2,1)S(1)} %get-tuple-element.36), channel_id=1, source_target_pairs={{0,15},{1,0},{2,1},{3,2},{4,3},{5,4},{6,5},{7,6},{8,7},{9,8},{10,9... | collective-permute-start | bytes 147464 | tf_op jit(solution)/shard_map/ppermute | solution.py:458
  67.4 2.5 %shard_map.83 = (f32[192,256]{1,0:T(8,128)S(1)}, f32[3,24,128]{2,1,0:T(8,128)S(1)}) custom-call(bf16[32,24,128]{2,1,0:T(8,128)(2,1)S(1)} %all-to-all-done.1.wall_ref, f32[192,256]{1,0:T(8,128)S(1)} %get-tuple-element.29.field_ref, f32[192,256]{1,0:T(8,128)S(1)} %get-tuple-element.30.tend_ref, f32[448,256]{1,0:T(8,128)S(1)} %get-tuple-element.31.sum_ref, ...), custom_call_target="tpu_custom_call" | custom-call | tf_op jit(solution)/shard_map/pallas_call | solution.py:493
  69.9 0.0 collective-permute-done.2.low2_ref
  69.9 3.8 %collective-permute-done.3.high2_ref = bf16[96,256]{1,0:T(8,128)(2,1)S(1)} collective-permute-done((bf16[96,256]{1,0:T(8,128)(2,1)S(1)}, bf16[96,256]{1,0:T(8,128)(2,1)S(1)}, u32[]{:S(2)}, u32[]{:S(2)}) %collective-permute-start.3) | collective-permute-done | bytes 49184 | tf_op jit(solution)/shard_map/ppermute | solution.py:458
  73.8 2.0 %shard_map.84 = (f32[192,256]{1,0:T(8,128)}, f32[3,24,128]{2,1,0:T(8,128)}) custom-call(f32[192,256]{1,0:T(8,128)S(1)} %get-tuple-element.34.base_ref, f32[192,256]{1,0:T(8,128)S(1)} %get-tuple-element.29.field_ref, bf16[240,256]{1,0:T(8,128)(2,1)S(1)} %collective-permute-done.low_ref, bf16[240,256]{1,0:T(8,128)(2,1)S(1)} %collective-permute-done.1.high_ref, ...), custom_call_target="tpu_custom_call" | custom-call | tf_op jit(solution)/shard_map/pallas_call | solution.py:496
  (5 shorter events, 0.0 us)
Async XLA Ops:
  0.6 0.7 copy-start.8
  1.3 0.9 %copy-start = (f32[3,4,16,256]{3,2,1,0:T(8,128)S(1)}, f32[3,4,16,256]{3,2,1,0:T(8,128)}, u32[]{:S(2)}) copy-start(f32[3,4,16,256]{3,2,1,0:T(8,128)} %param.6) | copy-start | bytes 589828
  2.2 0.7 copy-start.4
  3.0 0.8 %copy-start.6 = (f32[3,24,128]{2,1,0:T(8,128)S(1)}, f32[3,24,128]{2,1,0:T(8,128)}, u32[]{:S(2)}) copy-start(f32[3,24,128]{2,1,0:T(8,128)} %bubble_ref.5) | copy-start | bytes 110596
  4.2 11.6 %collective-permute-start = (bf16[240,256]{1,0:T(8,128)(2,1)S(1)}, bf16[240,256]{1,0:T(8,128)(2,1)S(1)}, u32[]{:S(2)}, u32[]{:S(2)}) collective-permute-start(bf16[240,256]{1,0:T(8,128)(2,1)S(1)} %get-tuple-element.22), channel_id=1, source_target_pairs={{0,1},{1,2},{2,3},{3,4},{4,5},{5,6},{6,7},{7,8},{8,9},{9,10},{10,1... | collective-permute-start | bytes 368648 | tf_op jit(solution)/shard_map/ppermute | solution.py:458
  11.3 11.0 %collective-permute-start.1 = (bf16[240,256]{1,0:T(8,128)(2,1)S(1)}, bf16[240,256]{1,0:T(8,128)(2,1)S(1)}, u32[]{:S(2)}, u32[]{:S(2)}) collective-permute-start(bf16[240,256]{1,0:T(8,128)(2,1)S(1)} %get-tuple-element.23), channel_id=1, source_target_pairs={{0,15},{1,0},{2,1},{3,2},{4,3},{5,4},{6,5},{7,6},{8,7},{9,8},{10,9... | collective-permute-start | bytes 368648 | tf_op jit(solution)/shard_map/ppermute | solution.py:458
  13.3 29.9 %copy-start.3 = (bf16[512,512]{1,0:T(8,128)(2,1)S(1)}, bf16[512,512]{1,0:T(8,128)(2,1)}, u32[]{:S(2)}) copy-start(bf16[512,512]{1,0:T(8,128)(2,1)} %second_ref.1) | copy-start | bytes 1572868
  15.8 27.4 %copy-start.2 = (bf16[512,512]{1,0:T(8,128)(2,1)S(1)}, bf16[512,512]{1,0:T(8,128)(2,1)}, u32[]{:S(2)}) copy-start(bf16[512,512]{1,0:T(8,128)(2,1)} %first_ref.1) | copy-start | bytes 1572868
  44.7 4.0 %copy-start.5 = (s32[2,24,128]{2,1,0:T(8,128)S(1)}, s32[2,24,128]{2,1,0:T(8,128)}, u32[]{:S(2)}) copy-start(s32[2,24,128]{2,1,0:T(8,128)} %owner_ref.7) | copy-start | bytes 73732
  44.7 4.0 %copy-start.7 = (f32[3,24,128]{2,1,0:T(8,128)S(1)}, f32[3,24,128]{2,1,0:T(8,128)}, u32[]{:S(2)}) copy-start(f32[3,24,128]{2,1,0:T(8,128)} %bubble_ref.5) | copy-start | bytes 110596
  44.7 15.0 %all-to-all-start.1 = ((bf16[32,24,128]{2,1,0:T(8,128)(2,1)}), bf16[32,24,128]{2,1,0:T(8,128)(2,1)S(1)}, u32[]{:S(2)}, u32[]{:S(2)}) async-start(bf16[32,24,128]{2,1,0:T(8,128)(2,1)} %shard_map.80), calls=%async_computation.1 | async-start | bytes 393216 | tf_op jit(solution)/shard_map/all_to_all | solution.py:462
  48.7 11.0 %copy-start.1 = (f32[3,4,16,256]{3,2,1,0:T(8,128)S(1)}, f32[3,4,16,256]{3,2,1,0:T(8,128)}, u32[]{:S(2)}) copy-start(f32[3,4,16,256]{3,2,1,0:T(8,128)} %param.6) | copy-start | bytes 589828
  60.6 9.3 %collective-permute-start.2 = (bf16[96,256]{1,0:T(8,128)(2,1)S(1)}, bf16[96,256]{1,0:T(8,128)(2,1)S(1)}, u32[]{:S(2)}, u32[]{:S(2)}) collective-permute-start(bf16[96,256]{1,0:T(8,128)(2,1)S(1)} %get-tuple-element.35), channel_id=1, source_target_pairs={{0,1},{1,2},{2,3},{3,4},{4,5},{5,6},{6,7},{7,8},{8,9},{9,10},{10,1... | collective-permute-start | bytes 147464 | tf_op jit(solution)/shard_map/ppermute | solution.py:458
  62.6 11.2 %collective-permute-start.3 = (bf16[96,256]{1,0:T(8,128)(2,1)S(1)}, bf16[96,256]{1,0:T(8,128)(2,1)S(1)}, u32[]{:S(2)}, u32[]{:S(2)}) collective-permute-start(bf16[96,256]{1,0:T(8,128)(2,1)S(1)} %get-tuple-element.36), channel_id=1, source_target_pairs={{0,15},{1,0},{2,1},{3,2},{4,3},{5,4},{6,5},{7,6},{8,7},{9,8},{10,9... | collective-permute-start | bytes 147464 | tf_op jit(solution)/shard_map/ppermute | solution.py:458
where the time goes:
time: 76.3 us; the launch traced here: 75.8 us
  starting transfers between devices  19.8 us (26%)
  blocking collectives  19.5 us (26%)
  waiting for transfers between devices  18.4 us (24%)
  Pallas kernels  14.3 us (19%)
  local copies, waits for them, and re-layouts  3.13 us (4%)
  between operations  0.78 us (1%)
    all_to_all x1, blocking collectives, exchange(): return lax.all_to_all(x, 'px', split_axis=0, concat_axis=0, tiled=True)  19.5 us
    ppermute x4, starting transfers between devices, shifted(): lax.ppermute(x, 'pz', [(i, (i + by) % length) for i in range(length)])  15.8 us
    ppermute x4, waiting for transfers between devices, shifted(): lax.ppermute(x, 'pz', [(i, (i + by) % length) for i in range(length)])  10.4 us
    all_to_all x1, waiting for transfers between devices, exchange(): return lax.all_to_all(x, 'px', split_axis=0, concat_axis=0, tiled=True)  7.99 us
    all_to_all x1, starting transfers between devices, exchange(): return lax.all_to_all(x, 'px', split_axis=0, concat_axis=0, tiled=True)  4 us
    unnamed x18, local copies, waits for them, and re-layouts  3.13 us
    pallas_call x1, Pallas kernels, on_device(): call(bubbles_first, (rows, rows, ((48, 256), F32), ((448, 256), F32)), (i...  2.92 us
    pallas_call x1, Pallas kernels, on_device(): call(home_second, (block, rows), (table, ids, ids, hot))  2.52 us
  transfers between devices with their start and end apart: 5, of which 3 were waited for; matrix products, arithmetic and copies ran while one was open for 0% of the time, Pallas kernels for 10%

commit v1 on v0

--- a/solution.py
+++ b/solution.py
@@ -81,24 +81,37 @@
     return row, cells & 255
 
 
+def spread(line):
+    return jnp.broadcast_to(line, (16, 128)).astype(BF16)
+
+
+def row_numbers(count):
+    at = iota((16, 128), 0)
+    return [(at + 16 * q).astype(F32).astype(BF16) for q in range(count)]
+
+
 def fill_columns(col, hot_ref):
-    at = iota((256, 128), 0)
+    numbers = row_numbers(16)
+    one, zero = jnp.ones((16, 128), BF16), jnp.zeros((16, 128), BF16)
+    col = col.astype(F32)
     for k in range(8):
-        hot = jnp.where(at == jnp.broadcast_to(col[k : k + 1], (256, 128)), 1.0, 0.0)
-        hot_ref[:, k * 128 : (k + 1) * 128] = hot.astype(BF16)
+        here = spread(col[k : k + 1])
+        for q in range(16):
+            hot_ref[q * 16 : q * 16 + 16, k * 128 : (k + 1) * 128] = jnp.where(numbers[q] == here, one, zero)
 
 
 def fill_values(row, highs, lows, load_ref):
-    at = iota((ROWS_A, 128), 0)
+    numbers = row_numbers(4)
+    one, zero = jnp.ones((16, 128), BF16), jnp.zeros((16, 128), BF16)
+    row = row.astype(F32)
     for k in range(8):
-        mask = at == jnp.broadcast_to(row[k : k + 1], (ROWS_A, 128))
-        lanes = slice(k * 128, (k + 1) * 128)
-        for part, values in enumerate((highs, lows)):
-            for a in range(3):
-                base = (part * 3 + a) * ROWS_A
-                value = jnp.broadcast_to(values[a][k : k + 1], (ROWS_A, 128))
-                load_ref[base : base + ROWS_A, lanes] = jnp.where(mask, value, 0.0).astype(BF16)
-        load_ref[384:448, lanes] = jnp.where(mask, 1.0, 0.0).astype(BF16)
+        here = spread(row[k : k + 1])
+        masks = [numbers[q] == here for q in range(4)]
+        values = [spread(x[k : k + 1]) for x in (*highs, *lows)] + [one]
+        for part, value in enumerate(values[: load_ref.shape[0] // ROWS_A]):
+            for q in range(4):
+                at = part * ROWS_A + q * 16
+                load_ref[at : at + 16, k * 128 : (k + 1) * 128] = jnp.where(masks[q], value, zero)
 
 
 def scatter(load_ref, hot_ref):
@@ -169,10 +182,14 @@
     return iota(shape, len(shape) - 1) // 32
 
 
-def first_send(field_ref, bubble_ref, owner_ref, dest_ref, up_ref, down_ref, moved_ref):
-    block = field_ref[...].astype(BF16)
-    up_ref[0:FIELD_ROWS] = block
-    down_ref[0:FIELD_ROWS] = block
+def first_send(field_hbm, bubble_hbm, owner_hbm, dest_hbm, up_ref, down_ref, moved_ref,
+               field_ref, bubble_ref, owner_ref, dest_ref, sems):
+    pairs = ((dest_hbm, dest_ref), (owner_hbm, owner_ref), (bubble_hbm, bubble_ref), (field_hbm, field_ref))
+    copies = [pltpu.make_async_copy(src, dst, sems.at[i]) for i, (src, dst) in enumerate(pairs)]
+    for copy in copies:
+        copy.start()
+    for copy in copies[:3]:
+        copy.wait()
     first, second = owner_ref[0], owner_ref[1]
     columns = [bubble_ref[a] for a in range(3)]
     columns += [((first >> 8) + 1).astype(F32), (first & 255).astype(F32)]
@@ -186,6 +203,10 @@
             lines.append(jnp.concatenate(hi_lo(picked[at : at + 8, a * 128 : (a + 1) * 128]), axis=1))
         lines += [picked[at : at + 8, 384:640], later[at : at + 8], jnp.zeros((8, 256), F32)]
         ref[FIELD_ROWS:SEND_ROWS] = jnp.concatenate(lines, axis=0).astype(BF16)
+    copies[3].wait()
+    block = field_ref[...].astype(BF16)
+    up_ref[0:FIELD_ROWS] = block
+    down_ref[0:FIELD_ROWS] = block
 
 
 def home_first(field_ref, bubble_ref, owner_ref, dest_ref, part_ref, seen_ref,
@@ -217,9 +238,8 @@
             part_ref[base : base + 16] = inner_tendency(field_ref, a, z) + push[base : base + 16]
 
 
-def tail_of(ref, line):
-    base = FIELD_ROWS + line * 8
-    return ref[base : base + 8, :].astype(F32)
+def tail_of(ref):
+    return ref[FIELD_ROWS:SEND_ROWS, :].astype(F32)
 
 
 def tail_cells(tail, line):
@@ -273,7 +293,7 @@
     field = field_ref[...]
     sums = None
     for ref in (low_ref, high_ref):
-        tail = ref[FIELD_ROWS:SEND_ROWS, :].astype(F32)
+        tail = tail_of(ref)
         row, col = tail_cells(tail, 3)
         fill_columns(col, hot_ref)
         highs = [tail[a * 8 : a * 8 + 8, 0:128] for a in range(3)]
@@ -292,12 +312,13 @@
             tend_ref[base : base + 16] = total
             here = field_ref[base : base + 16]
             six[a][z] = here
-            six[3 + a][z] = here + C1 * total
+            six[3 + a][z] = (here - here.astype(BF16).astype(F32)) + C1 * total
     pack_pair(six, send_ref)
 
 
 def bubbles_first(low_ref, high_ref, moved_ref, seen_ref, bubble_ref, owner_ref, dest_ref,
-                  rate_ref, next_ref, slots_ref, sum_ref, row_ref, col_ref, hot_ref, load_ref):
+                  rate_ref, next_ref, slots_ref, sum_ref, come_ref,
+                  row_ref, col_ref, hot_ref, load_ref, ones_ref):
     found = [[], [], []]
     for at, ref in ((0, high_ref), (8, low_ref)):
         cells = moved_ref[at : at + 8].astype(jnp.int32)
@@ -337,6 +358,11 @@
         return carry
 
     lax.fori_loop(0, 3, step, 0)
+    for i, ref in enumerate((low_ref, high_ref)):
+        row, col = tail_cells(tail_of(ref), 4)
+        fill_columns(col, come_ref.at[i])
+        fill_values(row, (), (), ones_ref)
+        sum_ref[384:448] += scatter(ones_ref, come_ref.at[i])
 
 
 def columns_body(got_ref, first_ref, second_ref, send_ref):
@@ -346,7 +372,7 @@
     other = pltpu.roll(rest, 64, 1)
     rest = jnp.concatenate([rest.reshape(32, 8, 128), other.reshape(32, 8, 128)], axis=1).reshape(512, 128)
     group = lane_group((512, 128))
-    guess = jnp.where(group == 0, pltpu.roll(main, 32, 1), pltpu.roll(rest, 32, 1))
+    gain = jnp.where(group == 0, pltpu.roll(main, 32, 1), pltpu.roll(rest, 32, 1))
 
     def wall(x):
         field = x.astype(BF16)
@@ -357,7 +383,7 @@
         return (viscosity * curves - normal * slopes).astype(BF16).astype(F32)
 
     wall_1 = wall(main)
-    wall_2 = wall(guess + C1 * wall_1)
+    wall_2 = wall(main + (gain + C1 * wall_1))
     back = pltpu.roll(wall_2, 96, 1)
     ahead = pltpu.roll(wall_2, 32, 1)
     out = jnp.where(group == 3, back, wall_1).reshape(32, 16, 128)
@@ -366,8 +392,8 @@
     send_ref[...] = jnp.concatenate([out, tail], axis=1).astype(BF16)
 
 
-def middle_body(wall_ref, field_ref, part_ref, low_ref, high_ref, slots_ref,
-                next_ref, tend_ref, up_ref, down_ref, table_ref, hot_ref):
+def middle_body(wall_ref, field_ref, part_ref, low_ref, high_ref, slots_ref, come_ref,
+                next_ref, tend_ref, up_ref, down_ref, table_ref):
     for a in range(3):
         for z in range(4):
             base = (a * 4 + z) * 16
@@ -375,11 +401,10 @@
             tend_ref[base : base + 16] = total
             next_ref[base : base + 16] = field_ref[base : base + 16] + C1 * total
     split_table(next_ref[...], table_ref)
-    for ref, out_ref, z, at in ((low_ref, down_ref, 0, 24), (high_ref, up_ref, 3, 0)):
-        tail = ref[FIELD_ROWS:SEND_ROWS, :].astype(F32)
-        row, col = tail_cells(tail, 4)
-        fill_columns(col, hot_ref)
-        seen = gather(table_ref[...], row, hot_ref)
+    ends = ((low_ref, down_ref, 0, 24), (high_ref, up_ref, 3, 0))
+    for i, (ref, out_ref, z, at) in enumerate(ends):
+        row, _ = tail_cells(tail_of(ref), 4)
+        seen = gather(table_ref[...], row, come_ref.at[i])
         lines = [plane(next_ref, a, z) for a in range(3)]
         lines.append(slots_ref[at : at + 24])
         lines += [jnp.concatenate(hi_lo(seen[a]), axis=1) for a in range(3)]
@@ -416,21 +441,18 @@
     lax.fori_loop(0, 3, step, 0)
 
 
-def arrivals_second(base_ref, field_ref, low_ref, high_ref, low2_ref, high2_ref, late_ref, dest_ref,
-                    out_ref, bubble_ref, hot_ref, load_ref):
-    field = field_ref[...]
+def arrivals_second(base_ref, field_ref, low_ref, high_ref, low2_ref, high2_ref, late_ref, dest_ref, come_ref,
+                    out_ref, bubble_ref, load_ref):
     sums = None
-    for ref, ref2 in ((low_ref, low2_ref), (high_ref, high2_ref)):
-        tail = ref[FIELD_ROWS:SEND_ROWS, :].astype(F32)
-        row, col = tail_cells(tail, 4)
-        fill_columns(col, hot_ref)
+    for i, (ref, ref2) in enumerate(((low_ref, low2_ref), (high_ref, high2_ref))):
+        row, _ = tail_cells(tail_of(ref), 4)
         extra = ref2[48:96, :].astype(F32)
         highs = [extra[a * 8 : a * 8 + 8, 0:128] for a in range(3)]
         lows = [extra[a * 8 : a * 8 + 8, 128:256] for a in range(3)]
         fill_values(row, highs, lows, load_ref)
-        got = scatter(load_ref, hot_ref)
+        got = scatter(load_ref, come_ref.at[i])
         sums = got if sums is None else sums + got
-    push = push_of(sums, field)
+    push = coupling * (sums[0:192] + sums[192:384])
     for a in range(3):
         for z in range(4):
             base = (a * 4 + z) * 16
@@ -472,29 +494,46 @@
     ids = pltpu.VMEM((24, 128), jnp.int32)
     packed = ((32, 24, 128), BF16)
 
-    sends = ((SEND_ROWS, 256), BF16)
-    up, down, moved = call(first_send, (sends, sends, ((16, 256), F32)))(field, bubble_vel, owner, dest)
+    velocity_in, bubbles_in, owner_in, dest_in = (
+        pltpu.with_memory_space_constraint(x, pltpu.HBM) for x in (field, bubble_vel, owner, dest)
+    )
+    up, down, moved, field, bubble_vel, owner, dest = pl.pallas_call(
+        first_send,
+        in_specs=[pl.BlockSpec(memory_space=pltpu.HBM)] * 4,
+        out_shape=(
+            pltpu.VMEM((SEND_ROWS, 256), BF16),
+            pltpu.VMEM((SEND_ROWS, 256), BF16),
+            pltpu.VMEM((16, 256), F32),
+            pltpu.VMEM((FIELD_ROWS, 256), F32),
+            pltpu.VMEM((3, 24, 128), F32),
+            pltpu.VMEM((2, 24, 128), jnp.int32),
+            pltpu.VMEM((2, 24), jnp.int32),
+        ),
+        scratch_shapes=[pltpu.SemaphoreType.DMA((4,))],
+    )(velocity_in, bubbles_in, owner_in, dest_in)
     low, high = shifted(up, 1), shifted(down, -1)
     part, seen = call(
         home_first, (block, rows), (table, ids, ids, hot, load, pltpu.VMEM((448, 256), F32))
     )(field, bubble_vel, owner, dest)
     part, to_columns = call(arrivals_first, (block, packed), (hot, load))(field, part, low, high)
     columns = exchange(to_columns)
-    rate, bubbles, slots, sums = call(
-        bubbles_first, (rows, rows, ((48, 256), F32), ((448, 256), F32)), (ids, ids, hot, load)
+    rate, bubbles, slots, sums, come = call(
+        bubbles_first,
+        (rows, rows, ((48, 256), F32), ((448, 256), F32), ((2, 256, 1024), BF16)),
+        (ids, ids, hot, load, pltpu.VMEM((64, 1024), BF16)),
     )(low, high, moved, seen, bubble_vel, owner, dest)
     (walls,) = call(columns_body, (packed,))(columns, first_deriv, second_deriv)
     walls = exchange(walls)
     lasts = ((LAST_ROWS, 256), BF16)
-    middle, tend, up, down = call(middle_body, (block, block, lasts, lasts), (table, hot))(
-        walls, field, part, low, high, slots
+    middle, tend, up, down = call(middle_body, (block, block, lasts, lasts), (table,))(
+        walls, field, part, low, high, slots, come
     )
     low2, high2 = shifted(up, 1), shifted(down, -1)
     base, late = call(home_second, (block, rows), (table, ids, ids, hot))(
         walls, middle, tend, sums, bubbles, rate, owner, dest
     )
-    field, bubbles = call(arrivals_second, (block, rows), (hot, load))(
-        base, middle, low, high, low2, high2, late, dest
+    field, bubbles = call(arrivals_second, (block, rows), (pltpu.VMEM((384, 1024), BF16),))(
+        base, middle, low, high, low2, high2, late, dest, come
     )
     return (field.reshape(velocity.shape), bubbles)
 

time: 76.3 us -> 72.8 us (0.954)
  local copies, waits for them, and re-layouts: 3.13 us -> 0.01 us
    unnamed x18 -> x4, local copies, waits for them, and re-layouts: 3.13 us -> 0.01 us
  transfers between devices with their start and end apart: 5 -> 5, of which waited for: 3 -> 3; matrix products, arithmetic and copies ran while one was open for 0% -> 0% of each run, Pallas kernels for 10% -> 11%
where the time goes in v1:
time: 72.8 us; the launch traced here: 72.5 us
  starting transfers between devices  19.6 us (27%)
  blocking collectives  19.5 us (27%)
  waiting for transfers between devices  18.5 us (25%)
  Pallas kernels  14.1 us (19%)
  between operations  0.74 us (1%)
    all_to_all x1, blocking collectives, exchange(): return lax.all_to_all(x, 'px', split_axis=0, concat_axis=0, tiled=True)  19.5 us
    ppermute x4, starting transfers between devices, shifted(): lax.ppermute(x, 'pz', [(i, (i + by) % length) for i in range(length)])  15.7 us
    ppermute x4, waiting for transfers between devices, shifted(): lax.ppermute(x, 'pz', [(i, (i + by) % length) for i in range(length)])  10.4 us
    all_to_all x1, waiting for transfers between devices, exchange(): return lax.all_to_all(x, 'px', split_axis=0, concat_axis=0, tiled=True)  8.06 us
    all_to_all x1, starting transfers between devices, exchange(): return lax.all_to_all(x, 'px', split_axis=0, concat_axis=0, tiled=True)  3.87 us
    pallas_call x1, Pallas kernels, on_device(): call(bubbles_first, (rows, rows, ((48, 256), F32), ((448, 256), F32), ((2...  2.89 us
    pallas_call x1, Pallas kernels, on_device(): call(home_first, (block, rows), (table, ids, ids, hot, load, pltpu.VMEM((...  2.49 us
    pallas_call x1, Pallas kernels, on_device(): call(home_second, (block, rows), (table, ids, ids, hot))  2.46 us
  transfers between devices with their start and end apart: 5, of which 3 were waited for; matrix products, arithmetic and copies ran while one was open for 0% of the time, Pallas kernels for 11%

profile of v1, /device:TPU:54, one launch (start us, length us, event | category | flops | bytes accessed | tf_op | source)
XLA Modules:
  0.0 72.5 jit_solution(2383453383090120228)
XLA Ops:
  0.6 1.4 %shard_map.77 = (bf16[240,256]{1,0:T(8,128)(2,1)S(1)}, bf16[240,256]{1,0:T(8,128)(2,1)S(1)}, f32[16,256]{1,0:T(8,128)S(1)}, f32[192,256]{1,0:T(8,128)S(1)}, f32[...) custom-call(f32[192,256]{1,0:T(8,128)} %bitcast.2, f32[3,24,128]{2,1,0:T(8,128)} %bubble_hbm.1, ...), custom_call_target="tpu_custom_call" | custom-call | tf_op jit(solution)/shard_map/pallas_call | solution.py:500
  2.0 7.1 %collective-permute-start = (bf16[240,256]{1,0:T(8,128)(2,1)S(1)}, bf16[240,256]{1,0:T(8,128)(2,1)S(1)}, u32[]{:S(2)}, u32[]{:S(2)}) collective-permute-start(bf16[240,256]{1,0:T(8,128)(2,1)S(1)} %get-tuple-element.31), channel_id=1, source_target_pairs={{0,1},{1,2},{2,3},{3,4},{4,5},{5,6},{6,7},{7,8},{8,9},{9,10},{10,1... | collective-permute-start | bytes 368648 | tf_op jit(solution)/shard_map/ppermute | solution.py:480
  9.1 1.9 %collective-permute-start.1 = (bf16[240,256]{1,0:T(8,128)(2,1)S(1)}, bf16[240,256]{1,0:T(8,128)(2,1)S(1)}, u32[]{:S(2)}, u32[]{:S(2)}) collective-permute-start(bf16[240,256]{1,0:T(8,128)(2,1)S(1)} %get-tuple-element.32), channel_id=1, source_target_pairs={{0,15},{1,0},{2,1},{3,2},{4,3},{5,4},{6,5},{7,6},{8,7},{9,8},{10,9... | collective-permute-start | bytes 368648 | tf_op jit(solution)/shard_map/ppermute | solution.py:480
  11.0 0.0 copy-start.1
  11.0 2.5 %shard_map.78 = (f32[192,256]{1,0:T(8,128)S(1)}, f32[3,24,128]{2,1,0:T(8,128)S(1)}) custom-call(f32[192,256]{1,0:T(8,128)S(1)} %get-tuple-element.26.field_ref, f32[3,24,128]{2,1,0:T(8,128)S(1)} %get-tuple-element.27.bubble_ref, s32[2,24,128]{2,1,0:T(8,128)S(1)} %get-tuple-element.28.owner_ref, s32[2,24]{1,0:T(2,128)S(1)} %get-tuple-element.29.dest_ref), custom_call_target="tpu_custom_call" | custom-call | tf_op jit(solution)/shard_map/pallas_call | solution.py:515
  13.5 0.0 copy-start
  13.5 0.0 collective-permute-done.low_ref
  13.6 6.5 %collective-permute-done.1.high_ref = bf16[240,256]{1,0:T(8,128)(2,1)S(1)} collective-permute-done((bf16[240,256]{1,0:T(8,128)(2,1)S(1)}, bf16[240,256]{1,0:T(8,128)(2,1)S(1)}, u32[]{:S(2)}, u32[]{:S(2)}) %collective-permute-start.1) | collective-permute-done | bytes 122912 | tf_op jit(solution)/shard_map/ppermute | solution.py:480
  20.1 1.1 %shard_map.79 = (f32[192,256]{1,0:T(8,128)S(1)}, bf16[32,24,128]{2,1,0:T(8,128)(2,1)S(1)}) custom-call(f32[192,256]{1,0:T(8,128)S(1)} %get-tuple-element.26.field_ref, f32[192,256]{1,0:T(8,128)S(1)} %get-tuple-element.30.part_ref, bf16[240,256]{1,0:T(8,128)(2,1)S(1)} %collective-permute-done.low_ref, bf16[240,256]{1,0:T(8,128)(2,1)S(1)} %collective-permute-done.1.high_ref), custom_call_target="tpu_custom_call" | custom-call | tf_op jit(solution)/shard_map/pallas_call | solution.py:518
  21.2 19.5 %all_to_all.10.got_ref = bf16[32,24,128]{2,1,0:T(8,128)(2,1)S(1)} all-to-all(bf16[32,24,128]{2,1,0:T(8,128)(2,1)S(1)} %get-tuple-element.33), channel_id=1, replica_groups=mesh['px'=32,'pz'=16] {'px'}, dimensions={0} | all-to-all | bytes 393216 | tf_op jit(solution)/shard_map/all_to_all | solution.py:484
  40.7 0.0 copy-done.1
  40.7 0.0 copy-done
  40.7 1.6 %shard_map.80 = bf16[32,24,128]{2,1,0:T(8,128)(2,1)} custom-call(bf16[32,24,128]{2,1,0:T(8,128)(2,1)S(1)} %all_to_all.10.got_ref, bf16[512,512]{1,0:T(8,128)(2,1)S(1)} %copy-done, bf16[512,512]{1,0:T(8,128)(2,1)S(1)} %copy-done.1), custom_call_target="tpu_custom_call" | custom-call | tf_op jit(solution)/shard_map/pallas_call | solution.py:525
  42.3 3.9 %all-to-all-start.1 = ((bf16[32,24,128]{2,1,0:T(8,128)(2,1)}), bf16[32,24,128]{2,1,0:T(8,128)(2,1)S(1)}, u32[]{:S(2)}, u32[]{:S(2)}) async-start(bf16[32,24,128]{2,1,0:T(8,128)(2,1)} %shard_map.80), calls=%async_computation.1 | async-start | bytes 393216 | tf_op jit(solution)/shard_map/all_to_all | solution.py:484
  46.2 2.9 %shard_map.81 = (f32[3,24,128]{2,1,0:T(8,128)S(1)}, f32[3,24,128]{2,1,0:T(8,128)S(1)}, f32[48,256]{1,0:T(8,128)S(1)}, f32[448,256]{1,0:T(8,128)S(1)}, bf16[2,256,1024]{2,1,0:T(8,128)(2,1)S(1)}) custom-call(bf16[240,256]{1,0:T(8,128)(2,1)S(1)} %collective-permute-done.low_ref, bf16[240,256]{1,0:T(8,128)(2,1)S(1)} %collective-permute-done.1.high_ref, ...), custom_call_target="tpu_custom_call" | custom-call | tf_op jit(solution)/shard_map/pallas_call | solution.py:520
  49.1 8.1 %all-to-all-done.1.wall_ref = bf16[32,24,128]{2,1,0:T(8,128)(2,1)S(1)} async-done(((bf16[32,24,128]{2,1,0:T(8,128)(2,1)}), bf16[32,24,128]{2,1,0:T(8,128)(2,1)S(1)}, u32[]{:S(2)}, u32[]{:S(2)}) %all-to-all-start.1) | async-done | bytes 196640 | tf_op jit(solution)/shard_map/all_to_all | solution.py:484
  57.1 0.7 shard_map.82
  57.8 1.9 %collective-permute-start.2 = (bf16[96,256]{1,0:T(8,128)(2,1)S(1)}, bf16[96,256]{1,0:T(8,128)(2,1)S(1)}, u32[]{:S(2)}, u32[]{:S(2)}) collective-permute-start(bf16[96,256]{1,0:T(8,128)(2,1)S(1)} %get-tuple-element.45), channel_id=1, source_target_pairs={{0,1},{1,2},{2,3},{3,4},{4,5},{5,6},{6,7},{7,8},{8,9},{9,10},{10,1... | collective-permute-start | bytes 147464 | tf_op jit(solution)/shard_map/ppermute | solution.py:480
  59.7 4.8 %collective-permute-start.3 = (bf16[96,256]{1,0:T(8,128)(2,1)S(1)}, bf16[96,256]{1,0:T(8,128)(2,1)S(1)}, u32[]{:S(2)}, u32[]{:S(2)}) collective-permute-start(bf16[96,256]{1,0:T(8,128)(2,1)S(1)} %get-tuple-element.46), channel_id=1, source_target_pairs={{0,15},{1,0},{2,1},{3,2},{4,3},{5,4},{6,5},{7,6},{8,7},{9,8},{10,9... | collective-permute-start | bytes 147464 | tf_op jit(solution)/shard_map/ppermute | solution.py:480
  64.6 2.5 %shard_map.83 = (f32[192,256]{1,0:T(8,128)S(1)}, f32[3,24,128]{2,1,0:T(8,128)S(1)}) custom-call(bf16[32,24,128]{2,1,0:T(8,128)(2,1)S(1)} %all-to-all-done.1.wall_ref, f32[192,256]{1,0:T(8,128)S(1)} %get-tuple-element.39.field_ref, f32[192,256]{1,0:T(8,128)S(1)} %get-tuple-element.40.tend_ref, f32[448,256]{1,0:T(8,128)S(1)} %get-tuple-element.41.sum_ref, ...), custom_call_target="tpu_custom_call" | custom-call | tf_op jit(solution)/shard_map/pallas_call | solution.py:532
  67.0 0.0 collective-permute-done.2.low2_ref
  67.0 3.9 %collective-permute-done.3.high2_ref = bf16[96,256]{1,0:T(8,128)(2,1)S(1)} collective-permute-done((bf16[96,256]{1,0:T(8,128)(2,1)S(1)}, bf16[96,256]{1,0:T(8,128)(2,1)S(1)}, u32[]{:S(2)}, u32[]{:S(2)}) %collective-permute-start.3) | collective-permute-done | bytes 49184 | tf_op jit(solution)/shard_map/ppermute | solution.py:480
  70.9 1.5 %shard_map.84 = (f32[192,256]{1,0:T(8,128)}, f32[3,24,128]{2,1,0:T(8,128)}) custom-call(f32[192,256]{1,0:T(8,128)S(1)} %get-tuple-element.44.base_ref, f32[192,256]{1,0:T(8,128)S(1)} %get-tuple-element.39.field_ref, bf16[240,256]{1,0:T(8,128)(2,1)S(1)} %collective-permute-done.low_ref, bf16[240,256]{1,0:T(8,128)(2,1)S(1)} %collective-permute-done.1.high_ref, ...), custom_call_target="tpu_custom_call" | custom-call | tf_op jit(solution)/shard_map/pallas_call | solution.py:535
Async XLA Ops:
  2.0 11.5 %collective-permute-start = (bf16[240,256]{1,0:T(8,128)(2,1)S(1)}, bf16[240,256]{1,0:T(8,128)(2,1)S(1)}, u32[]{:S(2)}, u32[]{:S(2)}) collective-permute-start(bf16[240,256]{1,0:T(8,128)(2,1)S(1)} %get-tuple-element.31), channel_id=1, source_target_pairs={{0,1},{1,2},{2,3},{3,4},{4,5},{5,6},{6,7},{7,8},{8,9},{9,10},{10,1... | collective-permute-start | bytes 368648 | tf_op jit(solution)/shard_map/ppermute | solution.py:480
  9.1 11.0 %collective-permute-start.1 = (bf16[240,256]{1,0:T(8,128)(2,1)S(1)}, bf16[240,256]{1,0:T(8,128)(2,1)S(1)}, u32[]{:S(2)}, u32[]{:S(2)}) collective-permute-start(bf16[240,256]{1,0:T(8,128)(2,1)S(1)} %get-tuple-element.32), channel_id=1, source_target_pairs={{0,15},{1,0},{2,1},{3,2},{4,3},{5,4},{6,5},{7,6},{8,7},{9,8},{10,9... | collective-permute-start | bytes 368648 | tf_op jit(solution)/shard_map/ppermute | solution.py:480
  11.0 29.7 %copy-start.1 = (bf16[512,512]{1,0:T(8,128)(2,1)S(1)}, bf16[512,512]{1,0:T(8,128)(2,1)}, u32[]{:S(2)}) copy-start(bf16[512,512]{1,0:T(8,128)(2,1)} %second_ref.1) | copy-start | bytes 1572868
  13.5 27.2 %copy-start = (bf16[512,512]{1,0:T(8,128)(2,1)S(1)}, bf16[512,512]{1,0:T(8,128)(2,1)}, u32[]{:S(2)}) copy-start(bf16[512,512]{1,0:T(8,128)(2,1)} %first_ref.1) | copy-start | bytes 1572868
  42.3 14.8 %all-to-all-start.1 = ((bf16[32,24,128]{2,1,0:T(8,128)(2,1)}), bf16[32,24,128]{2,1,0:T(8,128)(2,1)S(1)}, u32[]{:S(2)}, u32[]{:S(2)}) async-start(bf16[32,24,128]{2,1,0:T(8,128)(2,1)} %shard_map.80), calls=%async_computation.1 | async-start | bytes 393216 | tf_op jit(solution)/shard_map/all_to_all | solution.py:484
  57.8 9.2 %collective-permute-start.2 = (bf16[96,256]{1,0:T(8,128)(2,1)S(1)}, bf16[96,256]{1,0:T(8,128)(2,1)S(1)}, u32[]{:S(2)}, u32[]{:S(2)}) collective-permute-start(bf16[96,256]{1,0:T(8,128)(2,1)S(1)} %get-tuple-element.45), channel_id=1, source_target_pairs={{0,1},{1,2},{2,3},{3,4},{4,5},{5,6},{6,7},{7,8},{8,9},{9,10},{10,1... | collective-permute-start | bytes 147464 | tf_op jit(solution)/shard_map/ppermute | solution.py:480
  59.7 11.2 %collective-permute-start.3 = (bf16[96,256]{1,0:T(8,128)(2,1)S(1)}, bf16[96,256]{1,0:T(8,128)(2,1)S(1)}, u32[]{:S(2)}, u32[]{:S(2)}) collective-permute-start(bf16[96,256]{1,0:T(8,128)(2,1)S(1)} %get-tuple-element.46), channel_id=1, source_target_pairs={{0,15},{1,0},{2,1},{3,2},{4,3},{5,4},{6,5},{7,6},{8,7},{9,8},{10,9... | collective-permute-start | bytes 147464 | tf_op jit(solution)/shard_map/ppermute | solution.py:480

commit v2 on v1

--- a/solution.py
+++ b/solution.py
@@ -56,7 +56,7 @@
     slot = iota((16, 24), 0)
     marks = jnp.where(slot < 8, jnp.broadcast_to(up, (16, 24)), jnp.broadcast_to(down, (16, 24)))
     before = jnp.where(iota((24, 24), 0) < iota((24, 24), 1), 1.0, 0.0).astype(F32)
-    rank = exact_dot(marks, before)
+    rank = jnp.dot(marks.astype(BF16), before.astype(BF16), preferred_element_type=F32)
     wanted = jnp.where(slot < 8, slot, slot - 8).astype(F32)
     return jnp.where((rank == wanted) & (marks > 0.5), 1.0, 0.0).astype(F32)
 
@@ -172,9 +172,11 @@
     return total + forcing if a == 0 else total
 
 
-def halo_term(f_ref, below, above, a, z):
-    if z == 0:
-        return (viscosity + 0.5 * plane(f_ref, 2, 0)) * below
+def below_term(f_ref, below):
+    return (viscosity + 0.5 * plane(f_ref, 2, 0)) * below
+
+
+def above_term(f_ref, above):
     return (viscosity - 0.5 * plane(f_ref, 2, 3)) * above
 
 
@@ -191,17 +193,18 @@
     for copy in copies[:3]:
         copy.wait()
     first, second = owner_ref[0], owner_ref[1]
-    columns = [bubble_ref[a] for a in range(3)]
-    columns += [((first >> 8) + 1).astype(F32), (first & 255).astype(F32)]
-    picked = exact_dot(pick_matrix(dest_ref[0:1]), jnp.concatenate(columns, axis=1))
+    parts = []
+    for a in range(3):
+        parts += hi_lo(bubble_ref[a])
+    parts += [((first >> 8) + 1).astype(F32), (first & 255).astype(F32)]
+    parts = jnp.concatenate(parts, axis=1).astype(BF16)
+    picked = jnp.dot(pick_matrix(dest_ref[0:1]).astype(BF16), parts, preferred_element_type=F32)
     later = jnp.concatenate([((second >> 8) + 1).astype(F32), (second & 255).astype(F32)], axis=1)
-    later = exact_dot(pick_matrix(dest_ref[1:2]), later)
-    moved_ref[...] = picked[:, 384:640]
+    later = jnp.dot(pick_matrix(dest_ref[1:2]).astype(BF16), later.astype(BF16), preferred_element_type=F32)
+    moved_ref[...] = picked[:, 768:1024]
     for ref, at in ((up_ref, 0), (down_ref, 8)):
-        lines = []
-        for a in range(3):
-            lines.append(jnp.concatenate(hi_lo(picked[at : at + 8, a * 128 : (a + 1) * 128]), axis=1))
-        lines += [picked[at : at + 8, 384:640], later[at : at + 8], jnp.zeros((8, 256), F32)]
+        lines = [picked[at : at + 8, i * 256 : (i + 1) * 256] for i in range(4)]
+        lines += [later[at : at + 8], jnp.zeros((8, 256), F32)]
         ref[FIELD_ROWS:SEND_ROWS] = jnp.concatenate(lines, axis=0).astype(BF16)
     copies[3].wait()
     block = field_ref[...].astype(BF16)
@@ -289,26 +292,35 @@
     return jnp.concatenate(halves, axis=1)
 
 
-def arrivals_first(field_ref, part_ref, low_ref, high_ref, tend_ref, send_ref, hot_ref, load_ref):
-    field = field_ref[...]
-    sums = None
-    for ref in (low_ref, high_ref):
-        tail = tail_of(ref)
-        row, col = tail_cells(tail, 3)
-        fill_columns(col, hot_ref)
-        highs = [tail[a * 8 : a * 8 + 8, 0:128] for a in range(3)]
-        lows = [tail[a * 8 : a * 8 + 8, 128:256] for a in range(3)]
-        fill_values(row, highs, lows, load_ref)
-        got = scatter(load_ref, hot_ref)
-        sums = got if sums is None else sums + got
-    push = push_of(sums, field)
+def arrived(cells_ref, values_ref, first_line, cell_line, load_ref):
+    row, col = tail_cells(tail_of(cells_ref), cell_line)
+    tail = values_ref[first_line : first_line + 48, :].astype(F32)
+    highs = [tail[a * 8 : a * 8 + 8, 0:128] for a in range(3)]
+    lows = [tail[a * 8 : a * 8 + 8, 128:256] for a in range(3)]
+    fill_values(row, highs, lows, load_ref)
+    return col
+
+
+def low_first(field_ref, part_ref, low_ref, out_ref, hot_ref, load_ref):
+    fill_columns(arrived(low_ref, low_ref, FIELD_ROWS, 3, load_ref), hot_ref)
+    push = push_of(scatter(load_ref, hot_ref), field_ref[...])
+    for a in range(3):
+        for z in range(4):
+            base = (a * 4 + z) * 16
+            total = part_ref[base : base + 16] + push[base : base + 16]
+            out_ref[base : base + 16] = total + below_term(field_ref, plane(low_ref, a, 3)) if z == 0 else total
+
+
+def high_first(field_ref, part_ref, high_ref, tend_ref, send_ref, hot_ref, load_ref):
+    fill_columns(arrived(high_ref, high_ref, FIELD_ROWS, 3, load_ref), hot_ref)
+    push = push_of(scatter(load_ref, hot_ref), field_ref[...])
     six = [[None] * 4 for _ in range(6)]
     for a in range(3):
         for z in range(4):
             base = (a * 4 + z) * 16
             total = part_ref[base : base + 16] + push[base : base + 16]
-            if z == 0 or z == 3:
-                total = total + halo_term(field_ref, plane(low_ref, a, 3), plane(high_ref, a, 0), a, z)
+            if z == 3:
+                total = total + above_term(field_ref, plane(high_ref, a, 0))
             tend_ref[base : base + 16] = total
             here = field_ref[base : base + 16]
             six[a][z] = here
@@ -441,30 +453,27 @@
     lax.fori_loop(0, 3, step, 0)
 
 
-def arrivals_second(base_ref, field_ref, low_ref, high_ref, low2_ref, high2_ref, late_ref, dest_ref, come_ref,
-                    out_ref, bubble_ref, load_ref):
-    sums = None
-    for i, (ref, ref2) in enumerate(((low_ref, low2_ref), (high_ref, high2_ref))):
-        row, _ = tail_cells(tail_of(ref), 4)
-        extra = ref2[48:96, :].astype(F32)
-        highs = [extra[a * 8 : a * 8 + 8, 0:128] for a in range(3)]
-        lows = [extra[a * 8 : a * 8 + 8, 128:256] for a in range(3)]
-        fill_values(row, highs, lows, load_ref)
-        got = scatter(load_ref, come_ref.at[i])
-        sums = got if sums is None else sums + got
-    push = coupling * (sums[0:192] + sums[192:384])
-    for a in range(3):
-        for z in range(4):
-            base = (a * 4 + z) * 16
-            total = push[base : base + 16]
-            if z == 0 or z == 3:
-                below = low2_ref[a * 16 : a * 16 + 16, :].astype(F32)
-                above = high2_ref[a * 16 : a * 16 + 16, :].astype(F32)
-                total = total + halo_term(field_ref, below, above, a, z)
-            out_ref[base : base + 16] = base_ref[base : base + 16] + C2 * total
-    from_high = high2_ref[48:96, :].astype(F32)
-    from_low = low2_ref[48:96, :].astype(F32)
+def late_sum(cells_ref, values_ref, i, come_ref, load_ref):
+    arrived(cells_ref, values_ref, 48, 4, load_ref)
+    sums = scatter(load_ref, come_ref.at[i])
+    return C2 * coupling * (sums[0:192] + sums[192:384])
+
+
+def low_second(base_ref, field_ref, low_ref, low2_ref, come_ref, out_ref, load_ref):
+    push = late_sum(low_ref, low2_ref, 0, come_ref, load_ref)
+    for a in range(3):
+        for z in range(4):
+            base = (a * 4 + z) * 16
+            total = base_ref[base : base + 16] + push[base : base + 16]
+            if z == 0:
+                total = total + C2 * below_term(field_ref, low2_ref[a * 16 : a * 16 + 16, :].astype(F32))
+            out_ref[base : base + 16] = total
+
+
+def high_second(base_ref, field_ref, high_ref, low2_ref, high2_ref, late_ref, dest_ref, come_ref,
+                out_ref, bubble_ref, load_ref):
     found = []
+    from_low, from_high = low2_ref[48:96, :].astype(F32), high2_ref[48:96, :].astype(F32)
     for a in range(3):
         line = 24 + a * 8
         high = from_high[line : line + 8, 0:128] + from_high[line : line + 8, 128:256]
@@ -473,6 +482,14 @@
     back = exact_dot(put_matrix(dest_ref[1:2]), jnp.concatenate(found, axis=1))
     for a in range(3):
         bubble_ref[a] = late_ref[a] + (C2 / relax_time) * back[:, a * 128 : (a + 1) * 128]
+    push = late_sum(high_ref, high2_ref, 1, come_ref, load_ref)
+    for a in range(3):
+        for z in range(4):
+            base = (a * 4 + z) * 16
+            total = base_ref[base : base + 16] + push[base : base + 16]
+            if z == 3:
+                total = total + C2 * above_term(field_ref, high2_ref[a * 16 : a * 16 + 16, :].astype(F32))
+            out_ref[base : base + 16] = total
 
 
 def shifted(x, by):
@@ -515,7 +532,8 @@
     part, seen = call(
         home_first, (block, rows), (table, ids, ids, hot, load, pltpu.VMEM((448, 256), F32))
     )(field, bubble_vel, owner, dest)
-    part, to_columns = call(arrivals_first, (block, packed), (hot, load))(field, part, low, high)
+    (part,) = call(low_first, (block,), (hot, load))(field, part, low)
+    part, to_columns = call(high_first, (block, packed), (hot, load))(field, part, high)
     columns = exchange(to_columns)
     rate, bubbles, slots, sums, come = call(
         bubbles_first,
@@ -532,8 +550,10 @@
     base, late = call(home_second, (block, rows), (table, ids, ids, hot))(
         walls, middle, tend, sums, bubbles, rate, owner, dest
     )
-    field, bubbles = call(arrivals_second, (block, rows), (pltpu.VMEM((384, 1024), BF16),))(
-        base, middle, low, high, low2, high2, late, dest, come
+    late_load = pltpu.VMEM((384, 1024), BF16)
+    (base,) = call(low_second, (block,), (late_load,))(base, middle, low, low2, come)
+    field, bubbles = call(high_second, (block, rows), (late_load,))(
+        base, middle, high, low2, high2, late, dest, come
     )
     return (field.reshape(velocity.shape), bubbles)
 

time: 72.8 us -> 71.9 us (0.988)
  waiting for transfers between devices: 18.5 us -> 17.6 us
    ppermute x4, waiting for transfers between devices: 10.4 us -> 9.49 us  [shifted(): lax.ppermute(x, 'pz', [(i, (i + by) % length) for i in range(length)])]
    pallas_call x2 -> x4, Pallas kernels: 2.67 us -> 2.89 us  [the longest x1 1.24 us: on_device(): call(high_second, (block, rows), (late_load,))]
  transfers between devices with their start and end apart: 5 -> 5, of which waited for: 3 -> 3; matrix products, arithmetic and copies ran while one was open for 0% -> 0% of each run, Pallas kernels for 11% -> 12%
where the time goes in v2:
time: 71.9 us; the launch traced here: 71.6 us
  starting transfers between devices  19.6 us (27%)
  blocking collectives  19.5 us (27%)
  waiting for transfers between devices  17.6 us (24%)
  Pallas kernels  14.2 us (20%)
  between operations  0.76 us (1%)
    all_to_all x1, blocking collectives, exchange(): return lax.all_to_all(x, 'px', split_axis=0, concat_axis=0, tiled=True)  19.5 us
    ppermute x4, starting transfers between devices, shifted(): lax.ppermute(x, 'pz', [(i, (i + by) % length) for i in range(length)])  15.7 us
    ppermute x4, waiting for transfers between devices, shifted(): lax.ppermute(x, 'pz', [(i, (i + by) % length) for i in range(length)])  9.49 us
    all_to_all x1, waiting for transfers between devices, exchange(): return lax.all_to_all(x, 'px', split_axis=0, concat_axis=0, tiled=True)  8.08 us
    all_to_all x1, starting transfers between devices, exchange(): return lax.all_to_all(x, 'px', split_axis=0, concat_axis=0, tiled=True)  3.87 us
    pallas_call x1, Pallas kernels, on_device(): call(bubbles_first, (rows, rows, ((48, 256), F32), ((448, 256), F32), ((2...  2.86 us
    pallas_call x1, Pallas kernels, on_device(): call(home_first, (block, rows), (table, ids, ids, hot, load, pltpu.VMEM((...  2.49 us
    pallas_call x1, Pallas kernels, on_device(): call(home_second, (block, rows), (table, ids, ids, hot))  2.46 us
  transfers between devices with their start and end apart: 5, of which 3 were waited for; matrix products, arithmetic and copies ran while one was open for 0% of the time, Pallas kernels for 12%

profile of v2, /device:TPU:54, one launch (start us, length us, event | category | flops | bytes accessed | tf_op | source)
XLA Modules:
  0.0 71.6 jit_solution(10183538951281830868)
XLA Ops:
  0.6 1.2 %shard_map.77 = (bf16[240,256]{1,0:T(8,128)(2,1)S(1)}, bf16[240,256]{1,0:T(8,128)(2,1)S(1)}, f32[16,256]{1,0:T(8,128)S(1)}, f32[192,256]{1,0:T(8,128)S(1)}, f32[...) custom-call(f32[192,256]{1,0:T(8,128)} %bitcast.2, f32[3,24,128]{2,1,0:T(8,128)} %bubble_hbm.1, ...), custom_call_target="tpu_custom_call" | custom-call | tf_op jit(solution)/shard_map/pallas_call | solution.py:517
  1.9 7.1 %collective-permute-start = (bf16[240,256]{1,0:T(8,128)(2,1)S(1)}, bf16[240,256]{1,0:T(8,128)(2,1)S(1)}, u32[]{:S(2)}, u32[]{:S(2)}) collective-permute-start(bf16[240,256]{1,0:T(8,128)(2,1)S(1)} %get-tuple-element.31), channel_id=1, source_target_pairs={{0,1},{1,2},{2,3},{3,4},{4,5},{5,6},{6,7},{7,8},{8,9},{9,10},{10,1... | collective-permute-start | bytes 368648 | tf_op jit(solution)/shard_map/ppermute | solution.py:497
  8.9 1.9 %collective-permute-start.1 = (bf16[240,256]{1,0:T(8,128)(2,1)S(1)}, bf16[240,256]{1,0:T(8,128)(2,1)S(1)}, u32[]{:S(2)}, u32[]{:S(2)}) collective-permute-start(bf16[240,256]{1,0:T(8,128)(2,1)S(1)} %get-tuple-element.32), channel_id=1, source_target_pairs={{0,15},{1,0},{2,1},{3,2},{4,3},{5,4},{6,5},{7,6},{8,7},{9,8},{10,9... | collective-permute-start | bytes 368648 | tf_op jit(solution)/shard_map/ppermute | solution.py:497
  10.9 2.5 %shard_map.78 = (f32[192,256]{1,0:T(8,128)S(1)}, f32[3,24,128]{2,1,0:T(8,128)S(1)}) custom-call(f32[192,256]{1,0:T(8,128)S(1)} %get-tuple-element.26.field_ref, f32[3,24,128]{2,1,0:T(8,128)S(1)} %get-tuple-element.27.bubble_ref, s32[2,24,128]{2,1,0:T(8,128)S(1)} %get-tuple-element.28.owner_ref, s32[2,24]{1,0:T(2,128)S(1)} %get-tuple-element.29.dest_ref), custom_call_target="tpu_custom_call" | custom-call | tf_op jit(solution)/shard_map/pallas_call | solution.py:532
  13.4 0.0 collective-permute-done.low_ref
  13.4 0.0 copy-start.1
  13.4 0.5 shard_map.79.part_ref
  13.9 0.0 copy-start
  13.9 6.0 %collective-permute-done.1.high_ref = bf16[240,256]{1,0:T(8,128)(2,1)S(1)} collective-permute-done((bf16[240,256]{1,0:T(8,128)(2,1)S(1)}, bf16[240,256]{1,0:T(8,128)(2,1)S(1)}, u32[]{:S(2)}, u32[]{:S(2)}) %collective-permute-start.1) | collective-permute-done | bytes 122912 | tf_op jit(solution)/shard_map/ppermute | solution.py:497
  19.9 0.7 shard_map.80
  20.7 19.5 %all_to_all.10.got_ref = bf16[32,24,128]{2,1,0:T(8,128)(2,1)S(1)} all-to-all(bf16[32,24,128]{2,1,0:T(8,128)(2,1)S(1)} %get-tuple-element.33), channel_id=1, replica_groups=mesh['px'=32,'pz'=16] {'px'}, dimensions={0} | all-to-all | bytes 393216 | tf_op jit(solution)/shard_map/all_to_all | solution.py:501
  40.1 0.0 copy-done.1
  40.1 0.0 copy-done
  40.1 1.6 %shard_map.81 = bf16[32,24,128]{2,1,0:T(8,128)(2,1)} custom-call(bf16[32,24,128]{2,1,0:T(8,128)(2,1)S(1)} %all_to_all.10.got_ref, bf16[512,512]{1,0:T(8,128)(2,1)S(1)} %copy-done, bf16[512,512]{1,0:T(8,128)(2,1)S(1)} %copy-done.1), custom_call_target="tpu_custom_call" | custom-call | tf_op jit(solution)/shard_map/pallas_call | solution.py:543
  41.7 3.9 %all-to-all-start.1 = ((bf16[32,24,128]{2,1,0:T(8,128)(2,1)}), bf16[32,24,128]{2,1,0:T(8,128)(2,1)S(1)}, u32[]{:S(2)}, u32[]{:S(2)}) async-start(bf16[32,24,128]{2,1,0:T(8,128)(2,1)} %shard_map.81), calls=%async_computation.1 | async-start | bytes 393216 | tf_op jit(solution)/shard_map/all_to_all | solution.py:501
  45.6 2.9 %shard_map.82 = (f32[3,24,128]{2,1,0:T(8,128)S(1)}, f32[3,24,128]{2,1,0:T(8,128)S(1)}, f32[48,256]{1,0:T(8,128)S(1)}, f32[448,256]{1,0:T(8,128)S(1)}, bf16[2,256,1024]{2,1,0:T(8,128)(2,1)S(1)}) custom-call(bf16[240,256]{1,0:T(8,128)(2,1)S(1)} %collective-permute-done.low_ref, bf16[240,256]{1,0:T(8,128)(2,1)S(1)} %collective-permute-done.1.high_ref, ...), custom_call_target="tpu_custom_call" | custom-call | tf_op jit(solution)/shard_map/pallas_call | solution.py:538
  48.5 8.1 %all-to-all-done.1.wall_ref = bf16[32,24,128]{2,1,0:T(8,128)(2,1)S(1)} async-done(((bf16[32,24,128]{2,1,0:T(8,128)(2,1)}), bf16[32,24,128]{2,1,0:T(8,128)(2,1)S(1)}, u32[]{:S(2)}, u32[]{:S(2)}) %all-to-all-start.1) | async-done | bytes 196640 | tf_op jit(solution)/shard_map/all_to_all | solution.py:501
  56.5 0.7 shard_map.83
  57.2 1.9 %collective-permute-start.2 = (bf16[96,256]{1,0:T(8,128)(2,1)S(1)}, bf16[96,256]{1,0:T(8,128)(2,1)S(1)}, u32[]{:S(2)}, u32[]{:S(2)}) collective-permute-start(bf16[96,256]{1,0:T(8,128)(2,1)S(1)} %get-tuple-element.45), channel_id=1, source_target_pairs={{0,1},{1,2},{2,3},{3,4},{4,5},{5,6},{6,7},{7,8},{8,9},{9,10},{10,1... | collective-permute-start | bytes 147464 | tf_op jit(solution)/shard_map/ppermute | solution.py:497
  59.1 4.8 %collective-permute-start.3 = (bf16[96,256]{1,0:T(8,128)(2,1)S(1)}, bf16[96,256]{1,0:T(8,128)(2,1)S(1)}, u32[]{:S(2)}, u32[]{:S(2)}) collective-permute-start(bf16[96,256]{1,0:T(8,128)(2,1)S(1)} %get-tuple-element.46), channel_id=1, source_target_pairs={{0,15},{1,0},{2,1},{3,2},{4,3},{5,4},{6,5},{7,6},{8,7},{9,8},{10,9... | collective-permute-start | bytes 147464 | tf_op jit(solution)/shard_map/ppermute | solution.py:497
  64.0 2.5 %shard_map.84 = (f32[192,256]{1,0:T(8,128)S(1)}, f32[3,24,128]{2,1,0:T(8,128)S(1)}) custom-call(bf16[32,24,128]{2,1,0:T(8,128)(2,1)S(1)} %all-to-all-done.1.wall_ref, f32[192,256]{1,0:T(8,128)S(1)} %get-tuple-element.39.field_ref, f32[192,256]{1,0:T(8,128)S(1)} %get-tuple-element.40.tend_ref, f32[448,256]{1,0:T(8,128)S(1)} %get-tuple-element.41.sum_ref, ...), custom_call_target="tpu_custom_call" | custom-call | tf_op jit(solution)/shard_map/pallas_call | solution.py:550
  66.4 0.0 collective-permute-done.2.low2_ref
  66.5 0.4 shard_map.85.base_ref
  66.9 3.5 %collective-permute-done.3.high2_ref = bf16[96,256]{1,0:T(8,128)(2,1)S(1)} collective-permute-done((bf16[96,256]{1,0:T(8,128)(2,1)S(1)}, bf16[96,256]{1,0:T(8,128)(2,1)S(1)}, u32[]{:S(2)}, u32[]{:S(2)}) %collective-permute-start.3) | collective-permute-done | bytes 49184 | tf_op jit(solution)/shard_map/ppermute | solution.py:497
  70.4 1.2 %shard_map.86 = (f32[192,256]{1,0:T(8,128)}, f32[3,24,128]{2,1,0:T(8,128)}) custom-call(f32[192,256]{1,0:T(8,128)S(1)} %shard_map.85.base_ref, f32[192,256]{1,0:T(8,128)S(1)} %get-tuple-element.39.field_ref, bf16[240,256]{1,0:T(8,128)(2,1)S(1)} %collective-permute-done.1.high_ref, bf16[96,256]{1,0:T(8,128)(2,1)S(1)} %collective-permute-done.2.low2_ref, ...), custom_call_target="tpu_custom_call" | custom-call | tf_op jit(solution)/shard_map/pallas_call | solution.py:555
Async XLA Ops:
  1.9 11.5 %collective-permute-start = (bf16[240,256]{1,0:T(8,128)(2,1)S(1)}, bf16[240,256]{1,0:T(8,128)(2,1)S(1)}, u32[]{:S(2)}, u32[]{:S(2)}) collective-permute-start(bf16[240,256]{1,0:T(8,128)(2,1)S(1)} %get-tuple-element.31), channel_id=1, source_target_pairs={{0,1},{1,2},{2,3},{3,4},{4,5},{5,6},{6,7},{7,8},{8,9},{9,10},{10,1... | collective-permute-start | bytes 368648 | tf_op jit(solution)/shard_map/ppermute | solution.py:497
  8.9 11.0 %collective-permute-start.1 = (bf16[240,256]{1,0:T(8,128)(2,1)S(1)}, bf16[240,256]{1,0:T(8,128)(2,1)S(1)}, u32[]{:S(2)}, u32[]{:S(2)}) collective-permute-start(bf16[240,256]{1,0:T(8,128)(2,1)S(1)} %get-tuple-element.32), channel_id=1, source_target_pairs={{0,15},{1,0},{2,1},{3,2},{4,3},{5,4},{6,5},{7,6},{8,7},{9,8},{10,9... | collective-permute-start | bytes 368648 | tf_op jit(solution)/shard_map/ppermute | solution.py:497
  13.4 26.8 %copy-start.1 = (bf16[512,512]{1,0:T(8,128)(2,1)S(1)}, bf16[512,512]{1,0:T(8,128)(2,1)}, u32[]{:S(2)}) copy-start(bf16[512,512]{1,0:T(8,128)(2,1)} %second_ref.1) | copy-start | bytes 1572868
  13.9 26.2 %copy-start = (bf16[512,512]{1,0:T(8,128)(2,1)S(1)}, bf16[512,512]{1,0:T(8,128)(2,1)}, u32[]{:S(2)}) copy-start(bf16[512,512]{1,0:T(8,128)(2,1)} %first_ref.1) | copy-start | bytes 1572868
  41.7 14.8 %all-to-all-start.1 = ((bf16[32,24,128]{2,1,0:T(8,128)(2,1)}), bf16[32,24,128]{2,1,0:T(8,128)(2,1)S(1)}, u32[]{:S(2)}, u32[]{:S(2)}) async-start(bf16[32,24,128]{2,1,0:T(8,128)(2,1)} %shard_map.81), calls=%async_computation.1 | async-start | bytes 393216 | tf_op jit(solution)/shard_map/all_to_all | solution.py:501
  57.2 9.2 %collective-permute-start.2 = (bf16[96,256]{1,0:T(8,128)(2,1)S(1)}, bf16[96,256]{1,0:T(8,128)(2,1)S(1)}, u32[]{:S(2)}, u32[]{:S(2)}) collective-permute-start(bf16[96,256]{1,0:T(8,128)(2,1)S(1)} %get-tuple-element.45), channel_id=1, source_target_pairs={{0,1},{1,2},{2,3},{3,4},{4,5},{5,6},{6,7},{7,8},{8,9},{9,10},{10,1... | collective-permute-start | bytes 147464 | tf_op jit(solution)/shard_map/ppermute | solution.py:497
  59.1 11.2 %collective-permute-start.3 = (bf16[96,256]{1,0:T(8,128)(2,1)S(1)}, bf16[96,256]{1,0:T(8,128)(2,1)S(1)}, u32[]{:S(2)}, u32[]{:S(2)}) collective-permute-start(bf16[96,256]{1,0:T(8,128)(2,1)S(1)} %get-tuple-element.46), channel_id=1, source_target_pairs={{0,15},{1,0},{2,1},{3,2},{4,3},{5,4},{6,5},{7,6},{8,7},{9,8},{10,9... | collective-permute-start | bytes 147464 | tf_op jit(solution)/shard_map/ppermute | solution.py:497

commit v3 on v2

--- a/solution.py
+++ b/solution.py
@@ -39,10 +39,6 @@
         scratch_shapes=list(scratch),
         compiler_params=pltpu.CompilerParams(vmem_limit_bytes=48 * 1024 * 1024),
     )
-
-
-def exact_dot(a, b):
-    return jnp.dot(a, b, precision=lax.Precision.HIGHEST, preferred_element_type=F32)
 
 
 def hi_lo(x):
@@ -212,10 +208,12 @@
     down_ref[0:FIELD_ROWS] = block
 
 
-def home_first(field_ref, bubble_ref, owner_ref, dest_ref, part_ref, seen_ref,
+def home_first(field_ref, bubble_ref, owner_ref, dest_ref, part_ref, seen_ref, put_ref, pick_ref,
                table_ref, row_ref, col_ref, hot_ref, load_ref, sum_ref):
     field = field_ref[...]
     split_table(field, table_ref)
+    put_ref[...] = put_matrix(dest_ref[0:1])
+    pick_ref[...] = pick_matrix(dest_ref[1:2])
     row, col = home_cells(owner_ref[0], dest_ref[0:1])
     row_ref[...] = row
     col_ref[...] = col
@@ -301,7 +299,16 @@
     return col
 
 
-def low_first(field_ref, part_ref, low_ref, out_ref, hot_ref, load_ref):
+def seen_afar(moved_ref, at, far_ref, hot_ref):
+    cells = moved_ref[at : at + 8].astype(jnp.int32)
+    fill_columns(cells[:, 128:256], hot_ref)
+    return gather(far_ref[0:FIELD_ROWS], cells[:, 0:128] - 1, hot_ref)
+
+
+def low_first(field_ref, part_ref, low_ref, moved_ref, out_ref, afar_ref, come_ref, hot_ref, load_ref):
+    fill_columns(tail_cells(tail_of(low_ref), 4)[1], come_ref)
+    for a, line in enumerate(seen_afar(moved_ref, 8, low_ref, hot_ref)):
+        afar_ref[a] = line
     fill_columns(arrived(low_ref, low_ref, FIELD_ROWS, 3, load_ref), hot_ref)
     push = push_of(scatter(load_ref, hot_ref), field_ref[...])
     for a in range(3):
@@ -311,7 +318,27 @@
             out_ref[base : base + 16] = total + below_term(field_ref, plane(low_ref, a, 3)) if z == 0 else total
 
 
-def high_first(field_ref, part_ref, high_ref, tend_ref, send_ref, hot_ref, load_ref):
+def high_first(field_ref, part_ref, high_ref, moved_ref, afar_ref, seen_ref, bubble_ref, put_ref, pick_ref,
+               tend_ref, send_ref, rate_ref, next_ref, slots_ref, come_ref, hot_ref, load_ref):
+    fill_columns(tail_cells(tail_of(high_ref), 4)[1], come_ref)
+    near = seen_afar(moved_ref, 0, high_ref, hot_ref)
+    found = jnp.concatenate([jnp.concatenate([near[a], afar_ref[a]], axis=0) for a in range(3)], axis=1)
+    back = jnp.dot(put_ref[...].astype(BF16), found.astype(BF16), preferred_element_type=F32)
+    after = []
+    for a in range(3):
+        here = bubble_ref[a]
+        rate = (seen_ref[a] + back[:, a * 128 : (a + 1) * 128] - here) / relax_time
+        if a == 1:
+            rate = rate + buoyancy
+        rate_ref[a] = rate
+        after.append(here + C1 * rate)
+        next_ref[a] = after[a]
+    parts = jnp.concatenate([piece for x in after for piece in hi_lo(x)], axis=1).astype(BF16)
+    picked = jnp.dot(pick_ref[...].astype(BF16), parts, preferred_element_type=F32)
+    for at in (0, 8):
+        for a in range(3):
+            line = at * 3 + a * 8
+            slots_ref[line : line + 8] = picked[at : at + 8, a * 256 : (a + 1) * 256]
     fill_columns(arrived(high_ref, high_ref, FIELD_ROWS, 3, load_ref), hot_ref)
     push = push_of(scatter(load_ref, hot_ref), field_ref[...])
     six = [[None] * 4 for _ in range(6)]
@@ -328,55 +355,6 @@
     pack_pair(six, send_ref)
 
 
-def bubbles_first(low_ref, high_ref, moved_ref, seen_ref, bubble_ref, owner_ref, dest_ref,
-                  rate_ref, next_ref, slots_ref, sum_ref, come_ref,
-                  row_ref, col_ref, hot_ref, load_ref, ones_ref):
-    found = [[], [], []]
-    for at, ref in ((0, high_ref), (8, low_ref)):
-        cells = moved_ref[at : at + 8].astype(jnp.int32)
-        fill_columns(cells[:, 128:256], hot_ref)
-        seen = gather(ref[0:FIELD_ROWS], cells[:, 0:128] - 1, hot_ref)
-        for a in range(3):
-            found[a].append(seen[a])
-    found = jnp.concatenate([jnp.concatenate(f, axis=0) for f in found], axis=1)
-    back = exact_dot(put_matrix(dest_ref[0:1]), found)
-    after = []
-    for a in range(3):
-        here = bubble_ref[a]
-        rate = (seen_ref[a] + back[:, a * 128 : (a + 1) * 128] - here) / relax_time
-        if a == 1:
-            rate = rate + buoyancy
-        rate_ref[a] = rate
-        after.append(here + C1 * rate)
-        next_ref[a] = after[a]
-    picked = exact_dot(pick_matrix(dest_ref[1:2]), jnp.concatenate(after, axis=1))
-    for at in (0, 8):
-        for a in range(3):
-            line = at * 3 + a * 8
-            slots_ref[line : line + 8] = jnp.concatenate(
-                hi_lo(picked[at : at + 8, a * 128 : (a + 1) * 128]), axis=1
-            )
-    row, col = home_cells(owner_ref[1], dest_ref[1:2])
-    row_ref[...] = row
-    col_ref[...] = col
-    sum_ref[...] = jnp.zeros_like(sum_ref)
-
-    def step(i, carry):
-        rows = pl.ds(pl.multiple_of(i * 8, 8), 8)
-        fill_columns(col_ref[rows], hot_ref)
-        pairs = [hi_lo(next_ref[a, rows]) for a in range(3)]
-        fill_values(row_ref[rows], [p[0] for p in pairs], [p[1] for p in pairs], load_ref)
-        sum_ref[...] += scatter(load_ref, hot_ref)
-        return carry
-
-    lax.fori_loop(0, 3, step, 0)
-    for i, ref in enumerate((low_ref, high_ref)):
-        row, col = tail_cells(tail_of(ref), 4)
-        fill_columns(col, come_ref.at[i])
-        fill_values(row, (), (), ones_ref)
-        sum_ref[384:448] += scatter(ones_ref, come_ref.at[i])
-
-
 def columns_body(got_ref, first_ref, second_ref, send_ref):
     got = got_ref[...].astype(F32)
     main = got[:, 0:16].reshape(512, 128)
@@ -404,7 +382,7 @@
     send_ref[...] = jnp.concatenate([out, tail], axis=1).astype(BF16)
 
 
-def middle_body(wall_ref, field_ref, part_ref, low_ref, high_ref, slots_ref, come_ref,
+def middle_body(wall_ref, field_ref, part_ref, low_ref, high_ref, slots_ref, come_low_ref, come_high_ref,
                 next_ref, tend_ref, up_ref, down_ref, table_ref):
     for a in range(3):
         for z in range(4):
@@ -413,80 +391,84 @@
             tend_ref[base : base + 16] = total
             next_ref[base : base + 16] = field_ref[base : base + 16] + C1 * total
     split_table(next_ref[...], table_ref)
-    ends = ((low_ref, down_ref, 0, 24), (high_ref, up_ref, 3, 0))
-    for i, (ref, out_ref, z, at) in enumerate(ends):
+    ends = ((low_ref, come_low_ref, down_ref, 0, 24), (high_ref, come_high_ref, up_ref, 3, 0))
+    for ref, come_ref, out_ref, z, at in ends:
         row, _ = tail_cells(tail_of(ref), 4)
-        seen = gather(table_ref[...], row, come_ref.at[i])
+        seen = gather(table_ref[...], row, come_ref)
         lines = [plane(next_ref, a, z) for a in range(3)]
         lines.append(slots_ref[at : at + 24])
         lines += [jnp.concatenate(hi_lo(seen[a]), axis=1) for a in range(3)]
         out_ref[...] = jnp.concatenate(lines, axis=0).astype(BF16)
 
 
-def home_second(wall_ref, field_ref, tend_ref, sum_ref, bubble_ref, rate_ref, owner_ref, dest_ref,
-                base_ref, late_ref, table_ref, row_ref, col_ref, hot_ref):
+def home_second(wall_ref, field_ref, tend_ref, bubble_ref, rate_ref, owner_ref, dest_ref,
+                base_ref, late_ref, put_ref, table_ref, row_ref, col_ref, hot_ref, load_ref, sum_ref):
     field = field_ref[...]
-    push = push_of(sum_ref[...], field)
-    for a in range(3):
-        for z in range(4):
-            base = (a * 4 + z) * 16
-            total = inner_tendency(field_ref, a, z) + push[base : base + 16] + unpack(wall_ref, True, a, z)
-            earlier = tend_ref[base : base + 16]
-            base_ref[base : base + 16] = field_ref[base : base + 16] + (C2 * total + E2 * earlier)
     split_table(field, table_ref)
+    put_ref[...] = put_matrix(dest_ref[1:2])
     row, col = home_cells(owner_ref[1], dest_ref[1:2])
     row_ref[...] = row
     col_ref[...] = col
+    sum_ref[...] = jnp.zeros_like(sum_ref)
 
     def step(i, carry):
         rows = pl.ds(pl.multiple_of(i * 8, 8), 8)
+        row8 = row_ref[rows]
         fill_columns(col_ref[rows], hot_ref)
-        seen = gather(table_ref[...], row_ref[rows], hot_ref)
+        pairs = [hi_lo(bubble_ref[a, rows]) for a in range(3)]
+        fill_values(row8, [p[0] for p in pairs], [p[1] for p in pairs], load_ref)
+        seen = gather(table_ref[...], row8, hot_ref)
         for a in range(3):
             here = bubble_ref[a, rows]
             rate = (seen[a] - here) / relax_time
             if a == 1:
                 rate = rate + buoyancy
             late_ref[a, rows] = here + (C2 * rate + E2 * rate_ref[a, rows])
+        sum_ref[...] += scatter(load_ref, hot_ref)
         return carry
 
     lax.fori_loop(0, 3, step, 0)
-
-
-def late_sum(cells_ref, values_ref, i, come_ref, load_ref):
+    push = push_of(sum_ref[...], field)
+    for a in range(3):
+        for z in range(4):
+            base = (a * 4 + z) * 16
+            total = inner_tendency(field_ref, a, z) + push[base : base + 16] + unpack(wall_ref, True, a, z)
+            earlier = tend_ref[base : base + 16]
+            base_ref[base : base + 16] = field_ref[base : base + 16] + (C2 * total + E2 * earlier)
+
+
+def late_push(cells_ref, values_ref, field_ref, come_ref, load_ref):
     arrived(cells_ref, values_ref, 48, 4, load_ref)
-    sums = scatter(load_ref, come_ref.at[i])
-    return C2 * coupling * (sums[0:192] + sums[192:384])
+    return push_of(scatter(load_ref, come_ref), field_ref[...])
 
 
 def low_second(base_ref, field_ref, low_ref, low2_ref, come_ref, out_ref, load_ref):
-    push = late_sum(low_ref, low2_ref, 0, come_ref, load_ref)
-    for a in range(3):
-        for z in range(4):
-            base = (a * 4 + z) * 16
-            total = base_ref[base : base + 16] + push[base : base + 16]
+    push = late_push(low_ref, low2_ref, field_ref, come_ref, load_ref)
+    for a in range(3):
+        for z in range(4):
+            base = (a * 4 + z) * 16
+            total = base_ref[base : base + 16] + C2 * push[base : base + 16]
             if z == 0:
                 total = total + C2 * below_term(field_ref, low2_ref[a * 16 : a * 16 + 16, :].astype(F32))
             out_ref[base : base + 16] = total
 
 
-def high_second(base_ref, field_ref, high_ref, low2_ref, high2_ref, late_ref, dest_ref, come_ref,
+def high_second(base_ref, field_ref, high_ref, low2_ref, high2_ref, late_ref, put_ref, come_ref,
                 out_ref, bubble_ref, load_ref):
-    found = []
-    from_low, from_high = low2_ref[48:96, :].astype(F32), high2_ref[48:96, :].astype(F32)
-    for a in range(3):
-        line = 24 + a * 8
-        high = from_high[line : line + 8, 0:128] + from_high[line : line + 8, 128:256]
-        low = from_low[line : line + 8, 0:128] + from_low[line : line + 8, 128:256]
-        found.append(jnp.concatenate([high, low], axis=0))
-    back = exact_dot(put_matrix(dest_ref[1:2]), jnp.concatenate(found, axis=1))
-    for a in range(3):
-        bubble_ref[a] = late_ref[a] + (C2 / relax_time) * back[:, a * 128 : (a + 1) * 128]
-    push = late_sum(high_ref, high2_ref, 1, come_ref, load_ref)
-    for a in range(3):
-        for z in range(4):
-            base = (a * 4 + z) * 16
-            total = base_ref[base : base + 16] + push[base : base + 16]
+    returned = jnp.concatenate(
+        [jnp.concatenate([ref[72 + a * 8 : 80 + a * 8, :].astype(F32) for ref in (high2_ref, low2_ref)], axis=0)
+         for a in range(3)],
+        axis=1,
+    )
+    back = jnp.dot(put_ref[...].astype(BF16), returned.astype(BF16), preferred_element_type=F32)
+    for a in range(3):
+        seen = back[:, a * 256 : a * 256 + 128] + back[:, a * 256 + 128 : a * 256 + 256]
+        bubble_ref[a] = late_ref[a] + (C2 / relax_time) * seen
+    push = late_push(high_ref, high2_ref, field_ref, come_ref, load_ref)
+    for a in range(3):
+        for z in range(4):
+            base = (a * 4 + z) * 16
+            total = base_ref[base : base + 16] + C2 * push[base : base + 16]
             if z == 3:
                 total = total + C2 * above_term(field_ref, high2_ref[a * 16 : a * 16 + 16, :].astype(F32))
             out_ref[base : base + 16] = total
@@ -529,31 +511,30 @@
         scratch_shapes=[pltpu.SemaphoreType.DMA((4,))],
     )(velocity_in, bubbles_in, owner_in, dest_in)
     low, high = shifted(up, 1), shifted(down, -1)
-    part, seen = call(
-        home_first, (block, rows), (table, ids, ids, hot, load, pltpu.VMEM((448, 256), F32))
+    part, seen, put, pick = call(
+        home_first, (block, rows, ((24, 16), F32), ((16, 24), F32)), (table, ids, ids, hot, load, pltpu.VMEM((448, 256), F32))
     )(field, bubble_vel, owner, dest)
-    (part,) = call(low_first, (block,), (hot, load))(field, part, low)
-    part, to_columns = call(high_first, (block, packed), (hot, load))(field, part, high)
+    spread_hot = ((256, 1024), BF16)
+    part, afar, come_low = call(low_first, (block, ((3, 8, 128), F32), spread_hot), (hot, load))(
+        field, part, low, moved
+    )
+    part, to_columns, rate, bubbles, slots, come_high = call(
+        high_first, (block, packed, rows, rows, ((48, 256), F32), spread_hot), (hot, load)
+    )(field, part, high, moved, afar, seen, bubble_vel, put, pick)
     columns = exchange(to_columns)
-    rate, bubbles, slots, sums, come = call(
-        bubbles_first,
-        (rows, rows, ((48, 256), F32), ((448, 256), F32), ((2, 256, 1024), BF16)),
-        (ids, ids, hot, load, pltpu.VMEM((64, 1024), BF16)),
-    )(low, high, moved, seen, bubble_vel, owner, dest)
     (walls,) = call(columns_body, (packed,))(columns, first_deriv, second_deriv)
     walls = exchange(walls)
     lasts = ((LAST_ROWS, 256), BF16)
     middle, tend, up, down = call(middle_body, (block, block, lasts, lasts), (table,))(
-        walls, field, part, low, high, slots, come
+        walls, field, part, low, high, slots, come_low, come_high
     )
     low2, high2 = shifted(up, 1), shifted(down, -1)
-    base, late = call(home_second, (block, rows), (table, ids, ids, hot))(
-        walls, middle, tend, sums, bubbles, rate, owner, dest
-    )
-    late_load = pltpu.VMEM((384, 1024), BF16)
-    (base,) = call(low_second, (block,), (late_load,))(base, middle, low, low2, come)
-    field, bubbles = call(high_second, (block, rows), (late_load,))(
-        base, middle, high, low2, high2, late, dest, come
+    base, late, put = call(
+        home_second, (block, rows, ((24, 16), F32)), (table, ids, ids, hot, load, pltpu.VMEM((448, 256), F32))
+    )(walls, middle, tend, bubbles, rate, owner, dest)
+    (base,) = call(low_second, (block,), (load,))(base, middle, low, low2, come_low)
+    field, bubbles = call(high_second, (block, rows), (load,))(
+        base, middle, high, low2, high2, late, put, come_high
     )
     return (field.reshape(velocity.shape), bubbles)
 

time: 71.9 us -> 71.8 us (level)
  the two profiles are of different devices: /device:TPU:54 before, /device:TPU:8 now
where the time goes in v3:
time: 71.8 us; the launch traced here: 71.5 us
  blocking collectives  36.4 us (51%)
  starting transfers between devices  20.5 us (29%)
  Pallas kernels  12.5 us (17%)
  waiting for transfers between devices  1.33 us (2%)
  between operations  0.76 us (1%)
    all_to_all x2, blocking collectives, exchange(): return lax.all_to_all(x, 'px', split_axis=0, concat_axis=0, tiled=True)  36.4 us
    ppermute x4, starting transfers between devices, shifted(): lax.ppermute(x, 'pz', [(i, (i + by) % length) for i in range(length)])  20.5 us
    pallas_call x1, Pallas kernels, on_device(): call(home_second, (block, rows, ((24, 16), F32)), (table, ids, ids, hot,...  3.32 us
    pallas_call x1, Pallas kernels, on_device(): call(home_first, (block, rows, ((24, 16), F32), ((16, 24), F32)), (table,...  2.56 us
  transfers between devices with their start and end apart: 4, of which 1 were waited for; matrix products, arithmetic and copies ran while one was open for 0% of the time, Pallas kernels for 10%

profile of v3, /device:TPU:8, one launch (start us, length us, event | category | flops | bytes accessed | tf_op | source)
XLA Modules:
  0.0 71.5 jit_solution(11186748937852124425)
XLA Ops:
  0.6 1.2 %shard_map.77 = (bf16[240,256]{1,0:T(8,128)(2,1)S(1)}, bf16[240,256]{1,0:T(8,128)(2,1)S(1)}, f32[16,256]{1,0:T(8,128)S(1)}, f32[192,256]{1,0:T(8,128)S(1)}, f32[...) custom-call(f32[192,256]{1,0:T(8,128)} %bitcast.2, f32[3,24,128]{2,1,0:T(8,128)} %bubble_hbm.1, ...), custom_call_target="tpu_custom_call" | custom-call | tf_op jit(solution)/shard_map/pallas_call | solution.py:499
  1.9 4.5 %collective-permute-start = (bf16[240,256]{1,0:T(8,128)(2,1)S(1)}, bf16[240,256]{1,0:T(8,128)(2,1)S(1)}, u32[]{:S(2)}, u32[]{:S(2)}) collective-permute-start(bf16[240,256]{1,0:T(8,128)(2,1)S(1)} %get-tuple-element.36), channel_id=1, source_target_pairs={{0,1},{1,2},{2,3},{3,4},{4,5},{5,6},{6,7},{7,8},{8,9},{9,10},{10,1... | collective-permute-start | bytes 368648 | tf_op jit(solution)/shard_map/ppermute | solution.py:479
  6.4 5.6 %collective-permute-start.1 = (bf16[240,256]{1,0:T(8,128)(2,1)S(1)}, bf16[240,256]{1,0:T(8,128)(2,1)S(1)}, u32[]{:S(2)}, u32[]{:S(2)}) collective-permute-start(bf16[240,256]{1,0:T(8,128)(2,1)S(1)} %get-tuple-element.39), channel_id=1, source_target_pairs={{0,15},{1,0},{2,1},{3,2},{4,3},{5,4},{6,5},{7,6},{8,7},{9,8},{10,9... | collective-permute-start | bytes 368648 | tf_op jit(solution)/shard_map/ppermute | solution.py:479
  11.9 2.6 %shard_map.78 = (f32[192,256]{1,0:T(8,128)S(1)}, f32[3,24,128]{2,1,0:T(8,128)S(1)}, f32[24,16]{1,0:T(8,128)S(1)}, f32[16,24]{1,0:T(8,128)S(1)}) custom-call(f32[192,256]{1,0:T(8,128)S(1)} %get-tuple-element.31.field_ref, f32[3,24,128]{2,1,0:T(8,128)S(1)} %get-tuple-element.32.bubble_ref, s32[2,24,128]{2,1,0:T(8,128)S(1)} %get-tuple-element.33.owner_ref, ...), custom_call_target="tpu_custom_call" | custom-call | tf_op jit(solution)/shard_map/pallas_call | solution.py:514
  14.5 0.0 collective-permute-done.low_ref
  14.5 0.0 copy-start.1
  14.5 0.9 %shard_map.79 = (f32[192,256]{1,0:T(8,128)S(1)}, f32[3,8,128]{2,1,0:T(8,128)S(1)}, bf16[256,1024]{1,0:T(8,128)(2,1)S(1)}) custom-call(f32[192,256]{1,0:T(8,128)S(1)} %get-tuple-element.31.field_ref, f32[192,256]{1,0:T(8,128)S(1)} %get-tuple-element.35.part_ref, bf16[240,256]{1,0:T(8,128)(2,1)S(1)} %collective-permute-done.low_ref, ...), custom_call_target="tpu_custom_call" | custom-call | tf_op jit(solution)/shard_map/pallas_call | solution.py:518
  15.4 0.0 copy-start
  15.4 1.3 %collective-permute-done.1.high_ref = bf16[240,256]{1,0:T(8,128)(2,1)S(1)} collective-permute-done((bf16[240,256]{1,0:T(8,128)(2,1)S(1)}, bf16[240,256]{1,0:T(8,128)(2,1)S(1)}, u32[]{:S(2)}, u32[]{:S(2)}) %collective-permute-start.1) | collective-permute-done | bytes 122912 | tf_op jit(solution)/shard_map/ppermute | solution.py:479
  16.7 1.3 %shard_map.80 = (f32[192,256]{1,0:T(8,128)S(1)}, bf16[32,24,128]{2,1,0:T(8,128)(2,1)S(1)}, f32[3,24,128]{2,1,0:T(8,128)S(1)}, f32[3,24,128]{2,1,0:T(8,128)S(1)},...) custom-call(f32[192,256]{1,0:T(8,128)S(1)} %get-tuple-element.31.field_ref, ...), custom_call_target="tpu_custom_call" | custom-call | tf_op jit(solution)/shard_map/pallas_call | solution.py:521
  18.0 22.4 %all_to_all.10.got_ref = bf16[32,24,128]{2,1,0:T(8,128)(2,1)S(1)} all-to-all(bf16[32,24,128]{2,1,0:T(8,128)(2,1)S(1)} %get-tuple-element.44), channel_id=1, replica_groups=mesh['px'=32,'pz'=16] {'px'}, dimensions={0} | all-to-all | bytes 393216 | tf_op jit(solution)/shard_map/all_to_all | solution.py:483
  40.5 0.0 copy-done.1
  40.5 0.0 copy-done
  40.5 0.9 %shard_map.81 = bf16[32,24,128]{2,1,0:T(8,128)(2,1)S(1)} custom-call(bf16[32,24,128]{2,1,0:T(8,128)(2,1)S(1)} %all_to_all.10.got_ref, bf16[512,512]{1,0:T(8,128)(2,1)S(1)} %copy-done, bf16[512,512]{1,0:T(8,128)(2,1)S(1)} %copy-done.1), custom_call_target="tpu_custom_call" | custom-call | tf_op jit(solution)/shard_map/pallas_call | solution.py:525
  41.4 13.9 %all_to_all.11.wall_ref = bf16[32,24,128]{2,1,0:T(8,128)(2,1)S(1)} all-to-all(bf16[32,24,128]{2,1,0:T(8,128)(2,1)S(1)} %shard_map.81), channel_id=1, replica_groups=mesh['px'=32,'pz'=16] {'px'}, dimensions={0} | all-to-all | bytes 393216 | tf_op jit(solution)/shard_map/all_to_all | solution.py:483
  55.3 0.7 shard_map.82
  56.0 5.6 %collective-permute-start.2 = (bf16[96,256]{1,0:T(8,128)(2,1)S(1)}, bf16[96,256]{1,0:T(8,128)(2,1)S(1)}, u32[]{:S(2)}, u32[]{:S(2)}) collective-permute-start(bf16[96,256]{1,0:T(8,128)(2,1)S(1)} %get-tuple-element.54), channel_id=1, source_target_pairs={{0,1},{1,2},{2,3},{3,4},{4,5},{5,6},{6,7},{7,8},{8,9},{9,10},{10,1... | collective-permute-start | bytes 147464 | tf_op jit(solution)/shard_map/ppermute | solution.py:479
  61.7 4.8 %collective-permute-start.3 = (bf16[96,256]{1,0:T(8,128)(2,1)S(1)}, bf16[96,256]{1,0:T(8,128)(2,1)S(1)}, u32[]{:S(2)}, u32[]{:S(2)}) collective-permute-start(bf16[96,256]{1,0:T(8,128)(2,1)S(1)} %get-tuple-element.55), channel_id=1, source_target_pairs={{0,15},{1,0},{2,1},{3,2},{4,3},{5,4},{6,5},{7,6},{8,7},{9,8},{10,9... | collective-permute-start | bytes 147464 | tf_op jit(solution)/shard_map/ppermute | solution.py:479
  66.4 3.3 %shard_map.83 = (f32[192,256]{1,0:T(8,128)S(1)}, f32[3,24,128]{2,1,0:T(8,128)S(1)}, f32[24,16]{1,0:T(8,128)S(1)}) custom-call(bf16[32,24,128]{2,1,0:T(8,128)(2,1)S(1)} %all_to_all.11.wall_ref, f32[192,256]{1,0:T(8,128)S(1)} %get-tuple-element.49.field_ref, f32[192,256]{1,0:T(8,128)S(1)} %get-tuple-element.50.tend_ref, ...), custom_call_target="tpu_custom_call" | custom-call | tf_op jit(solution)/shard_map/pallas_call | solution.py:532
  69.8 0.0 collective-permute-done.2.low2_ref
  69.8 0.5 shard_map.84.base_ref
  70.3 0.0 collective-permute-done.3.high2_ref
  70.3 1.2 %shard_map.85 = (f32[192,256]{1,0:T(8,128)}, f32[3,24,128]{2,1,0:T(8,128)}) custom-call(f32[192,256]{1,0:T(8,128)S(1)} %shard_map.84.base_ref, f32[192,256]{1,0:T(8,128)S(1)} %get-tuple-element.49.field_ref, bf16[240,256]{1,0:T(8,128)(2,1)S(1)} %collective-permute-done.1.high_ref, bf16[96,256]{1,0:T(8,128)(2,1)S(1)} %collective-permute-done.2.low2_ref, ...), custom_call_target="tpu_custom_call" | custom-call | tf_op jit(solution)/shard_map/pallas_call | solution.py:536
Async XLA Ops:
  1.9 12.6 %collective-permute-start = (bf16[240,256]{1,0:T(8,128)(2,1)S(1)}, bf16[240,256]{1,0:T(8,128)(2,1)S(1)}, u32[]{:S(2)}, u32[]{:S(2)}) collective-permute-start(bf16[240,256]{1,0:T(8,128)(2,1)S(1)} %get-tuple-element.36), channel_id=1, source_target_pairs={{0,1},{1,2},{2,3},{3,4},{4,5},{5,6},{6,7},{7,8},{8,9},{9,10},{10,1... | collective-permute-start | bytes 368648 | tf_op jit(solution)/shard_map/ppermute | solution.py:479
  6.4 10.4 %collective-permute-start.1 = (bf16[240,256]{1,0:T(8,128)(2,1)S(1)}, bf16[240,256]{1,0:T(8,128)(2,1)S(1)}, u32[]{:S(2)}, u32[]{:S(2)}) collective-permute-start(bf16[240,256]{1,0:T(8,128)(2,1)S(1)} %get-tuple-element.39), channel_id=1, source_target_pairs={{0,15},{1,0},{2,1},{3,2},{4,3},{5,4},{6,5},{7,6},{8,7},{9,8},{10,9... | collective-permute-start | bytes 368648 | tf_op jit(solution)/shard_map/ppermute | solution.py:479
  14.5 26.0 %copy-start.1 = (bf16[512,512]{1,0:T(8,128)(2,1)S(1)}, bf16[512,512]{1,0:T(8,128)(2,1)}, u32[]{:S(2)}) copy-start(bf16[512,512]{1,0:T(8,128)(2,1)} %second_ref.1) | copy-start | bytes 1572868
  15.4 25.1 %copy-start = (bf16[512,512]{1,0:T(8,128)(2,1)S(1)}, bf16[512,512]{1,0:T(8,128)(2,1)}, u32[]{:S(2)}) copy-start(bf16[512,512]{1,0:T(8,128)(2,1)} %first_ref.1) | copy-start | bytes 1572868
  56.0 13.8 %collective-permute-start.2 = (bf16[96,256]{1,0:T(8,128)(2,1)S(1)}, bf16[96,256]{1,0:T(8,128)(2,1)S(1)}, u32[]{:S(2)}, u32[]{:S(2)}) collective-permute-start(bf16[96,256]{1,0:T(8,128)(2,1)S(1)} %get-tuple-element.54), channel_id=1, source_target_pairs={{0,1},{1,2},{2,3},{3,4},{4,5},{5,6},{6,7},{7,8},{8,9},{9,10},{10,1... | collective-permute-start | bytes 147464 | tf_op jit(solution)/shard_map/ppermute | solution.py:479
  61.7 8.6 %collective-permute-start.3 = (bf16[96,256]{1,0:T(8,128)(2,1)S(1)}, bf16[96,256]{1,0:T(8,128)(2,1)S(1)}, u32[]{:S(2)}, u32[]{:S(2)}) collective-permute-start(bf16[96,256]{1,0:T(8,128)(2,1)S(1)} %get-tuple-element.55), channel_id=1, source_target_pairs={{0,15},{1,0},{2,1},{3,2},{4,3},{5,4},{6,5},{7,6},{8,7},{9,8},{10,9... | collective-permute-start | bytes 147464 | tf_op jit(solution)/shard_map/ppermute | solution.py:479

commit v4 on v3

--- a/solution.py
+++ b/solution.py
@@ -209,30 +209,24 @@
 
 
 def home_first(field_ref, bubble_ref, owner_ref, dest_ref, part_ref, seen_ref, put_ref, pick_ref,
-               table_ref, row_ref, col_ref, hot_ref, load_ref, sum_ref):
+               table_ref, hot_ref, load_ref):
     field = field_ref[...]
     split_table(field, table_ref)
     put_ref[...] = put_matrix(dest_ref[0:1])
     pick_ref[...] = pick_matrix(dest_ref[1:2])
     row, col = home_cells(owner_ref[0], dest_ref[0:1])
-    row_ref[...] = row
-    col_ref[...] = col
-    sum_ref[...] = jnp.zeros_like(sum_ref)
-
-    def step(i, carry):
-        rows = pl.ds(pl.multiple_of(i * 8, 8), 8)
-        row8, col8 = row_ref[rows], col_ref[rows]
-        fill_columns(col8, hot_ref)
+    sums = None
+    for i in range(3):
+        rows = slice(i * 8, i * 8 + 8)
+        fill_columns(col[rows], hot_ref.at[i])
         pairs = [hi_lo(bubble_ref[a, rows]) for a in range(3)]
-        fill_values(row8, [p[0] for p in pairs], [p[1] for p in pairs], load_ref)
-        seen = gather(table_ref[...], row8, hot_ref)
+        fill_values(row[rows], [p[0] for p in pairs], [p[1] for p in pairs], load_ref.at[i])
+        got = scatter(load_ref.at[i], hot_ref.at[i])
+        sums = got if sums is None else sums + got
+        seen = gather(table_ref[...], row[rows], hot_ref.at[i])
         for a in range(3):
             seen_ref[a, rows] = seen[a]
-        sum_ref[...] += scatter(load_ref, hot_ref)
-        return carry
-
-    lax.fori_loop(0, 3, step, 0)
-    push = push_of(sum_ref[...], field)
+    push = push_of(sums, field)
     for a in range(3):
         for z in range(4):
             base = (a * 4 + z) * 16
@@ -305,9 +299,9 @@
     return gather(far_ref[0:FIELD_ROWS], cells[:, 0:128] - 1, hot_ref)
 
 
-def low_first(field_ref, part_ref, low_ref, moved_ref, out_ref, afar_ref, come_ref, hot_ref, load_ref):
+def low_first(field_ref, part_ref, low_ref, moved_ref, out_ref, afar_ref, come_ref, hot_ref, far_ref, load_ref):
     fill_columns(tail_cells(tail_of(low_ref), 4)[1], come_ref)
-    for a, line in enumerate(seen_afar(moved_ref, 8, low_ref, hot_ref)):
+    for a, line in enumerate(seen_afar(moved_ref, 8, low_ref, far_ref)):
         afar_ref[a] = line
     fill_columns(arrived(low_ref, low_ref, FIELD_ROWS, 3, load_ref), hot_ref)
     push = push_of(scatter(load_ref, hot_ref), field_ref[...])
@@ -319,9 +313,11 @@
 
 
 def high_first(field_ref, part_ref, high_ref, moved_ref, afar_ref, seen_ref, bubble_ref, put_ref, pick_ref,
-               tend_ref, send_ref, rate_ref, next_ref, slots_ref, come_ref, hot_ref, load_ref):
+               tend_ref, send_ref, rate_ref, next_ref, slots_ref, come_ref, hot_ref, far_ref, load_ref):
+    fill_columns(arrived(high_ref, high_ref, FIELD_ROWS, 3, load_ref), hot_ref)
+    sums = scatter(load_ref, hot_ref)
     fill_columns(tail_cells(tail_of(high_ref), 4)[1], come_ref)
-    near = seen_afar(moved_ref, 0, high_ref, hot_ref)
+    near = seen_afar(moved_ref, 0, high_ref, far_ref)
     found = jnp.concatenate([jnp.concatenate([near[a], afar_ref[a]], axis=0) for a in range(3)], axis=1)
     back = jnp.dot(put_ref[...].astype(BF16), found.astype(BF16), preferred_element_type=F32)
     after = []
@@ -339,8 +335,7 @@
         for a in range(3):
             line = at * 3 + a * 8
             slots_ref[line : line + 8] = picked[at : at + 8, a * 256 : (a + 1) * 256]
-    fill_columns(arrived(high_ref, high_ref, FIELD_ROWS, 3, load_ref), hot_ref)
-    push = push_of(scatter(load_ref, hot_ref), field_ref[...])
+    push = push_of(sums, field_ref[...])
     six = [[None] * 4 for _ in range(6)]
     for a in range(3):
         for z in range(4):
@@ -402,33 +397,29 @@
 
 
 def home_second(wall_ref, field_ref, tend_ref, bubble_ref, rate_ref, owner_ref, dest_ref,
-                base_ref, late_ref, put_ref, table_ref, row_ref, col_ref, hot_ref, load_ref, sum_ref):
+                base_ref, late_ref, put_ref, table_ref, hot_ref, load_ref):
     field = field_ref[...]
     split_table(field, table_ref)
     put_ref[...] = put_matrix(dest_ref[1:2])
     row, col = home_cells(owner_ref[1], dest_ref[1:2])
-    row_ref[...] = row
-    col_ref[...] = col
-    sum_ref[...] = jnp.zeros_like(sum_ref)
-
-    def step(i, carry):
-        rows = pl.ds(pl.multiple_of(i * 8, 8), 8)
-        row8 = row_ref[rows]
-        fill_columns(col_ref[rows], hot_ref)
+
+    sums = None
+    for i in range(3):
+        rows = slice(i * 8, i * 8 + 8)
+        hot, load = hot_ref.at[i], load_ref.at[i]
+        fill_columns(col[rows], hot)
         pairs = [hi_lo(bubble_ref[a, rows]) for a in range(3)]
-        fill_values(row8, [p[0] for p in pairs], [p[1] for p in pairs], load_ref)
-        seen = gather(table_ref[...], row8, hot_ref)
+        fill_values(row[rows], [p[0] for p in pairs], [p[1] for p in pairs], load)
+        got = scatter(load_ref.at[i], hot_ref.at[i])
+        sums = got if sums is None else sums + got
+        seen = gather(table_ref[...], row[rows], hot_ref.at[i])
         for a in range(3):
             here = bubble_ref[a, rows]
             rate = (seen[a] - here) / relax_time
             if a == 1:
                 rate = rate + buoyancy
             late_ref[a, rows] = here + (C2 * rate + E2 * rate_ref[a, rows])
-        sum_ref[...] += scatter(load_ref, hot_ref)
-        return carry
-
-    lax.fori_loop(0, 3, step, 0)
-    push = push_of(sum_ref[...], field)
+    push = push_of(sums, field)
     for a in range(3):
         for z in range(4):
             base = (a * 4 + z) * 16
@@ -490,7 +481,7 @@
     hot = pltpu.VMEM((256, 1024), BF16)
     load = pltpu.VMEM((448, 1024), BF16)
     table = pltpu.VMEM((384, 256), BF16)
-    ids = pltpu.VMEM((24, 128), jnp.int32)
+    hots, loads = pltpu.VMEM((3, 256, 1024), BF16), pltpu.VMEM((3, 448, 1024), BF16)
     packed = ((32, 24, 128), BF16)
 
     velocity_in, bubbles_in, owner_in, dest_in = (
@@ -512,14 +503,14 @@
     )(velocity_in, bubbles_in, owner_in, dest_in)
     low, high = shifted(up, 1), shifted(down, -1)
     part, seen, put, pick = call(
-        home_first, (block, rows, ((24, 16), F32), ((16, 24), F32)), (table, ids, ids, hot, load, pltpu.VMEM((448, 256), F32))
+        home_first, (block, rows, ((24, 16), F32), ((16, 24), F32)), (table, hots, loads)
     )(field, bubble_vel, owner, dest)
     spread_hot = ((256, 1024), BF16)
-    part, afar, come_low = call(low_first, (block, ((3, 8, 128), F32), spread_hot), (hot, load))(
+    part, afar, come_low = call(low_first, (block, ((3, 8, 128), F32), spread_hot), (hot, hot, load))(
         field, part, low, moved
     )
     part, to_columns, rate, bubbles, slots, come_high = call(
-        high_first, (block, packed, rows, rows, ((48, 256), F32), spread_hot), (hot, load)
+        high_first, (block, packed, rows, rows, ((48, 256), F32), spread_hot), (hot, hot, load)
     )(field, part, high, moved, afar, seen, bubble_vel, put, pick)
     columns = exchange(to_columns)
     (walls,) = call(columns_body, (packed,))(columns, first_deriv, second_deriv)
@@ -530,7 +521,7 @@
     )
     low2, high2 = shifted(up, 1), shifted(down, -1)
     base, late, put = call(
-        home_second, (block, rows, ((24, 16), F32)), (table, ids, ids, hot, load, pltpu.VMEM((448, 256), F32))
+        home_second, (block, rows, ((24, 16), F32)), (table, hots, loads)
     )(walls, middle, tend, bubbles, rate, owner, dest)
     (base,) = call(low_second, (block,), (load,))(base, middle, low, low2, come_low)
     field, bubbles = call(high_second, (block, rows), (load,))(

time: 71.8 us -> 70.5 us (0.982)
  the two profiles are of different devices: /device:TPU:8 before, /device:TPU:54 now
where the time goes in v4:
time: 70.5 us; the launch traced here: 70.2 us
  blocking collectives  33.4 us (47%)
  starting transfers between devices  15.7 us (22%)
  waiting for transfers between devices  10.4 us (15%)
  Pallas kernels  9.93 us (14%)
  between operations  0.74 us (1%)
    all_to_all x2, blocking collectives, exchange(): return lax.all_to_all(x, 'px', split_axis=0, concat_axis=0, tiled=True)  33.4 us
    ppermute x4, starting transfers between devices, shifted(): lax.ppermute(x, 'pz', [(i, (i + by) % length) for i in range(length)])  15.7 us
    ppermute x4, waiting for transfers between devices, shifted(): lax.ppermute(x, 'pz', [(i, (i + by) % length) for i in range(length)])  10.4 us
    pallas_call x1, Pallas kernels, on_device(): call(home_second, (block, rows, ((24, 16), F32)), (table, hots, loads))  1.86 us
    pallas_call x1, Pallas kernels, on_device(): call(home_first, (block, rows, ((24, 16), F32), ((16, 24), F32)), (table,...  1.74 us
  transfers between devices with their start and end apart: 4, of which 2 were waited for; matrix products, arithmetic and copies ran while one was open for 0% of the time, Pallas kernels for 7%

profile of v4, /device:TPU:54, one launch (start us, length us, event | category | flops | bytes accessed | tf_op | source)
XLA Modules:
  0.0 70.2 jit_solution(6873850100070197816)
XLA Ops:
  0.6 1.2 %shard_map.77 = (bf16[240,256]{1,0:T(8,128)(2,1)S(1)}, bf16[240,256]{1,0:T(8,128)(2,1)S(1)}, f32[16,256]{1,0:T(8,128)S(1)}, f32[192,256]{1,0:T(8,128)S(1)}, f32[...) custom-call(f32[192,256]{1,0:T(8,128)} %bitcast.2, f32[3,24,128]{2,1,0:T(8,128)} %bubble_hbm.1, ...), custom_call_target="tpu_custom_call" | custom-call | tf_op jit(solution)/shard_map/pallas_call | solution.py:490
  1.9 7.1 %collective-permute-start = (bf16[240,256]{1,0:T(8,128)(2,1)S(1)}, bf16[240,256]{1,0:T(8,128)(2,1)S(1)}, u32[]{:S(2)}, u32[]{:S(2)}) collective-permute-start(bf16[240,256]{1,0:T(8,128)(2,1)S(1)} %get-tuple-element.36), channel_id=1, source_target_pairs={{0,1},{1,2},{2,3},{3,4},{4,5},{5,6},{6,7},{7,8},{8,9},{9,10},{10,1... | collective-permute-start | bytes 368648 | tf_op jit(solution)/shard_map/ppermute | solution.py:470
  8.9 1.9 %collective-permute-start.1 = (bf16[240,256]{1,0:T(8,128)(2,1)S(1)}, bf16[240,256]{1,0:T(8,128)(2,1)S(1)}, u32[]{:S(2)}, u32[]{:S(2)}) collective-permute-start(bf16[240,256]{1,0:T(8,128)(2,1)S(1)} %get-tuple-element.39), channel_id=1, source_target_pairs={{0,15},{1,0},{2,1},{3,2},{4,3},{5,4},{6,5},{7,6},{8,7},{9,8},{10,9... | collective-permute-start | bytes 368648 | tf_op jit(solution)/shard_map/ppermute | solution.py:470
  10.9 1.7 %shard_map.78 = (f32[192,256]{1,0:T(8,128)S(1)}, f32[3,24,128]{2,1,0:T(8,128)S(1)}, f32[24,16]{1,0:T(8,128)S(1)}, f32[16,24]{1,0:T(8,128)S(1)}) custom-call(f32[192,256]{1,0:T(8,128)S(1)} %get-tuple-element.31.field_ref, f32[3,24,128]{2,1,0:T(8,128)S(1)} %get-tuple-element.32.bubble_ref, s32[2,24,128]{2,1,0:T(8,128)S(1)} %get-tuple-element.33.owner_ref, ...), custom_call_target="tpu_custom_call" | custom-call | tf_op jit(solution)/shard_map/pallas_call | solution.py:505
  12.6 0.0 collective-permute-done.low_ref
  12.6 0.0 copy-start.1
  12.6 0.9 %shard_map.79 = (f32[192,256]{1,0:T(8,128)S(1)}, f32[3,8,128]{2,1,0:T(8,128)S(1)}, bf16[256,1024]{1,0:T(8,128)(2,1)S(1)}) custom-call(f32[192,256]{1,0:T(8,128)S(1)} %get-tuple-element.31.field_ref, f32[192,256]{1,0:T(8,128)S(1)} %get-tuple-element.35.part_ref, bf16[240,256]{1,0:T(8,128)(2,1)S(1)} %collective-permute-done.low_ref, ...), custom_call_target="tpu_custom_call" | custom-call | tf_op jit(solution)/shard_map/pallas_call | solution.py:509
  13.5 0.0 copy-start
  13.5 6.4 %collective-permute-done.1.high_ref = bf16[240,256]{1,0:T(8,128)(2,1)S(1)} collective-permute-done((bf16[240,256]{1,0:T(8,128)(2,1)S(1)}, bf16[240,256]{1,0:T(8,128)(2,1)S(1)}, u32[]{:S(2)}, u32[]{:S(2)}) %collective-permute-start.1) | collective-permute-done | bytes 122912 | tf_op jit(solution)/shard_map/ppermute | solution.py:470
  19.9 1.0 %shard_map.80 = (f32[192,256]{1,0:T(8,128)S(1)}, bf16[32,24,128]{2,1,0:T(8,128)(2,1)S(1)}, f32[3,24,128]{2,1,0:T(8,128)S(1)}, f32[3,24,128]{2,1,0:T(8,128)S(1)},...) custom-call(f32[192,256]{1,0:T(8,128)S(1)} %get-tuple-element.31.field_ref, ...), custom_call_target="tpu_custom_call" | custom-call | tf_op jit(solution)/shard_map/pallas_call | solution.py:512
  20.9 19.5 %all_to_all.10.got_ref = bf16[32,24,128]{2,1,0:T(8,128)(2,1)S(1)} all-to-all(bf16[32,24,128]{2,1,0:T(8,128)(2,1)S(1)} %get-tuple-element.44), channel_id=1, replica_groups=mesh['px'=32,'pz'=16] {'px'}, dimensions={0} | all-to-all | bytes 393216 | tf_op jit(solution)/shard_map/all_to_all | solution.py:474
  40.4 0.0 copy-done.1
  40.4 0.0 copy-done
  40.4 0.9 %shard_map.81 = bf16[32,24,128]{2,1,0:T(8,128)(2,1)S(1)} custom-call(bf16[32,24,128]{2,1,0:T(8,128)(2,1)S(1)} %all_to_all.10.got_ref, bf16[512,512]{1,0:T(8,128)(2,1)S(1)} %copy-done, bf16[512,512]{1,0:T(8,128)(2,1)S(1)} %copy-done.1), custom_call_target="tpu_custom_call" | custom-call | tf_op jit(solution)/shard_map/pallas_call | solution.py:516
  41.3 13.9 %all_to_all.11.wall_ref = bf16[32,24,128]{2,1,0:T(8,128)(2,1)S(1)} all-to-all(bf16[32,24,128]{2,1,0:T(8,128)(2,1)S(1)} %shard_map.81), channel_id=1, replica_groups=mesh['px'=32,'pz'=16] {'px'}, dimensions={0} | all-to-all | bytes 393216 | tf_op jit(solution)/shard_map/all_to_all | solution.py:474
  55.2 0.7 shard_map.82
  55.9 1.9 %collective-permute-start.2 = (bf16[96,256]{1,0:T(8,128)(2,1)S(1)}, bf16[96,256]{1,0:T(8,128)(2,1)S(1)}, u32[]{:S(2)}, u32[]{:S(2)}) collective-permute-start(bf16[96,256]{1,0:T(8,128)(2,1)S(1)} %get-tuple-element.54), channel_id=1, source_target_pairs={{0,1},{1,2},{2,3},{3,4},{4,5},{5,6},{6,7},{7,8},{8,9},{9,10},{10,1... | collective-permute-start | bytes 147464 | tf_op jit(solution)/shard_map/ppermute | solution.py:470
  57.8 4.8 %collective-permute-start.3 = (bf16[96,256]{1,0:T(8,128)(2,1)S(1)}, bf16[96,256]{1,0:T(8,128)(2,1)S(1)}, u32[]{:S(2)}, u32[]{:S(2)}) collective-permute-start(bf16[96,256]{1,0:T(8,128)(2,1)S(1)} %get-tuple-element.55), channel_id=1, source_target_pairs={{0,15},{1,0},{2,1},{3,2},{4,3},{5,4},{6,5},{7,6},{8,7},{9,8},{10,9... | collective-permute-start | bytes 147464 | tf_op jit(solution)/shard_map/ppermute | solution.py:470
  62.7 1.9 %shard_map.83 = (f32[192,256]{1,0:T(8,128)S(1)}, f32[3,24,128]{2,1,0:T(8,128)S(1)}, f32[24,16]{1,0:T(8,128)S(1)}) custom-call(bf16[32,24,128]{2,1,0:T(8,128)(2,1)S(1)} %all_to_all.11.wall_ref, f32[192,256]{1,0:T(8,128)S(1)} %get-tuple-element.49.field_ref, f32[192,256]{1,0:T(8,128)S(1)} %get-tuple-element.50.tend_ref, ...), custom_call_target="tpu_custom_call" | custom-call | tf_op jit(solution)/shard_map/pallas_call | solution.py:523
  64.5 0.0 collective-permute-done.2.low2_ref
  64.6 0.5 shard_map.84.base_ref
  65.1 4.0 %collective-permute-done.3.high2_ref = bf16[96,256]{1,0:T(8,128)(2,1)S(1)} collective-permute-done((bf16[96,256]{1,0:T(8,128)(2,1)S(1)}, bf16[96,256]{1,0:T(8,128)(2,1)S(1)}, u32[]{:S(2)}, u32[]{:S(2)}) %collective-permute-start.3) | collective-permute-done | bytes 49184 | tf_op jit(solution)/shard_map/ppermute | solution.py:470
  69.1 1.2 %shard_map.85 = (f32[192,256]{1,0:T(8,128)}, f32[3,24,128]{2,1,0:T(8,128)}) custom-call(f32[192,256]{1,0:T(8,128)S(1)} %shard_map.84.base_ref, f32[192,256]{1,0:T(8,128)S(1)} %get-tuple-element.49.field_ref, bf16[240,256]{1,0:T(8,128)(2,1)S(1)} %collective-permute-done.1.high_ref, bf16[96,256]{1,0:T(8,128)(2,1)S(1)} %collective-permute-done.2.low2_ref, ...), custom_call_target="tpu_custom_call" | custom-call | tf_op jit(solution)/shard_map/pallas_call | solution.py:527
Async XLA Ops:
  1.9 10.8 %collective-permute-start = (bf16[240,256]{1,0:T(8,128)(2,1)S(1)}, bf16[240,256]{1,0:T(8,128)(2,1)S(1)}, u32[]{:S(2)}, u32[]{:S(2)}) collective-permute-start(bf16[240,256]{1,0:T(8,128)(2,1)S(1)} %get-tuple-element.36), channel_id=1, source_target_pairs={{0,1},{1,2},{2,3},{3,4},{4,5},{5,6},{6,7},{7,8},{8,9},{9,10},{10,1... | collective-permute-start | bytes 368648 | tf_op jit(solution)/shard_map/ppermute | solution.py:470
  8.9 11.0 %collective-permute-start.1 = (bf16[240,256]{1,0:T(8,128)(2,1)S(1)}, bf16[240,256]{1,0:T(8,128)(2,1)S(1)}, u32[]{:S(2)}, u32[]{:S(2)}) collective-permute-start(bf16[240,256]{1,0:T(8,128)(2,1)S(1)} %get-tuple-element.39), channel_id=1, source_target_pairs={{0,15},{1,0},{2,1},{3,2},{4,3},{5,4},{6,5},{7,6},{8,7},{9,8},{10,9... | collective-permute-start | bytes 368648 | tf_op jit(solution)/shard_map/ppermute | solution.py:470
  12.6 27.8 %copy-start.1 = (bf16[512,512]{1,0:T(8,128)(2,1)S(1)}, bf16[512,512]{1,0:T(8,128)(2,1)}, u32[]{:S(2)}) copy-start(bf16[512,512]{1,0:T(8,128)(2,1)} %second_ref.1) | copy-start | bytes 1572868
  13.5 26.9 %copy-start = (bf16[512,512]{1,0:T(8,128)(2,1)S(1)}, bf16[512,512]{1,0:T(8,128)(2,1)}, u32[]{:S(2)}) copy-start(bf16[512,512]{1,0:T(8,128)(2,1)} %first_ref.1) | copy-start | bytes 1572868
  55.9 8.6 %collective-permute-start.2 = (bf16[96,256]{1,0:T(8,128)(2,1)S(1)}, bf16[96,256]{1,0:T(8,128)(2,1)S(1)}, u32[]{:S(2)}, u32[]{:S(2)}) collective-permute-start(bf16[96,256]{1,0:T(8,128)(2,1)S(1)} %get-tuple-element.54), channel_id=1, source_target_pairs={{0,1},{1,2},{2,3},{3,4},{4,5},{5,6},{6,7},{7,8},{8,9},{9,10},{10,1... | collective-permute-start | bytes 147464 | tf_op jit(solution)/shard_map/ppermute | solution.py:470
  57.8 11.2 %collective-permute-start.3 = (bf16[96,256]{1,0:T(8,128)(2,1)S(1)}, bf16[96,256]{1,0:T(8,128)(2,1)S(1)}, u32[]{:S(2)}, u32[]{:S(2)}) collective-permute-start(bf16[96,256]{1,0:T(8,128)(2,1)S(1)} %get-tuple-element.55), channel_id=1, source_target_pairs={{0,15},{1,0},{2,1},{3,2},{4,3},{5,4},{6,5},{7,6},{8,7},{9,8},{10,9... | collective-permute-start | bytes 147464 | tf_op jit(solution)/shard_map/ppermute | solution.py:470

commit v5 on v4

--- a/solution.py
+++ b/solution.py
@@ -378,22 +378,32 @@
 
 
 def middle_body(wall_ref, field_ref, part_ref, low_ref, high_ref, slots_ref, come_low_ref, come_high_ref,
-                next_ref, tend_ref, up_ref, down_ref, table_ref):
+                next_ref, tend_ref, first_ref, second_ref, table_ref):
     for a in range(3):
         for z in range(4):
             base = (a * 4 + z) * 16
             total = part_ref[base : base + 16] + unpack(wall_ref, False, a, z)
             tend_ref[base : base + 16] = total
             next_ref[base : base + 16] = field_ref[base : base + 16] + C1 * total
-    split_table(next_ref[...], table_ref)
-    ends = ((low_ref, come_low_ref, down_ref, 0, 24), (high_ref, come_high_ref, up_ref, 3, 0))
-    for ref, come_ref, out_ref, z, at in ends:
+    table_ref[...] = next_ref[...].astype(BF16)
+    sends = []
+    for ref, come_ref, z, at in ((low_ref, come_low_ref, 0, 24), (high_ref, come_high_ref, 3, 0)):
         row, _ = tail_cells(tail_of(ref), 4)
         seen = gather(table_ref[...], row, come_ref)
         lines = [plane(next_ref, a, z) for a in range(3)]
         lines.append(slots_ref[at : at + 24])
-        lines += [jnp.concatenate(hi_lo(seen[a]), axis=1) for a in range(3)]
-        out_ref[...] = jnp.concatenate(lines, axis=0).astype(BF16)
+        lines += [jnp.concatenate(seen[0:2], axis=1), jnp.concatenate([seen[2], jnp.zeros((8, 128), F32)], axis=1)]
+        lines.append(jnp.zeros((8, 256), F32))
+        sends.append(jnp.concatenate(lines, axis=0).astype(BF16))
+    odd = parity()
+
+    @pl.when(odd == 0)
+    def _():
+        first_ref[...], second_ref[...] = sends[0], sends[1]
+
+    @pl.when(odd == 1)
+    def _():
+        first_ref[...], second_ref[...] = sends[1], sends[0]
 
 
 def home_second(wall_ref, field_ref, tend_ref, bubble_ref, rate_ref, owner_ref, dest_ref,
@@ -433,36 +443,62 @@
     return push_of(scatter(load_ref, come_ref), field_ref[...])
 
 
-def low_second(base_ref, field_ref, low_ref, low2_ref, come_ref, out_ref, load_ref):
-    push = late_push(low_ref, low2_ref, field_ref, come_ref, load_ref)
+def late_side(below, base_ref, field_ref, cells_ref, come_ref, got_ref, out_ref, load_ref):
+    push = late_push(cells_ref, got_ref, field_ref, come_ref, load_ref)
     for a in range(3):
         for z in range(4):
             base = (a * 4 + z) * 16
-            total = base_ref[base : base + 16] + C2 * push[base : base + 16]
-            if z == 0:
-                total = total + C2 * below_term(field_ref, low2_ref[a * 16 : a * 16 + 16, :].astype(F32))
-            out_ref[base : base + 16] = total
-
-
-def high_second(base_ref, field_ref, high_ref, low2_ref, high2_ref, late_ref, put_ref, come_ref,
-                out_ref, bubble_ref, load_ref):
-    returned = jnp.concatenate(
-        [jnp.concatenate([ref[72 + a * 8 : 80 + a * 8, :].astype(F32) for ref in (high2_ref, low2_ref)], axis=0)
-         for a in range(3)],
-        axis=1,
-    )
-    back = jnp.dot(put_ref[...].astype(BF16), returned.astype(BF16), preferred_element_type=F32)
-    for a in range(3):
-        seen = back[:, a * 256 : a * 256 + 128] + back[:, a * 256 + 128 : a * 256 + 256]
-        bubble_ref[a] = late_ref[a] + (C2 / relax_time) * seen
-    push = late_push(high_ref, high2_ref, field_ref, come_ref, load_ref)
-    for a in range(3):
-        for z in range(4):
-            base = (a * 4 + z) * 16
-            total = base_ref[base : base + 16] + C2 * push[base : base + 16]
-            if z == 3:
-                total = total + C2 * above_term(field_ref, high2_ref[a * 16 : a * 16 + 16, :].astype(F32))
-            out_ref[base : base + 16] = total
+            total = push[base : base + 16]
+            if z == (0 if below else 3):
+                term = below_term if below else above_term
+                total = total + term(field_ref, got_ref[a * 16 : a * 16 + 16, :].astype(F32))
+            out_ref[base : base + 16] = base_ref[base : base + 16] + C2 * total
+
+
+def first_late(base_ref, field_ref, low_ref, high_ref, come_low_ref, come_high_ref, first_ref, out_ref, load_ref):
+    odd = parity()
+
+    @pl.when(odd == 0)
+    def _():
+        late_side(True, base_ref, field_ref, low_ref, come_low_ref, first_ref, out_ref, load_ref)
+
+    @pl.when(odd == 1)
+    def _():
+        late_side(False, base_ref, field_ref, high_ref, come_high_ref, first_ref, out_ref, load_ref)
+
+
+def second_late(base_ref, field_ref, low_ref, high_ref, come_low_ref, come_high_ref, first_ref, second_ref,
+                late_ref, put_ref, out_ref, bubble_ref, load_ref):
+    odd = parity()
+
+    def bubbles(high2_ref, low2_ref):
+        returned = jnp.concatenate(
+            [jnp.concatenate([ref[at : at + 8, :].astype(F32) for ref in (high2_ref, low2_ref)], axis=0) for at in (72, 80)],
+            axis=1,
+        )
+        back = jnp.dot(put_ref[...].astype(BF16), returned.astype(BF16), preferred_element_type=F32)
+        for a in range(3):
+            bubble_ref[a] = late_ref[a] + (C2 / relax_time) * back[:, a * 128 : (a + 1) * 128]
+
+    @pl.when(odd == 0)
+    def _():
+        bubbles(second_ref, first_ref)
+        late_side(False, base_ref, field_ref, high_ref, come_high_ref, second_ref, out_ref, load_ref)
+
+    @pl.when(odd == 1)
+    def _():
+        bubbles(first_ref, second_ref)
+        late_side(True, base_ref, field_ref, low_ref, come_low_ref, second_ref, out_ref, load_ref)
+
+
+def parity():
+    return lax.axis_index("pz") % 2
+
+
+def swapped(x, first):
+    length = lax.axis_size("pz")
+    step = [(1 if (i % 2 == 1) == first else -1) for i in range(length)]
+    return lax.ppermute(x, "pz", [(i, (i + step[i]) % length) for i in range(length)])
 
 
 def shifted(x, by):
@@ -516,16 +552,16 @@
     (walls,) = call(columns_body, (packed,))(columns, first_deriv, second_deriv)
     walls = exchange(walls)
     lasts = ((LAST_ROWS, 256), BF16)
-    middle, tend, up, down = call(middle_body, (block, block, lasts, lasts), (table,))(
-        walls, field, part, low, high, slots, come_low, come_high
-    )
-    low2, high2 = shifted(up, 1), shifted(down, -1)
-    base, late, put = call(
-        home_second, (block, rows, ((24, 16), F32)), (table, hots, loads)
-    )(walls, middle, tend, bubbles, rate, owner, dest)
-    (base,) = call(low_second, (block,), (load,))(base, middle, low, low2, come_low)
-    field, bubbles = call(high_second, (block, rows), (load,))(
-        base, middle, high, low2, high2, late, put, come_high
+    middle, tend, first, second = call(
+        middle_body, (block, block, lasts, lasts), (pltpu.VMEM((FIELD_ROWS, 256), BF16),)
+    )(walls, field, part, low, high, slots, come_low, come_high)
+    first, second = swapped(first, True), swapped(second, False)
+    base, late, put = call(home_second, (block, rows, ((24, 16), F32)), (table, hots, loads))(
+        walls, middle, tend, bubbles, rate, owner, dest
+    )
+    (base,) = call(first_late, (block,), (load,))(base, middle, low, high, come_low, come_high, first)
+    field, bubbles = call(second_late, (block, rows), (load,))(
+        base, middle, low, high, come_low, come_high, first, second, late, put
     )
     return (field.reshape(velocity.shape), bubbles)
 

time: 70.5 us -> 72.4 us (1.027)
  the two profiles are of different devices: /device:TPU:54 before, /device:TPU:8 now
where the time goes in v5:
time: 72.4 us; the launch traced here: 72.1 us
  blocking collectives  36.4 us (50%)
  starting transfers between devices  20.5 us (28%)
  Pallas kernels  9.8 us (14%)
  waiting for transfers between devices  4.66 us (6%)
  between operations  0.73 us (1%)
    all_to_all x2, blocking collectives, exchange(): return lax.all_to_all(x, 'px', split_axis=0, concat_axis=0, tiled=True)  36.4 us
    ppermute x2, starting transfers between devices, swapped(): lax.ppermute(x, 'pz', [(i, (i + step[i]) % length) for i in range(length)])  10.4 us
    ppermute x2, starting transfers between devices, shifted(): lax.ppermute(x, 'pz', [(i, (i + by) % length) for i in range(length)])  10.1 us
    ppermute x2, waiting for transfers between devices, swapped(): lax.ppermute(x, 'pz', [(i, (i + step[i]) % length) for i in range(length)])  2.52 us
    ppermute x2, waiting for transfers between devices, shifted(): lax.ppermute(x, 'pz', [(i, (i + by) % length) for i in range(length)])  2.14 us
    pallas_call x1, Pallas kernels, on_device(): call(home_second, (block, rows, ((24, 16), F32)), (table, hots, loads))  1.91 us
    pallas_call x1, Pallas kernels, on_device(): call(home_first, (block, rows, ((24, 16), F32), ((16, 24), F32)), (table,...  1.75 us
  transfers between devices with their start and end apart: 4, of which 3 were waited for; matrix products, arithmetic and copies ran while one was open for 0% of the time, Pallas kernels for 7%

profile of v5, /device:TPU:8, one launch (start us, length us, event | category | flops | bytes accessed | tf_op | source)
XLA Modules:
  0.0 72.1 jit_solution(5401513085664212872)
XLA Ops:
  0.6 1.2 %shard_map.77 = (bf16[240,256]{1,0:T(8,128)(2,1)S(1)}, bf16[240,256]{1,0:T(8,128)(2,1)S(1)}, f32[16,256]{1,0:T(8,128)S(1)}, f32[192,256]{1,0:T(8,128)S(1)}, f32[...) custom-call(f32[192,256]{1,0:T(8,128)} %bitcast.2, f32[3,24,128]{2,1,0:T(8,128)} %bubble_hbm.1, ...), custom_call_target="tpu_custom_call" | custom-call | tf_op jit(solution)/shard_map/pallas_call | solution.py:526
  1.9 4.5 %collective-permute-start = (bf16[240,256]{1,0:T(8,128)(2,1)S(1)}, bf16[240,256]{1,0:T(8,128)(2,1)S(1)}, u32[]{:S(2)}, u32[]{:S(2)}) collective-permute-start(bf16[240,256]{1,0:T(8,128)(2,1)S(1)} %get-tuple-element.36), channel_id=1, source_target_pairs={{0,1},{1,2},{2,3},{3,4},{4,5},{5,6},{6,7},{7,8},{8,9},{9,10},{10,1... | collective-permute-start | bytes 368648 | tf_op jit(solution)/shard_map/ppermute | solution.py:506
  6.4 5.6 %collective-permute-start.1 = (bf16[240,256]{1,0:T(8,128)(2,1)S(1)}, bf16[240,256]{1,0:T(8,128)(2,1)S(1)}, u32[]{:S(2)}, u32[]{:S(2)}) collective-permute-start(bf16[240,256]{1,0:T(8,128)(2,1)S(1)} %get-tuple-element.39), channel_id=1, source_target_pairs={{0,15},{1,0},{2,1},{3,2},{4,3},{5,4},{6,5},{7,6},{8,7},{9,8},{10,9... | collective-permute-start | bytes 368648 | tf_op jit(solution)/shard_map/ppermute | solution.py:506
  11.9 1.7 %shard_map.78 = (f32[192,256]{1,0:T(8,128)S(1)}, f32[3,24,128]{2,1,0:T(8,128)S(1)}, f32[24,16]{1,0:T(8,128)S(1)}, f32[16,24]{1,0:T(8,128)S(1)}) custom-call(f32[192,256]{1,0:T(8,128)S(1)} %get-tuple-element.31.field_ref, f32[3,24,128]{2,1,0:T(8,128)S(1)} %get-tuple-element.32.bubble_ref, s32[2,24,128]{2,1,0:T(8,128)S(1)} %get-tuple-element.33.owner_ref, ...), custom_call_target="tpu_custom_call" | custom-call | tf_op jit(solution)/shard_map/pallas_call | solution.py:541
  13.7 0.8 %collective-permute-done.low_ref = bf16[240,256]{1,0:T(8,128)(2,1)S(1)} collective-permute-done((bf16[240,256]{1,0:T(8,128)(2,1)S(1)}, bf16[240,256]{1,0:T(8,128)(2,1)S(1)}, u32[]{:S(2)}, u32[]{:S(2)}) %collective-permute-start) | collective-permute-done | bytes 122912 | tf_op jit(solution)/shard_map/ppermute | solution.py:506
  14.5 0.0 copy-start.1
  14.5 0.9 %shard_map.79 = (f32[192,256]{1,0:T(8,128)S(1)}, f32[3,8,128]{2,1,0:T(8,128)S(1)}, bf16[256,1024]{1,0:T(8,128)(2,1)S(1)}) custom-call(f32[192,256]{1,0:T(8,128)S(1)} %get-tuple-element.31.field_ref, f32[192,256]{1,0:T(8,128)S(1)} %get-tuple-element.35.part_ref, bf16[240,256]{1,0:T(8,128)(2,1)S(1)} %collective-permute-done.low_ref, ...), custom_call_target="tpu_custom_call" | custom-call | tf_op jit(solution)/shard_map/pallas_call | solution.py:545
  15.3 0.0 copy-start
  15.4 1.4 %collective-permute-done.1.high_ref = bf16[240,256]{1,0:T(8,128)(2,1)S(1)} collective-permute-done((bf16[240,256]{1,0:T(8,128)(2,1)S(1)}, bf16[240,256]{1,0:T(8,128)(2,1)S(1)}, u32[]{:S(2)}, u32[]{:S(2)}) %collective-permute-start.1) | collective-permute-done | bytes 122912 | tf_op jit(solution)/shard_map/ppermute | solution.py:506
  16.7 1.0 %shard_map.80 = (f32[192,256]{1,0:T(8,128)S(1)}, bf16[32,24,128]{2,1,0:T(8,128)(2,1)S(1)}, f32[3,24,128]{2,1,0:T(8,128)S(1)}, f32[3,24,128]{2,1,0:T(8,128)S(1)},...) custom-call(f32[192,256]{1,0:T(8,128)S(1)} %get-tuple-element.31.field_ref, ...), custom_call_target="tpu_custom_call" | custom-call | tf_op jit(solution)/shard_map/pallas_call | solution.py:548
  17.7 22.4 %all_to_all.10.got_ref = bf16[32,24,128]{2,1,0:T(8,128)(2,1)S(1)} all-to-all(bf16[32,24,128]{2,1,0:T(8,128)(2,1)S(1)} %get-tuple-element.44), channel_id=1, replica_groups=mesh['px'=32,'pz'=16] {'px'}, dimensions={0} | all-to-all | bytes 393216 | tf_op jit(solution)/shard_map/all_to_all | solution.py:510
  40.1 0.0 copy-done.1
  40.2 0.0 copy-done
  40.2 0.9 %shard_map.81 = bf16[32,24,128]{2,1,0:T(8,128)(2,1)S(1)} custom-call(bf16[32,24,128]{2,1,0:T(8,128)(2,1)S(1)} %all_to_all.10.got_ref, bf16[512,512]{1,0:T(8,128)(2,1)S(1)} %copy-done, bf16[512,512]{1,0:T(8,128)(2,1)S(1)} %copy-done.1), custom_call_target="tpu_custom_call" | custom-call | tf_op jit(solution)/shard_map/pallas_call | solution.py:552
  41.1 13.9 %all_to_all.11.wall_ref = bf16[32,24,128]{2,1,0:T(8,128)(2,1)S(1)} all-to-all(bf16[32,24,128]{2,1,0:T(8,128)(2,1)S(1)} %shard_map.81), channel_id=1, replica_groups=mesh['px'=32,'pz'=16] {'px'}, dimensions={0} | all-to-all | bytes 393216 | tf_op jit(solution)/shard_map/all_to_all | solution.py:510
  55.0 0.5 shard_map.82
  55.5 8.5 %collective-permute-start.2 = (bf16[96,256]{1,0:T(8,128)(2,1)S(1)}, bf16[96,256]{1,0:T(8,128)(2,1)S(1)}, u32[]{:S(2)}, u32[]{:S(2)}) collective-permute-start(bf16[96,256]{1,0:T(8,128)(2,1)S(1)} %get-tuple-element.54), channel_id=1, source_target_pairs={{0,15},{1,2},{2,1},{3,4},{4,3},{5,6},{6,5},{7,8},{8,7},{9,10},{10,... | collective-permute-start | bytes 147464 | tf_op jit(solution)/shard_map/ppermute | solution.py:501
  64.0 1.9 %collective-permute-start.3 = (bf16[96,256]{1,0:T(8,128)(2,1)S(1)}, bf16[96,256]{1,0:T(8,128)(2,1)S(1)}, u32[]{:S(2)}, u32[]{:S(2)}) collective-permute-start(bf16[96,256]{1,0:T(8,128)(2,1)S(1)} %get-tuple-element.55), channel_id=1, source_target_pairs={{0,1},{1,0},{2,3},{3,2},{4,5},{5,4},{6,7},{7,6},{8,9},{9,8},{10,11... | collective-permute-start | bytes 147464 | tf_op jit(solution)/shard_map/ppermute | solution.py:501
  65.9 1.9 %shard_map.83 = (f32[192,256]{1,0:T(8,128)S(1)}, f32[3,24,128]{2,1,0:T(8,128)S(1)}, f32[24,16]{1,0:T(8,128)S(1)}) custom-call(bf16[32,24,128]{2,1,0:T(8,128)(2,1)S(1)} %all_to_all.11.wall_ref, f32[192,256]{1,0:T(8,128)S(1)} %get-tuple-element.49.field_ref, f32[192,256]{1,0:T(8,128)S(1)} %get-tuple-element.50.tend_ref, ...), custom_call_target="tpu_custom_call" | custom-call | tf_op jit(solution)/shard_map/pallas_call | solution.py:559
  67.8 0.0 collective-permute-done.2.first_ref
  67.9 0.5 shard_map.84.base_ref
  68.4 2.5 %collective-permute-done.3.second_ref = bf16[96,256]{1,0:T(8,128)(2,1)S(1)} collective-permute-done((bf16[96,256]{1,0:T(8,128)(2,1)S(1)}, bf16[96,256]{1,0:T(8,128)(2,1)S(1)}, u32[]{:S(2)}, u32[]{:S(2)}) %collective-permute-start.3) | collective-permute-done | bytes 49184 | tf_op jit(solution)/shard_map/ppermute | solution.py:501
  70.9 1.2 %shard_map.85 = (f32[192,256]{1,0:T(8,128)}, f32[3,24,128]{2,1,0:T(8,128)}) custom-call(f32[192,256]{1,0:T(8,128)S(1)} %shard_map.84.base_ref, f32[192,256]{1,0:T(8,128)S(1)} %get-tuple-element.49.field_ref, bf16[240,256]{1,0:T(8,128)(2,1)S(1)} %collective-permute-done.low_ref, bf16[240,256]{1,0:T(8,128)(2,1)S(1)} %collective-permute-done.1.high_ref, ...), custom_call_target="tpu_custom_call" | custom-call | tf_op jit(solution)/shard_map/pallas_call | solution.py:563
Async XLA Ops:
  1.9 12.6 %collective-permute-start = (bf16[240,256]{1,0:T(8,128)(2,1)S(1)}, bf16[240,256]{1,0:T(8,128)(2,1)S(1)}, u32[]{:S(2)}, u32[]{:S(2)}) collective-permute-start(bf16[240,256]{1,0:T(8,128)(2,1)S(1)} %get-tuple-element.36), channel_id=1, source_target_pairs={{0,1},{1,2},{2,3},{3,4},{4,5},{5,6},{6,7},{7,8},{8,9},{9,10},{10,1... | collective-permute-start | bytes 368648 | tf_op jit(solution)/shard_map/ppermute | solution.py:506
  6.4 10.4 %collective-permute-start.1 = (bf16[240,256]{1,0:T(8,128)(2,1)S(1)}, bf16[240,256]{1,0:T(8,128)(2,1)S(1)}, u32[]{:S(2)}, u32[]{:S(2)}) collective-permute-start(bf16[240,256]{1,0:T(8,128)(2,1)S(1)} %get-tuple-element.39), channel_id=1, source_target_pairs={{0,15},{1,0},{2,1},{3,2},{4,3},{5,4},{6,5},{7,6},{8,7},{9,8},{10,9... | collective-permute-start | bytes 368648 | tf_op jit(solution)/shard_map/ppermute | solution.py:506
  14.5 25.7 %copy-start.1 = (bf16[512,512]{1,0:T(8,128)(2,1)S(1)}, bf16[512,512]{1,0:T(8,128)(2,1)}, u32[]{:S(2)}) copy-start(bf16[512,512]{1,0:T(8,128)(2,1)} %second_ref.1) | copy-start | bytes 1572868
  15.3 24.8 %copy-start = (bf16[512,512]{1,0:T(8,128)(2,1)S(1)}, bf16[512,512]{1,0:T(8,128)(2,1)}, u32[]{:S(2)}) copy-start(bf16[512,512]{1,0:T(8,128)(2,1)} %first_ref.1) | copy-start | bytes 1572868
  55.5 12.4 %collective-permute-start.2 = (bf16[96,256]{1,0:T(8,128)(2,1)S(1)}, bf16[96,256]{1,0:T(8,128)(2,1)S(1)}, u32[]{:S(2)}, u32[]{:S(2)}) collective-permute-start(bf16[96,256]{1,0:T(8,128)(2,1)S(1)} %get-tuple-element.54), channel_id=1, source_target_pairs={{0,15},{1,2},{2,1},{3,4},{4,3},{5,6},{6,5},{7,8},{8,7},{9,10},{10,... | collective-permute-start | bytes 147464 | tf_op jit(solution)/shard_map/ppermute | solution.py:501
  64.0 6.9 %collective-permute-start.3 = (bf16[96,256]{1,0:T(8,128)(2,1)S(1)}, bf16[96,256]{1,0:T(8,128)(2,1)S(1)}, u32[]{:S(2)}, u32[]{:S(2)}) collective-permute-start(bf16[96,256]{1,0:T(8,128)(2,1)S(1)} %get-tuple-element.55), channel_id=1, source_target_pairs={{0,1},{1,0},{2,3},{3,2},{4,5},{5,4},{6,7},{7,6},{8,9},{9,8},{10,11... | collective-permute-start | bytes 147464 | tf_op jit(solution)/shard_map/ppermute | solution.py:501

commit v6 on v5

--- a/solution.py
+++ b/solution.py
@@ -378,7 +378,7 @@
 
 
 def middle_body(wall_ref, field_ref, part_ref, low_ref, high_ref, slots_ref, come_low_ref, come_high_ref,
-                next_ref, tend_ref, first_ref, second_ref, table_ref):
+                next_ref, tend_ref, down_ref, up_ref, table_ref):
     for a in range(3):
         for z in range(4):
             base = (a * 4 + z) * 16
@@ -395,15 +395,7 @@
         lines += [jnp.concatenate(seen[0:2], axis=1), jnp.concatenate([seen[2], jnp.zeros((8, 128), F32)], axis=1)]
         lines.append(jnp.zeros((8, 256), F32))
         sends.append(jnp.concatenate(lines, axis=0).astype(BF16))
-    odd = parity()
-
-    @pl.when(odd == 0)
-    def _():
-        first_ref[...], second_ref[...] = sends[0], sends[1]
-
-    @pl.when(odd == 1)
-    def _():
-        first_ref[...], second_ref[...] = sends[1], sends[0]
+    down_ref[...], up_ref[...] = sends
 
 
 def home_second(wall_ref, field_ref, tend_ref, bubble_ref, rate_ref, owner_ref, dest_ref,
@@ -455,50 +447,20 @@
             out_ref[base : base + 16] = base_ref[base : base + 16] + C2 * total
 
 
-def first_late(base_ref, field_ref, low_ref, high_ref, come_low_ref, come_high_ref, first_ref, out_ref, load_ref):
-    odd = parity()
-
-    @pl.when(odd == 0)
-    def _():
-        late_side(True, base_ref, field_ref, low_ref, come_low_ref, first_ref, out_ref, load_ref)
-
-    @pl.when(odd == 1)
-    def _():
-        late_side(False, base_ref, field_ref, high_ref, come_high_ref, first_ref, out_ref, load_ref)
-
-
-def second_late(base_ref, field_ref, low_ref, high_ref, come_low_ref, come_high_ref, first_ref, second_ref,
-                late_ref, put_ref, out_ref, bubble_ref, load_ref):
-    odd = parity()
-
-    def bubbles(high2_ref, low2_ref):
-        returned = jnp.concatenate(
-            [jnp.concatenate([ref[at : at + 8, :].astype(F32) for ref in (high2_ref, low2_ref)], axis=0) for at in (72, 80)],
-            axis=1,
-        )
-        back = jnp.dot(put_ref[...].astype(BF16), returned.astype(BF16), preferred_element_type=F32)
-        for a in range(3):
-            bubble_ref[a] = late_ref[a] + (C2 / relax_time) * back[:, a * 128 : (a + 1) * 128]
-
-    @pl.when(odd == 0)
-    def _():
-        bubbles(second_ref, first_ref)
-        late_side(False, base_ref, field_ref, high_ref, come_high_ref, second_ref, out_ref, load_ref)
-
-    @pl.when(odd == 1)
-    def _():
-        bubbles(first_ref, second_ref)
-        late_side(True, base_ref, field_ref, low_ref, come_low_ref, second_ref, out_ref, load_ref)
-
-
-def parity():
-    return lax.axis_index("pz") % 2
-
-
-def swapped(x, first):
-    length = lax.axis_size("pz")
-    step = [(1 if (i % 2 == 1) == first else -1) for i in range(length)]
-    return lax.ppermute(x, "pz", [(i, (i + step[i]) % length) for i in range(length)])
+def high_second(base_ref, field_ref, high_ref, come_ref, high2_ref, out_ref, load_ref):
+    late_side(False, base_ref, field_ref, high_ref, come_ref, high2_ref, out_ref, load_ref)
+
+
+def low_second(base_ref, field_ref, low_ref, come_ref, high2_ref, low2_ref, late_ref, put_ref,
+               out_ref, bubble_ref, load_ref):
+    returned = jnp.concatenate(
+        [jnp.concatenate([ref[at : at + 8, :].astype(F32) for ref in (high2_ref, low2_ref)], axis=0) for at in (72, 80)],
+        axis=1,
+    )
+    back = jnp.dot(put_ref[...].astype(BF16), returned.astype(BF16), preferred_element_type=F32)
+    for a in range(3):
+        bubble_ref[a] = late_ref[a] + (C2 / relax_time) * back[:, a * 128 : (a + 1) * 128]
+    late_side(True, base_ref, field_ref, low_ref, come_ref, low2_ref, out_ref, load_ref)
 
 
 def shifted(x, by):
@@ -552,16 +514,16 @@
     (walls,) = call(columns_body, (packed,))(columns, first_deriv, second_deriv)
     walls = exchange(walls)
     lasts = ((LAST_ROWS, 256), BF16)
-    middle, tend, first, second = call(
+    middle, tend, down, up = call(
         middle_body, (block, block, lasts, lasts), (pltpu.VMEM((FIELD_ROWS, 256), BF16),)
     )(walls, field, part, low, high, slots, come_low, come_high)
-    first, second = swapped(first, True), swapped(second, False)
+    high2, low2 = shifted(down, -1), shifted(up, 1)
     base, late, put = call(home_second, (block, rows, ((24, 16), F32)), (table, hots, loads))(
         walls, middle, tend, bubbles, rate, owner, dest
     )
-    (base,) = call(first_late, (block,), (load,))(base, middle, low, high, come_low, come_high, first)
-    field, bubbles = call(second_late, (block, rows), (load,))(
-        base, middle, low, high, come_low, come_high, first, second, late, put
+    (base,) = call(high_second, (block,), (load,))(base, middle, high, come_high, high2)
+    field, bubbles = call(low_second, (block, rows), (load,))(
+        base, middle, low, come_low, high2, low2, late, put
     )
     return (field.reshape(velocity.shape), bubbles)
 

time: 72.4 us -> 76.2 us (1.052)
  waiting for transfers between devices: 4.66 us -> 8.53 us
    ppermute x2 -> x0, starting transfers between devices: 10.4 us -> none  [swapped(): lax.ppermute(x, 'pz', [(i, (i + step[i]) % length) for i in range(length)])]
    ppermute x2 -> x4, starting transfers between devices: 10.1 us -> 20.5 us  [shifted(): lax.ppermute(x, 'pz', [(i, (i + by) % length) for i in range(length)])]
    ppermute x2 -> x4, waiting for transfers between devices: 2.14 us -> 8.53 us  [shifted(): lax.ppermute(x, 'pz', [(i, (i + by) % length) for i in range(length)])]
    ppermute x2 -> x0, waiting for transfers between devices: 2.52 us -> none  [swapped(): lax.ppermute(x, 'pz', [(i, (i + step[i]) % length) for i in range(length)])]
where the time goes in v6:
time: 76.2 us; the launch traced here: 75.9 us
  blocking collectives  36.4 us (48%)
  starting transfers between devices  20.5 us (27%)
  Pallas kernels  9.73 us (13%)
  waiting for transfers between devices  8.53 us (11%)
    all_to_all x2, blocking collectives, exchange(): return lax.all_to_all(x, 'px', split_axis=0, concat_axis=0, tiled=True)  36.4 us
    ppermute x4, starting transfers between devices, shifted(): lax.ppermute(x, 'pz', [(i, (i + by) % length) for i in range(length)])  20.5 us
    ppermute x4, waiting for transfers between devices, shifted(): lax.ppermute(x, 'pz', [(i, (i + by) % length) for i in range(length)])  8.53 us
    pallas_call x1, Pallas kernels, on_device(): call(home_second, (block, rows, ((24, 16), F32)), (table, hots, loads))  1.87 us
    pallas_call x1, Pallas kernels, on_device(): call(home_first, (block, rows, ((24, 16), F32), ((16, 24), F32)), (table,...  1.75 us
  transfers between devices with their start and end apart: 4, of which 3 were waited for; matrix products, arithmetic and copies ran while one was open for 0% of the time, Pallas kernels for 7%

profile of v6, /device:TPU:8, one launch (start us, length us, event | category | flops | bytes accessed | tf_op | source)
XLA Modules:
  0.0 75.9 jit_solution(15627022110818053133)
XLA Ops:
  0.6 1.2 %shard_map.77 = (bf16[240,256]{1,0:T(8,128)(2,1)S(1)}, bf16[240,256]{1,0:T(8,128)(2,1)S(1)}, f32[16,256]{1,0:T(8,128)S(1)}, f32[192,256]{1,0:T(8,128)S(1)}, f32[...) custom-call(f32[192,256]{1,0:T(8,128)} %bitcast.2, f32[3,24,128]{2,1,0:T(8,128)} %bubble_hbm.1, ...), custom_call_target="tpu_custom_call" | custom-call | tf_op jit(solution)/shard_map/pallas_call | solution.py:488
  1.9 4.5 %collective-permute-start = (bf16[240,256]{1,0:T(8,128)(2,1)S(1)}, bf16[240,256]{1,0:T(8,128)(2,1)S(1)}, u32[]{:S(2)}, u32[]{:S(2)}) collective-permute-start(bf16[240,256]{1,0:T(8,128)(2,1)S(1)} %get-tuple-element.36), channel_id=1, source_target_pairs={{0,1},{1,2},{2,3},{3,4},{4,5},{5,6},{6,7},{7,8},{8,9},{9,10},{10,1... | collective-permute-start | bytes 368648 | tf_op jit(solution)/shard_map/ppermute | solution.py:468
  6.4 5.6 %collective-permute-start.1 = (bf16[240,256]{1,0:T(8,128)(2,1)S(1)}, bf16[240,256]{1,0:T(8,128)(2,1)S(1)}, u32[]{:S(2)}, u32[]{:S(2)}) collective-permute-start(bf16[240,256]{1,0:T(8,128)(2,1)S(1)} %get-tuple-element.39), channel_id=1, source_target_pairs={{0,15},{1,0},{2,1},{3,2},{4,3},{5,4},{6,5},{7,6},{8,7},{9,8},{10,9... | collective-permute-start | bytes 368648 | tf_op jit(solution)/shard_map/ppermute | solution.py:468
  11.9 1.7 %shard_map.78 = (f32[192,256]{1,0:T(8,128)S(1)}, f32[3,24,128]{2,1,0:T(8,128)S(1)}, f32[24,16]{1,0:T(8,128)S(1)}, f32[16,24]{1,0:T(8,128)S(1)}) custom-call(f32[192,256]{1,0:T(8,128)S(1)} %get-tuple-element.31.field_ref, f32[3,24,128]{2,1,0:T(8,128)S(1)} %get-tuple-element.32.bubble_ref, s32[2,24,128]{2,1,0:T(8,128)S(1)} %get-tuple-element.33.owner_ref, ...), custom_call_target="tpu_custom_call" | custom-call | tf_op jit(solution)/shard_map/pallas_call | solution.py:503
  13.7 0.8 %collective-permute-done.low_ref = bf16[240,256]{1,0:T(8,128)(2,1)S(1)} collective-permute-done((bf16[240,256]{1,0:T(8,128)(2,1)S(1)}, bf16[240,256]{1,0:T(8,128)(2,1)S(1)}, u32[]{:S(2)}, u32[]{:S(2)}) %collective-permute-start) | collective-permute-done | bytes 122912 | tf_op jit(solution)/shard_map/ppermute | solution.py:468
  14.5 0.0 copy-start.1
  14.5 0.9 %shard_map.79 = (f32[192,256]{1,0:T(8,128)S(1)}, f32[3,8,128]{2,1,0:T(8,128)S(1)}, bf16[256,1024]{1,0:T(8,128)(2,1)S(1)}) custom-call(f32[192,256]{1,0:T(8,128)S(1)} %get-tuple-element.31.field_ref, f32[192,256]{1,0:T(8,128)S(1)} %get-tuple-element.35.part_ref, bf16[240,256]{1,0:T(8,128)(2,1)S(1)} %collective-permute-done.low_ref, ...), custom_call_target="tpu_custom_call" | custom-call | tf_op jit(solution)/shard_map/pallas_call | solution.py:507
  15.3 0.0 copy-start
  15.4 1.4 %collective-permute-done.1.high_ref = bf16[240,256]{1,0:T(8,128)(2,1)S(1)} collective-permute-done((bf16[240,256]{1,0:T(8,128)(2,1)S(1)}, bf16[240,256]{1,0:T(8,128)(2,1)S(1)}, u32[]{:S(2)}, u32[]{:S(2)}) %collective-permute-start.1) | collective-permute-done | bytes 122912 | tf_op jit(solution)/shard_map/ppermute | solution.py:468
  16.7 1.0 %shard_map.80 = (f32[192,256]{1,0:T(8,128)S(1)}, bf16[32,24,128]{2,1,0:T(8,128)(2,1)S(1)}, f32[3,24,128]{2,1,0:T(8,128)S(1)}, f32[3,24,128]{2,1,0:T(8,128)S(1)},...) custom-call(f32[192,256]{1,0:T(8,128)S(1)} %get-tuple-element.31.field_ref, ...), custom_call_target="tpu_custom_call" | custom-call | tf_op jit(solution)/shard_map/pallas_call | solution.py:510
  17.7 22.4 %all_to_all.10.got_ref = bf16[32,24,128]{2,1,0:T(8,128)(2,1)S(1)} all-to-all(bf16[32,24,128]{2,1,0:T(8,128)(2,1)S(1)} %get-tuple-element.44), channel_id=1, replica_groups=mesh['px'=32,'pz'=16] {'px'}, dimensions={0} | all-to-all | bytes 393216 | tf_op jit(solution)/shard_map/all_to_all | solution.py:472
  40.1 0.0 copy-done.1
  40.2 0.0 copy-done
  40.2 0.9 %shard_map.81 = bf16[32,24,128]{2,1,0:T(8,128)(2,1)S(1)} custom-call(bf16[32,24,128]{2,1,0:T(8,128)(2,1)S(1)} %all_to_all.10.got_ref, bf16[512,512]{1,0:T(8,128)(2,1)S(1)} %copy-done, bf16[512,512]{1,0:T(8,128)(2,1)S(1)} %copy-done.1), custom_call_target="tpu_custom_call" | custom-call | tf_op jit(solution)/shard_map/pallas_call | solution.py:514
  41.1 13.9 %all_to_all.11.wall_ref = bf16[32,24,128]{2,1,0:T(8,128)(2,1)S(1)} all-to-all(bf16[32,24,128]{2,1,0:T(8,128)(2,1)S(1)} %shard_map.81), channel_id=1, replica_groups=mesh['px'=32,'pz'=16] {'px'}, dimensions={0} | all-to-all | bytes 393216 | tf_op jit(solution)/shard_map/all_to_all | solution.py:472
  55.0 0.5 shard_map.82
  55.5 8.5 %collective-permute-start.2 = (bf16[96,256]{1,0:T(8,128)(2,1)S(1)}, bf16[96,256]{1,0:T(8,128)(2,1)S(1)}, u32[]{:S(2)}, u32[]{:S(2)}) collective-permute-start(bf16[96,256]{1,0:T(8,128)(2,1)S(1)} %get-tuple-element.54), channel_id=1, source_target_pairs={{0,15},{1,0},{2,1},{3,2},{4,3},{5,4},{6,5},{7,6},{8,7},{9,8},{10,9... | collective-permute-start | bytes 147464 | tf_op jit(solution)/shard_map/ppermute | solution.py:468
  64.0 1.9 %collective-permute-start.3 = (bf16[96,256]{1,0:T(8,128)(2,1)S(1)}, bf16[96,256]{1,0:T(8,128)(2,1)S(1)}, u32[]{:S(2)}, u32[]{:S(2)}) collective-permute-start(bf16[96,256]{1,0:T(8,128)(2,1)S(1)} %get-tuple-element.55), channel_id=1, source_target_pairs={{0,1},{1,2},{2,3},{3,4},{4,5},{5,6},{6,7},{7,8},{8,9},{9,10},{10,1... | collective-permute-start | bytes 147464 | tf_op jit(solution)/shard_map/ppermute | solution.py:468
  65.9 1.9 %shard_map.83 = (f32[192,256]{1,0:T(8,128)S(1)}, f32[3,24,128]{2,1,0:T(8,128)S(1)}, f32[24,16]{1,0:T(8,128)S(1)}) custom-call(bf16[32,24,128]{2,1,0:T(8,128)(2,1)S(1)} %all_to_all.11.wall_ref, f32[192,256]{1,0:T(8,128)S(1)} %get-tuple-element.49.field_ref, f32[192,256]{1,0:T(8,128)S(1)} %get-tuple-element.50.tend_ref, ...), custom_call_target="tpu_custom_call" | custom-call | tf_op jit(solution)/shard_map/pallas_call | solution.py:521
  67.8 0.0 collective-permute-done.2.high2_ref
  67.8 0.5 shard_map.84.base_ref
  68.3 6.4 %collective-permute-done.3.low2_ref = bf16[96,256]{1,0:T(8,128)(2,1)S(1)} collective-permute-done((bf16[96,256]{1,0:T(8,128)(2,1)S(1)}, bf16[96,256]{1,0:T(8,128)(2,1)S(1)}, u32[]{:S(2)}, u32[]{:S(2)}) %collective-permute-start.3) | collective-permute-done | bytes 49184 | tf_op jit(solution)/shard_map/ppermute | solution.py:468
  74.7 1.2 %shard_map.85 = (f32[192,256]{1,0:T(8,128)}, f32[3,24,128]{2,1,0:T(8,128)}) custom-call(f32[192,256]{1,0:T(8,128)S(1)} %shard_map.84.base_ref, f32[192,256]{1,0:T(8,128)S(1)} %get-tuple-element.49.field_ref, bf16[240,256]{1,0:T(8,128)(2,1)S(1)} %collective-permute-done.low_ref, bf16[256,1024]{1,0:T(8,128)(2,1)S(1)} %get-tuple-element.47.come_low_ref.come_ref, ...), custom_call_target="tpu_custom_call" | custom-call | tf_op jit(solution)/shard_map/pallas_call | solution.py:525
Async XLA Ops:
  1.9 12.6 %collective-permute-start = (bf16[240,256]{1,0:T(8,128)(2,1)S(1)}, bf16[240,256]{1,0:T(8,128)(2,1)S(1)}, u32[]{:S(2)}, u32[]{:S(2)}) collective-permute-start(bf16[240,256]{1,0:T(8,128)(2,1)S(1)} %get-tuple-element.36), channel_id=1, source_target_pairs={{0,1},{1,2},{2,3},{3,4},{4,5},{5,6},{6,7},{7,8},{8,9},{9,10},{10,1... | collective-permute-start | bytes 368648 | tf_op jit(solution)/shard_map/ppermute | solution.py:468
  6.4 10.4 %collective-permute-start.1 = (bf16[240,256]{1,0:T(8,128)(2,1)S(1)}, bf16[240,256]{1,0:T(8,128)(2,1)S(1)}, u32[]{:S(2)}, u32[]{:S(2)}) collective-permute-start(bf16[240,256]{1,0:T(8,128)(2,1)S(1)} %get-tuple-element.39), channel_id=1, source_target_pairs={{0,15},{1,0},{2,1},{3,2},{4,3},{5,4},{6,5},{7,6},{8,7},{9,8},{10,9... | collective-permute-start | bytes 368648 | tf_op jit(solution)/shard_map/ppermute | solution.py:468
  14.5 25.7 %copy-start.1 = (bf16[512,512]{1,0:T(8,128)(2,1)S(1)}, bf16[512,512]{1,0:T(8,128)(2,1)}, u32[]{:S(2)}) copy-start(bf16[512,512]{1,0:T(8,128)(2,1)} %second_ref.1) | copy-start | bytes 1572868
  15.3 24.8 %copy-start = (bf16[512,512]{1,0:T(8,128)(2,1)S(1)}, bf16[512,512]{1,0:T(8,128)(2,1)}, u32[]{:S(2)}) copy-start(bf16[512,512]{1,0:T(8,128)(2,1)} %first_ref.1) | copy-start | bytes 1572868
  55.5 12.3 %collective-permute-start.2 = (bf16[96,256]{1,0:T(8,128)(2,1)S(1)}, bf16[96,256]{1,0:T(8,128)(2,1)S(1)}, u32[]{:S(2)}, u32[]{:S(2)}) collective-permute-start(bf16[96,256]{1,0:T(8,128)(2,1)S(1)} %get-tuple-element.54), channel_id=1, source_target_pairs={{0,15},{1,0},{2,1},{3,2},{4,3},{5,4},{6,5},{7,6},{8,7},{9,8},{10,9... | collective-permute-start | bytes 147464 | tf_op jit(solution)/shard_map/ppermute | solution.py:468
  64.0 10.7 %collective-permute-start.3 = (bf16[96,256]{1,0:T(8,128)(2,1)S(1)}, bf16[96,256]{1,0:T(8,128)(2,1)S(1)}, u32[]{:S(2)}, u32[]{:S(2)}) collective-permute-start(bf16[96,256]{1,0:T(8,128)(2,1)S(1)} %get-tuple-element.55), channel_id=1, source_target_pairs={{0,1},{1,2},{2,3},{3,4},{4,5},{5,6},{6,7},{7,8},{8,9},{9,10},{10,1... | collective-permute-start | bytes 147464 | tf_op jit(solution)/shard_map/ppermute | solution.py:468

commit v7 on v5

--- a/solution.py
+++ b/solution.py
@@ -492,12 +492,12 @@
 
 
 def parity():
-    return lax.axis_index("pz") % 2
+    return (lax.axis_index("pz") + 1) % 2
 
 
 def swapped(x, first):
     length = lax.axis_size("pz")
-    step = [(1 if (i % 2 == 1) == first else -1) for i in range(length)]
+    step = [(1 if (i % 2 == 0) == first else -1) for i in range(length)]
     return lax.ppermute(x, "pz", [(i, (i + step[i]) % length) for i in range(length)])
 
 

time: 72.4 us -> 73.3 us (1.012)
  waiting for transfers between devices: 4.66 us -> 5.61 us
    ppermute x2, waiting for transfers between devices: 2.52 us -> 3.47 us  [swapped(): lax.ppermute(x, 'pz', [(i, (i + step[i]) % length) for i in range(length)])]
where the time goes in v7:
time: 73.3 us; the launch traced here: 73 us
  blocking collectives  36.4 us (50%)
  starting transfers between devices  20.5 us (28%)
  Pallas kernels  9.79 us (13%)
  waiting for transfers between devices  5.61 us (8%)
    all_to_all x2, blocking collectives, exchange(): return lax.all_to_all(x, 'px', split_axis=0, concat_axis=0, tiled=True)  36.4 us
    ppermute x2, starting transfers between devices, swapped(): lax.ppermute(x, 'pz', [(i, (i + step[i]) % length) for i in range(length)])  10.4 us
    ppermute x2, starting transfers between devices, shifted(): lax.ppermute(x, 'pz', [(i, (i + by) % length) for i in range(length)])  10.1 us
    ppermute x2, waiting for transfers between devices, swapped(): lax.ppermute(x, 'pz', [(i, (i + step[i]) % length) for i in range(length)])  3.47 us
    ppermute x2, waiting for transfers between devices, shifted(): lax.ppermute(x, 'pz', [(i, (i + by) % length) for i in range(length)])  2.14 us
    pallas_call x1, Pallas kernels, on_device(): call(home_second, (block, rows, ((24, 16), F32)), (table, hots, loads))  1.9 us
    pallas_call x1, Pallas kernels, on_device(): call(home_first, (block, rows, ((24, 16), F32), ((16, 24), F32)), (table,...  1.75 us
  transfers between devices with their start and end apart: 4, of which 3 were waited for; matrix products, arithmetic and copies ran while one was open for 0% of the time, Pallas kernels for 7%

profile of v7, /device:TPU:8, one launch (start us, length us, event | category | flops | bytes accessed | tf_op | source)
XLA Modules:
  0.0 73.0 jit_solution(16887908639087245483)
XLA Ops:
  0.6 1.2 %shard_map.77 = (bf16[240,256]{1,0:T(8,128)(2,1)S(1)}, bf16[240,256]{1,0:T(8,128)(2,1)S(1)}, f32[16,256]{1,0:T(8,128)S(1)}, f32[192,256]{1,0:T(8,128)S(1)}, f32[...) custom-call(f32[192,256]{1,0:T(8,128)} %bitcast.2, f32[3,24,128]{2,1,0:T(8,128)} %bubble_hbm.1, ...), custom_call_target="tpu_custom_call" | custom-call | tf_op jit(solution)/shard_map/pallas_call | solution.py:526
  1.9 4.5 %collective-permute-start = (bf16[240,256]{1,0:T(8,128)(2,1)S(1)}, bf16[240,256]{1,0:T(8,128)(2,1)S(1)}, u32[]{:S(2)}, u32[]{:S(2)}) collective-permute-start(bf16[240,256]{1,0:T(8,128)(2,1)S(1)} %get-tuple-element.36), channel_id=1, source_target_pairs={{0,1},{1,2},{2,3},{3,4},{4,5},{5,6},{6,7},{7,8},{8,9},{9,10},{10,1... | collective-permute-start | bytes 368648 | tf_op jit(solution)/shard_map/ppermute | solution.py:506
  6.4 5.6 %collective-permute-start.1 = (bf16[240,256]{1,0:T(8,128)(2,1)S(1)}, bf16[240,256]{1,0:T(8,128)(2,1)S(1)}, u32[]{:S(2)}, u32[]{:S(2)}) collective-permute-start(bf16[240,256]{1,0:T(8,128)(2,1)S(1)} %get-tuple-element.39), channel_id=1, source_target_pairs={{0,15},{1,0},{2,1},{3,2},{4,3},{5,4},{6,5},{7,6},{8,7},{9,8},{10,9... | collective-permute-start | bytes 368648 | tf_op jit(solution)/shard_map/ppermute | solution.py:506
  11.9 1.7 %shard_map.78 = (f32[192,256]{1,0:T(8,128)S(1)}, f32[3,24,128]{2,1,0:T(8,128)S(1)}, f32[24,16]{1,0:T(8,128)S(1)}, f32[16,24]{1,0:T(8,128)S(1)}) custom-call(f32[192,256]{1,0:T(8,128)S(1)} %get-tuple-element.31.field_ref, f32[3,24,128]{2,1,0:T(8,128)S(1)} %get-tuple-element.32.bubble_ref, s32[2,24,128]{2,1,0:T(8,128)S(1)} %get-tuple-element.33.owner_ref, ...), custom_call_target="tpu_custom_call" | custom-call | tf_op jit(solution)/shard_map/pallas_call | solution.py:541
  13.7 0.8 %collective-permute-done.low_ref = bf16[240,256]{1,0:T(8,128)(2,1)S(1)} collective-permute-done((bf16[240,256]{1,0:T(8,128)(2,1)S(1)}, bf16[240,256]{1,0:T(8,128)(2,1)S(1)}, u32[]{:S(2)}, u32[]{:S(2)}) %collective-permute-start) | collective-permute-done | bytes 122912 | tf_op jit(solution)/shard_map/ppermute | solution.py:506
  14.5 0.0 copy-start.1
  14.5 0.9 %shard_map.79 = (f32[192,256]{1,0:T(8,128)S(1)}, f32[3,8,128]{2,1,0:T(8,128)S(1)}, bf16[256,1024]{1,0:T(8,128)(2,1)S(1)}) custom-call(f32[192,256]{1,0:T(8,128)S(1)} %get-tuple-element.31.field_ref, f32[192,256]{1,0:T(8,128)S(1)} %get-tuple-element.35.part_ref, bf16[240,256]{1,0:T(8,128)(2,1)S(1)} %collective-permute-done.low_ref, ...), custom_call_target="tpu_custom_call" | custom-call | tf_op jit(solution)/shard_map/pallas_call | solution.py:545
  15.3 0.0 copy-start
  15.4 1.4 %collective-permute-done.1.high_ref = bf16[240,256]{1,0:T(8,128)(2,1)S(1)} collective-permute-done((bf16[240,256]{1,0:T(8,128)(2,1)S(1)}, bf16[240,256]{1,0:T(8,128)(2,1)S(1)}, u32[]{:S(2)}, u32[]{:S(2)}) %collective-permute-start.1) | collective-permute-done | bytes 122912 | tf_op jit(solution)/shard_map/ppermute | solution.py:506
  16.7 1.0 %shard_map.80 = (f32[192,256]{1,0:T(8,128)S(1)}, bf16[32,24,128]{2,1,0:T(8,128)(2,1)S(1)}, f32[3,24,128]{2,1,0:T(8,128)S(1)}, f32[3,24,128]{2,1,0:T(8,128)S(1)},...) custom-call(f32[192,256]{1,0:T(8,128)S(1)} %get-tuple-element.31.field_ref, ...), custom_call_target="tpu_custom_call" | custom-call | tf_op jit(solution)/shard_map/pallas_call | solution.py:548
  17.7 22.4 %all_to_all.10.got_ref = bf16[32,24,128]{2,1,0:T(8,128)(2,1)S(1)} all-to-all(bf16[32,24,128]{2,1,0:T(8,128)(2,1)S(1)} %get-tuple-element.44), channel_id=1, replica_groups=mesh['px'=32,'pz'=16] {'px'}, dimensions={0} | all-to-all | bytes 393216 | tf_op jit(solution)/shard_map/all_to_all | solution.py:510
  40.1 0.0 copy-done.1
  40.2 0.0 copy-done
  40.2 0.9 %shard_map.81 = bf16[32,24,128]{2,1,0:T(8,128)(2,1)S(1)} custom-call(bf16[32,24,128]{2,1,0:T(8,128)(2,1)S(1)} %all_to_all.10.got_ref, bf16[512,512]{1,0:T(8,128)(2,1)S(1)} %copy-done, bf16[512,512]{1,0:T(8,128)(2,1)S(1)} %copy-done.1), custom_call_target="tpu_custom_call" | custom-call | tf_op jit(solution)/shard_map/pallas_call | solution.py:552
  41.1 13.9 %all_to_all.11.wall_ref = bf16[32,24,128]{2,1,0:T(8,128)(2,1)S(1)} all-to-all(bf16[32,24,128]{2,1,0:T(8,128)(2,1)S(1)} %shard_map.81), channel_id=1, replica_groups=mesh['px'=32,'pz'=16] {'px'}, dimensions={0} | all-to-all | bytes 393216 | tf_op jit(solution)/shard_map/all_to_all | solution.py:510
  55.0 0.5 shard_map.82
  55.5 5.6 %collective-permute-start.2 = (bf16[96,256]{1,0:T(8,128)(2,1)S(1)}, bf16[96,256]{1,0:T(8,128)(2,1)S(1)}, u32[]{:S(2)}, u32[]{:S(2)}) collective-permute-start(bf16[96,256]{1,0:T(8,128)(2,1)S(1)} %get-tuple-element.54), channel_id=1, source_target_pairs={{0,1},{1,0},{2,3},{3,2},{4,5},{5,4},{6,7},{7,6},{8,9},{9,8},{10,11... | collective-permute-start | bytes 147464 | tf_op jit(solution)/shard_map/ppermute | solution.py:501
  61.1 4.8 %collective-permute-start.3 = (bf16[96,256]{1,0:T(8,128)(2,1)S(1)}, bf16[96,256]{1,0:T(8,128)(2,1)S(1)}, u32[]{:S(2)}, u32[]{:S(2)}) collective-permute-start(bf16[96,256]{1,0:T(8,128)(2,1)S(1)} %get-tuple-element.55), channel_id=1, source_target_pairs={{0,15},{1,2},{2,1},{3,4},{4,3},{5,6},{6,5},{7,8},{8,7},{9,10},{10,... | collective-permute-start | bytes 147464 | tf_op jit(solution)/shard_map/ppermute | solution.py:501
  65.9 1.9 %shard_map.83 = (f32[192,256]{1,0:T(8,128)S(1)}, f32[3,24,128]{2,1,0:T(8,128)S(1)}, f32[24,16]{1,0:T(8,128)S(1)}) custom-call(bf16[32,24,128]{2,1,0:T(8,128)(2,1)S(1)} %all_to_all.11.wall_ref, f32[192,256]{1,0:T(8,128)S(1)} %get-tuple-element.49.field_ref, f32[192,256]{1,0:T(8,128)S(1)} %get-tuple-element.50.tend_ref, ...), custom_call_target="tpu_custom_call" | custom-call | tf_op jit(solution)/shard_map/pallas_call | solution.py:559
  67.8 0.0 collective-permute-done.2.first_ref
  67.9 0.5 shard_map.84.base_ref
  68.4 3.5 %collective-permute-done.3.second_ref = bf16[96,256]{1,0:T(8,128)(2,1)S(1)} collective-permute-done((bf16[96,256]{1,0:T(8,128)(2,1)S(1)}, bf16[96,256]{1,0:T(8,128)(2,1)S(1)}, u32[]{:S(2)}, u32[]{:S(2)}) %collective-permute-start.3) | collective-permute-done | bytes 49184 | tf_op jit(solution)/shard_map/ppermute | solution.py:501
  71.8 1.2 %shard_map.85 = (f32[192,256]{1,0:T(8,128)}, f32[3,24,128]{2,1,0:T(8,128)}) custom-call(f32[192,256]{1,0:T(8,128)S(1)} %shard_map.84.base_ref, f32[192,256]{1,0:T(8,128)S(1)} %get-tuple-element.49.field_ref, bf16[240,256]{1,0:T(8,128)(2,1)S(1)} %collective-permute-done.low_ref, bf16[240,256]{1,0:T(8,128)(2,1)S(1)} %collective-permute-done.1.high_ref, ...), custom_call_target="tpu_custom_call" | custom-call | tf_op jit(solution)/shard_map/pallas_call | solution.py:563
Async XLA Ops:
  1.9 12.6 %collective-permute-start = (bf16[240,256]{1,0:T(8,128)(2,1)S(1)}, bf16[240,256]{1,0:T(8,128)(2,1)S(1)}, u32[]{:S(2)}, u32[]{:S(2)}) collective-permute-start(bf16[240,256]{1,0:T(8,128)(2,1)S(1)} %get-tuple-element.36), channel_id=1, source_target_pairs={{0,1},{1,2},{2,3},{3,4},{4,5},{5,6},{6,7},{7,8},{8,9},{9,10},{10,1... | collective-permute-start | bytes 368648 | tf_op jit(solution)/shard_map/ppermute | solution.py:506
  6.4 10.4 %collective-permute-start.1 = (bf16[240,256]{1,0:T(8,128)(2,1)S(1)}, bf16[240,256]{1,0:T(8,128)(2,1)S(1)}, u32[]{:S(2)}, u32[]{:S(2)}) collective-permute-start(bf16[240,256]{1,0:T(8,128)(2,1)S(1)} %get-tuple-element.39), channel_id=1, source_target_pairs={{0,15},{1,0},{2,1},{3,2},{4,3},{5,4},{6,5},{7,6},{8,7},{9,8},{10,9... | collective-permute-start | bytes 368648 | tf_op jit(solution)/shard_map/ppermute | solution.py:506
  14.5 25.7 %copy-start.1 = (bf16[512,512]{1,0:T(8,128)(2,1)S(1)}, bf16[512,512]{1,0:T(8,128)(2,1)}, u32[]{:S(2)}) copy-start(bf16[512,512]{1,0:T(8,128)(2,1)} %second_ref.1) | copy-start | bytes 1572868
  15.3 24.8 %copy-start = (bf16[512,512]{1,0:T(8,128)(2,1)S(1)}, bf16[512,512]{1,0:T(8,128)(2,1)}, u32[]{:S(2)}) copy-start(bf16[512,512]{1,0:T(8,128)(2,1)} %first_ref.1) | copy-start | bytes 1572868
  55.5 12.4 %collective-permute-start.2 = (bf16[96,256]{1,0:T(8,128)(2,1)S(1)}, bf16[96,256]{1,0:T(8,128)(2,1)S(1)}, u32[]{:S(2)}, u32[]{:S(2)}) collective-permute-start(bf16[96,256]{1,0:T(8,128)(2,1)S(1)} %get-tuple-element.54), channel_id=1, source_target_pairs={{0,1},{1,0},{2,3},{3,2},{4,5},{5,4},{6,7},{7,6},{8,9},{9,8},{10,11... | collective-permute-start | bytes 147464 | tf_op jit(solution)/shard_map/ppermute | solution.py:501
  61.1 10.7 %collective-permute-start.3 = (bf16[96,256]{1,0:T(8,128)(2,1)S(1)}, bf16[96,256]{1,0:T(8,128)(2,1)S(1)}, u32[]{:S(2)}, u32[]{:S(2)}) collective-permute-start(bf16[96,256]{1,0:T(8,128)(2,1)S(1)} %get-tuple-element.55), channel_id=1, source_target_pairs={{0,15},{1,2},{2,1},{3,4},{4,3},{5,6},{6,5},{7,8},{8,7},{9,10},{10,... | collective-permute-start | bytes 147464 | tf_op jit(solution)/shard_map/ppermute | solution.py:501

commit v8 on v4

--- a/solution.py
+++ b/solution.py
@@ -385,14 +385,15 @@
             total = part_ref[base : base + 16] + unpack(wall_ref, False, a, z)
             tend_ref[base : base + 16] = total
             next_ref[base : base + 16] = field_ref[base : base + 16] + C1 * total
-    split_table(next_ref[...], table_ref)
+    table_ref[...] = next_ref[...].astype(BF16)
     ends = ((low_ref, come_low_ref, down_ref, 0, 24), (high_ref, come_high_ref, up_ref, 3, 0))
     for ref, come_ref, out_ref, z, at in ends:
         row, _ = tail_cells(tail_of(ref), 4)
         seen = gather(table_ref[...], row, come_ref)
         lines = [plane(next_ref, a, z) for a in range(3)]
         lines.append(slots_ref[at : at + 24])
-        lines += [jnp.concatenate(hi_lo(seen[a]), axis=1) for a in range(3)]
+        lines += [jnp.concatenate(seen[0:2], axis=1), jnp.concatenate([seen[2], jnp.zeros((8, 128), F32)], axis=1)]
+        lines.append(jnp.zeros((8, 256), F32))
         out_ref[...] = jnp.concatenate(lines, axis=0).astype(BF16)
 
 
@@ -446,16 +447,14 @@
 
 def high_second(base_ref, field_ref, high_ref, low2_ref, high2_ref, late_ref, put_ref, come_ref,
                 out_ref, bubble_ref, load_ref):
+    push = late_push(high_ref, high2_ref, field_ref, come_ref, load_ref)
     returned = jnp.concatenate(
-        [jnp.concatenate([ref[72 + a * 8 : 80 + a * 8, :].astype(F32) for ref in (high2_ref, low2_ref)], axis=0)
-         for a in range(3)],
+        [jnp.concatenate([ref[at : at + 8, :].astype(F32) for ref in (high2_ref, low2_ref)], axis=0) for at in (72, 80)],
         axis=1,
     )
     back = jnp.dot(put_ref[...].astype(BF16), returned.astype(BF16), preferred_element_type=F32)
     for a in range(3):
-        seen = back[:, a * 256 : a * 256 + 128] + back[:, a * 256 + 128 : a * 256 + 256]
-        bubble_ref[a] = late_ref[a] + (C2 / relax_time) * seen
-    push = late_push(high_ref, high2_ref, field_ref, come_ref, load_ref)
+        bubble_ref[a] = late_ref[a] + (C2 / relax_time) * back[:, a * 128 : (a + 1) * 128]
     for a in range(3):
         for z in range(4):
             base = (a * 4 + z) * 16
@@ -516,7 +515,7 @@
     (walls,) = call(columns_body, (packed,))(columns, first_deriv, second_deriv)
     walls = exchange(walls)
     lasts = ((LAST_ROWS, 256), BF16)
-    middle, tend, up, down = call(middle_body, (block, block, lasts, lasts), (table,))(
+    middle, tend, up, down = call(middle_body, (block, block, lasts, lasts), (pltpu.VMEM((FIELD_ROWS, 256), BF16),))(
         walls, field, part, low, high, slots, come_low, come_high
     )
     low2, high2 = shifted(up, 1), shifted(down, -1)

time: 70.5 us -> 70.3 us (level)
  no operation moved by 1% of the time
where the time goes in v8:
time: 70.3 us; the launch traced here: 70 us
  blocking collectives  33.4 us (48%)
  starting transfers between devices  15.7 us (22%)
  waiting for transfers between devices  10.4 us (15%)
  Pallas kernels  9.74 us (14%)
  between operations  0.74 us (1%)
    all_to_all x2, blocking collectives, exchange(): return lax.all_to_all(x, 'px', split_axis=0, concat_axis=0, tiled=True)  33.4 us
    ppermute x4, starting transfers between devices, shifted(): lax.ppermute(x, 'pz', [(i, (i + by) % length) for i in range(length)])  15.7 us
    ppermute x4, waiting for transfers between devices, shifted(): lax.ppermute(x, 'pz', [(i, (i + by) % length) for i in range(length)])  10.4 us
    pallas_call x1, Pallas kernels, on_device(): call(home_second, (block, rows, ((24, 16), F32)), (table, hots, loads))  1.86 us
    pallas_call x1, Pallas kernels, on_device(): call(home_first, (block, rows, ((24, 16), F32), ((16, 24), F32)), (table,...  1.74 us
  transfers between devices with their start and end apart: 4, of which 2 were waited for; matrix products, arithmetic and copies ran while one was open for 0% of the time, Pallas kernels for 7%

profile of v8, /device:TPU:54, one launch (start us, length us, event | category | flops | bytes accessed | tf_op | source)
XLA Modules:
  0.0 70.0 jit_solution(15310276498440703174)
XLA Ops:
  0.6 1.2 %shard_map.77 = (bf16[240,256]{1,0:T(8,128)(2,1)S(1)}, bf16[240,256]{1,0:T(8,128)(2,1)S(1)}, f32[16,256]{1,0:T(8,128)S(1)}, f32[192,256]{1,0:T(8,128)S(1)}, f32[...) custom-call(f32[192,256]{1,0:T(8,128)} %bitcast.2, f32[3,24,128]{2,1,0:T(8,128)} %bubble_hbm.1, ...), custom_call_target="tpu_custom_call" | custom-call | tf_op jit(solution)/shard_map/pallas_call | solution.py:489
  1.9 7.1 %collective-permute-start = (bf16[240,256]{1,0:T(8,128)(2,1)S(1)}, bf16[240,256]{1,0:T(8,128)(2,1)S(1)}, u32[]{:S(2)}, u32[]{:S(2)}) collective-permute-start(bf16[240,256]{1,0:T(8,128)(2,1)S(1)} %get-tuple-element.36), channel_id=1, source_target_pairs={{0,1},{1,2},{2,3},{3,4},{4,5},{5,6},{6,7},{7,8},{8,9},{9,10},{10,1... | collective-permute-start | bytes 368648 | tf_op jit(solution)/shard_map/ppermute | solution.py:469
  8.9 1.9 %collective-permute-start.1 = (bf16[240,256]{1,0:T(8,128)(2,1)S(1)}, bf16[240,256]{1,0:T(8,128)(2,1)S(1)}, u32[]{:S(2)}, u32[]{:S(2)}) collective-permute-start(bf16[240,256]{1,0:T(8,128)(2,1)S(1)} %get-tuple-element.39), channel_id=1, source_target_pairs={{0,15},{1,0},{2,1},{3,2},{4,3},{5,4},{6,5},{7,6},{8,7},{9,8},{10,9... | collective-permute-start | bytes 368648 | tf_op jit(solution)/shard_map/ppermute | solution.py:469
  10.9 1.7 %shard_map.78 = (f32[192,256]{1,0:T(8,128)S(1)}, f32[3,24,128]{2,1,0:T(8,128)S(1)}, f32[24,16]{1,0:T(8,128)S(1)}, f32[16,24]{1,0:T(8,128)S(1)}) custom-call(f32[192,256]{1,0:T(8,128)S(1)} %get-tuple-element.31.field_ref, f32[3,24,128]{2,1,0:T(8,128)S(1)} %get-tuple-element.32.bubble_ref, s32[2,24,128]{2,1,0:T(8,128)S(1)} %get-tuple-element.33.owner_ref, ...), custom_call_target="tpu_custom_call" | custom-call | tf_op jit(solution)/shard_map/pallas_call | solution.py:504
  12.6 0.0 collective-permute-done.low_ref
  12.6 0.0 copy-start.1
  12.6 0.9 %shard_map.79 = (f32[192,256]{1,0:T(8,128)S(1)}, f32[3,8,128]{2,1,0:T(8,128)S(1)}, bf16[256,1024]{1,0:T(8,128)(2,1)S(1)}) custom-call(f32[192,256]{1,0:T(8,128)S(1)} %get-tuple-element.31.field_ref, f32[192,256]{1,0:T(8,128)S(1)} %get-tuple-element.35.part_ref, bf16[240,256]{1,0:T(8,128)(2,1)S(1)} %collective-permute-done.low_ref, ...), custom_call_target="tpu_custom_call" | custom-call | tf_op jit(solution)/shard_map/pallas_call | solution.py:508
  13.5 0.0 copy-start
  13.5 6.4 %collective-permute-done.1.high_ref = bf16[240,256]{1,0:T(8,128)(2,1)S(1)} collective-permute-done((bf16[240,256]{1,0:T(8,128)(2,1)S(1)}, bf16[240,256]{1,0:T(8,128)(2,1)S(1)}, u32[]{:S(2)}, u32[]{:S(2)}) %collective-permute-start.1) | collective-permute-done | bytes 122912 | tf_op jit(solution)/shard_map/ppermute | solution.py:469
  19.9 1.0 %shard_map.80 = (f32[192,256]{1,0:T(8,128)S(1)}, bf16[32,24,128]{2,1,0:T(8,128)(2,1)S(1)}, f32[3,24,128]{2,1,0:T(8,128)S(1)}, f32[3,24,128]{2,1,0:T(8,128)S(1)},...) custom-call(f32[192,256]{1,0:T(8,128)S(1)} %get-tuple-element.31.field_ref, ...), custom_call_target="tpu_custom_call" | custom-call | tf_op jit(solution)/shard_map/pallas_call | solution.py:511
  20.9 19.5 %all_to_all.10.got_ref = bf16[32,24,128]{2,1,0:T(8,128)(2,1)S(1)} all-to-all(bf16[32,24,128]{2,1,0:T(8,128)(2,1)S(1)} %get-tuple-element.44), channel_id=1, replica_groups=mesh['px'=32,'pz'=16] {'px'}, dimensions={0} | all-to-all | bytes 393216 | tf_op jit(solution)/shard_map/all_to_all | solution.py:473
  40.4 0.0 copy-done.1
  40.4 0.0 copy-done
  40.4 0.9 %shard_map.81 = bf16[32,24,128]{2,1,0:T(8,128)(2,1)S(1)} custom-call(bf16[32,24,128]{2,1,0:T(8,128)(2,1)S(1)} %all_to_all.10.got_ref, bf16[512,512]{1,0:T(8,128)(2,1)S(1)} %copy-done, bf16[512,512]{1,0:T(8,128)(2,1)S(1)} %copy-done.1), custom_call_target="tpu_custom_call" | custom-call | tf_op jit(solution)/shard_map/pallas_call | solution.py:515
  41.3 13.9 %all_to_all.11.wall_ref = bf16[32,24,128]{2,1,0:T(8,128)(2,1)S(1)} all-to-all(bf16[32,24,128]{2,1,0:T(8,128)(2,1)S(1)} %shard_map.81), channel_id=1, replica_groups=mesh['px'=32,'pz'=16] {'px'}, dimensions={0} | all-to-all | bytes 393216 | tf_op jit(solution)/shard_map/all_to_all | solution.py:473
  55.2 0.5 shard_map.82
  55.7 1.9 %collective-permute-start.2 = (bf16[96,256]{1,0:T(8,128)(2,1)S(1)}, bf16[96,256]{1,0:T(8,128)(2,1)S(1)}, u32[]{:S(2)}, u32[]{:S(2)}) collective-permute-start(bf16[96,256]{1,0:T(8,128)(2,1)S(1)} %get-tuple-element.54), channel_id=1, source_target_pairs={{0,1},{1,2},{2,3},{3,4},{4,5},{5,6},{6,7},{7,8},{8,9},{9,10},{10,1... | collective-permute-start | bytes 147464 | tf_op jit(solution)/shard_map/ppermute | solution.py:469
  57.6 4.8 %collective-permute-start.3 = (bf16[96,256]{1,0:T(8,128)(2,1)S(1)}, bf16[96,256]{1,0:T(8,128)(2,1)S(1)}, u32[]{:S(2)}, u32[]{:S(2)}) collective-permute-start(bf16[96,256]{1,0:T(8,128)(2,1)S(1)} %get-tuple-element.55), channel_id=1, source_target_pairs={{0,15},{1,0},{2,1},{3,2},{4,3},{5,4},{6,5},{7,6},{8,7},{9,8},{10,9... | collective-permute-start | bytes 147464 | tf_op jit(solution)/shard_map/ppermute | solution.py:469
  62.5 1.9 %shard_map.83 = (f32[192,256]{1,0:T(8,128)S(1)}, f32[3,24,128]{2,1,0:T(8,128)S(1)}, f32[24,16]{1,0:T(8,128)S(1)}) custom-call(bf16[32,24,128]{2,1,0:T(8,128)(2,1)S(1)} %all_to_all.11.wall_ref, f32[192,256]{1,0:T(8,128)S(1)} %get-tuple-element.49.field_ref, f32[192,256]{1,0:T(8,128)S(1)} %get-tuple-element.50.tend_ref, ...), custom_call_target="tpu_custom_call" | custom-call | tf_op jit(solution)/shard_map/pallas_call | solution.py:522
  64.3 0.0 collective-permute-done.2.low2_ref
  64.4 0.5 shard_map.84.base_ref
  64.9 4.0 %collective-permute-done.3.high2_ref = bf16[96,256]{1,0:T(8,128)(2,1)S(1)} collective-permute-done((bf16[96,256]{1,0:T(8,128)(2,1)S(1)}, bf16[96,256]{1,0:T(8,128)(2,1)S(1)}, u32[]{:S(2)}, u32[]{:S(2)}) %collective-permute-start.3) | collective-permute-done | bytes 49184 | tf_op jit(solution)/shard_map/ppermute | solution.py:469
  68.9 1.2 %shard_map.85 = (f32[192,256]{1,0:T(8,128)}, f32[3,24,128]{2,1,0:T(8,128)}) custom-call(f32[192,256]{1,0:T(8,128)S(1)} %shard_map.84.base_ref, f32[192,256]{1,0:T(8,128)S(1)} %get-tuple-element.49.field_ref, bf16[240,256]{1,0:T(8,128)(2,1)S(1)} %collective-permute-done.1.high_ref, bf16[96,256]{1,0:T(8,128)(2,1)S(1)} %collective-permute-done.2.low2_ref, ...), custom_call_target="tpu_custom_call" | custom-call | tf_op jit(solution)/shard_map/pallas_call | solution.py:526
Async XLA Ops:
  1.9 10.8 %collective-permute-start = (bf16[240,256]{1,0:T(8,128)(2,1)S(1)}, bf16[240,256]{1,0:T(8,128)(2,1)S(1)}, u32[]{:S(2)}, u32[]{:S(2)}) collective-permute-start(bf16[240,256]{1,0:T(8,128)(2,1)S(1)} %get-tuple-element.36), channel_id=1, source_target_pairs={{0,1},{1,2},{2,3},{3,4},{4,5},{5,6},{6,7},{7,8},{8,9},{9,10},{10,1... | collective-permute-start | bytes 368648 | tf_op jit(solution)/shard_map/ppermute | solution.py:469
  8.9 11.0 %collective-permute-start.1 = (bf16[240,256]{1,0:T(8,128)(2,1)S(1)}, bf16[240,256]{1,0:T(8,128)(2,1)S(1)}, u32[]{:S(2)}, u32[]{:S(2)}) collective-permute-start(bf16[240,256]{1,0:T(8,128)(2,1)S(1)} %get-tuple-element.39), channel_id=1, source_target_pairs={{0,15},{1,0},{2,1},{3,2},{4,3},{5,4},{6,5},{7,6},{8,7},{9,8},{10,9... | collective-permute-start | bytes 368648 | tf_op jit(solution)/shard_map/ppermute | solution.py:469
  12.6 27.8 %copy-start.1 = (bf16[512,512]{1,0:T(8,128)(2,1)S(1)}, bf16[512,512]{1,0:T(8,128)(2,1)}, u32[]{:S(2)}) copy-start(bf16[512,512]{1,0:T(8,128)(2,1)} %second_ref.1) | copy-start | bytes 1572868
  13.5 26.9 %copy-start = (bf16[512,512]{1,0:T(8,128)(2,1)S(1)}, bf16[512,512]{1,0:T(8,128)(2,1)}, u32[]{:S(2)}) copy-start(bf16[512,512]{1,0:T(8,128)(2,1)} %first_ref.1) | copy-start | bytes 1572868
  55.7 8.6 %collective-permute-start.2 = (bf16[96,256]{1,0:T(8,128)(2,1)S(1)}, bf16[96,256]{1,0:T(8,128)(2,1)S(1)}, u32[]{:S(2)}, u32[]{:S(2)}) collective-permute-start(bf16[96,256]{1,0:T(8,128)(2,1)S(1)} %get-tuple-element.54), channel_id=1, source_target_pairs={{0,1},{1,2},{2,3},{3,4},{4,5},{5,6},{6,7},{7,8},{8,9},{9,10},{10,1... | collective-permute-start | bytes 147464 | tf_op jit(solution)/shard_map/ppermute | solution.py:469
  57.6 11.2 %collective-permute-start.3 = (bf16[96,256]{1,0:T(8,128)(2,1)S(1)}, bf16[96,256]{1,0:T(8,128)(2,1)S(1)}, u32[]{:S(2)}, u32[]{:S(2)}) collective-permute-start(bf16[96,256]{1,0:T(8,128)(2,1)S(1)} %get-tuple-element.55), channel_id=1, source_target_pairs={{0,15},{1,0},{2,1},{3,2},{4,3},{5,4},{6,5},{7,6},{8,7},{9,8},{10,9... | collective-permute-start | bytes 147464 | tf_op jit(solution)/shard_map/ppermute | solution.py:469

commit v9 on v8

--- a/solution.py
+++ b/solution.py
@@ -24,8 +24,8 @@
 
 ROWS_A = 64
 FIELD_ROWS = 192
-SEND_ROWS = 240
-LAST_ROWS = 96
+SEND_ROWS = 232
+LAST_ROWS = 88
 
 
 def iota(shape, dim):
@@ -200,7 +200,7 @@
     moved_ref[...] = picked[:, 768:1024]
     for ref, at in ((up_ref, 0), (down_ref, 8)):
         lines = [picked[at : at + 8, i * 256 : (i + 1) * 256] for i in range(4)]
-        lines += [later[at : at + 8], jnp.zeros((8, 256), F32)]
+        lines.append(later[at : at + 8])
         ref[FIELD_ROWS:SEND_ROWS] = jnp.concatenate(lines, axis=0).astype(BF16)
     copies[3].wait()
     block = field_ref[...].astype(BF16)
@@ -286,7 +286,7 @@
 
 def arrived(cells_ref, values_ref, first_line, cell_line, load_ref):
     row, col = tail_cells(tail_of(cells_ref), cell_line)
-    tail = values_ref[first_line : first_line + 48, :].astype(F32)
+    tail = values_ref[first_line : first_line + 40, :].astype(F32)
     highs = [tail[a * 8 : a * 8 + 8, 0:128] for a in range(3)]
     lows = [tail[a * 8 : a * 8 + 8, 128:256] for a in range(3)]
     fill_values(row, highs, lows, load_ref)
@@ -393,7 +393,6 @@
         lines = [plane(next_ref, a, z) for a in range(3)]
         lines.append(slots_ref[at : at + 24])
         lines += [jnp.concatenate(seen[0:2], axis=1), jnp.concatenate([seen[2], jnp.zeros((8, 128), F32)], axis=1)]
-        lines.append(jnp.zeros((8, 256), F32))
         out_ref[...] = jnp.concatenate(lines, axis=0).astype(BF16)
 
 

time: 70.3 us -> 70 us (level)
  the two profiles are of different devices: /device:TPU:54 before, /device:TPU:62 now
where the time goes in v9:
time: 70 us; the launch traced here: 69.7 us
  blocking collectives  36.3 us (52%)
  starting transfers between devices  13.5 us (19%)
  Pallas kernels  9.82 us (14%)
  waiting for transfers between devices  9.37 us (13%)
  between operations  0.73 us (1%)
    all_to_all x2, blocking collectives, exchange(): return lax.all_to_all(x, 'px', split_axis=0, concat_axis=0, tiled=True)  36.3 us
    ppermute x4, starting transfers between devices, shifted(): lax.ppermute(x, 'pz', [(i, (i + by) % length) for i in range(length)])  13.5 us
    ppermute x4, waiting for transfers between devices, shifted(): lax.ppermute(x, 'pz', [(i, (i + by) % length) for i in range(length)])  9.37 us
    pallas_call x1, Pallas kernels, on_device(): call(home_second, (block, rows, ((24, 16), F32)), (table, hots, loads))  1.9 us
    pallas_call x1, Pallas kernels, on_device(): call(home_first, (block, rows, ((24, 16), F32), ((16, 24), F32)), (table,...  1.76 us
  transfers between devices with their start and end apart: 4, of which 3 were waited for; matrix products, arithmetic and copies ran while one was open for 0% of the time, Pallas kernels for 7%

profile of v9, /device:TPU:62, one launch (start us, length us, event | category | flops | bytes accessed | tf_op | source)
XLA Modules:
  0.0 69.7 jit_solution(17987038275173811181)
XLA Ops:
  0.6 1.2 %shard_map.77 = (bf16[232,256]{1,0:T(8,128)(2,1)S(1)}, bf16[232,256]{1,0:T(8,128)(2,1)S(1)}, f32[16,256]{1,0:T(8,128)S(1)}, f32[192,256]{1,0:T(8,128)S(1)}, f32[...) custom-call(f32[192,256]{1,0:T(8,128)} %bitcast.2, f32[3,24,128]{2,1,0:T(8,128)} %bubble_hbm.1, ...), custom_call_target="tpu_custom_call" | custom-call | tf_op jit(solution)/shard_map/pallas_call | solution.py:488
  1.9 2.6 %collective-permute-start = (bf16[232,256]{1,0:T(8,128)(2,1)S(1)}, bf16[232,256]{1,0:T(8,128)(2,1)S(1)}, u32[]{:S(2)}, u32[]{:S(2)}) collective-permute-start(bf16[232,256]{1,0:T(8,128)(2,1)S(1)} %get-tuple-element.36), channel_id=1, source_target_pairs={{0,1},{1,2},{2,3},{3,4},{4,5},{5,6},{6,7},{7,8},{8,9},{9,10},{10,1... | collective-permute-start | bytes 356360 | tf_op jit(solution)/shard_map/ppermute | solution.py:468
  4.5 4.1 %collective-permute-start.1 = (bf16[232,256]{1,0:T(8,128)(2,1)S(1)}, bf16[232,256]{1,0:T(8,128)(2,1)S(1)}, u32[]{:S(2)}, u32[]{:S(2)}) collective-permute-start(bf16[232,256]{1,0:T(8,128)(2,1)S(1)} %get-tuple-element.39), channel_id=1, source_target_pairs={{0,15},{1,0},{2,1},{3,2},{4,3},{5,4},{6,5},{7,6},{8,7},{9,8},{10,9... | collective-permute-start | bytes 356360 | tf_op jit(solution)/shard_map/ppermute | solution.py:468
  8.6 1.8 %shard_map.78 = (f32[192,256]{1,0:T(8,128)S(1)}, f32[3,24,128]{2,1,0:T(8,128)S(1)}, f32[24,16]{1,0:T(8,128)S(1)}, f32[16,24]{1,0:T(8,128)S(1)}) custom-call(f32[192,256]{1,0:T(8,128)S(1)} %get-tuple-element.31.field_ref, f32[3,24,128]{2,1,0:T(8,128)S(1)} %get-tuple-element.32.bubble_ref, s32[2,24,128]{2,1,0:T(8,128)S(1)} %get-tuple-element.33.owner_ref, ...), custom_call_target="tpu_custom_call" | custom-call | tf_op jit(solution)/shard_map/pallas_call | solution.py:503
  10.4 1.8 %collective-permute-done.low_ref = bf16[232,256]{1,0:T(8,128)(2,1)S(1)} collective-permute-done((bf16[232,256]{1,0:T(8,128)(2,1)S(1)}, bf16[232,256]{1,0:T(8,128)(2,1)S(1)}, u32[]{:S(2)}, u32[]{:S(2)}) %collective-permute-start) | collective-permute-done | bytes 118816 | tf_op jit(solution)/shard_map/ppermute | solution.py:468
  12.2 0.0 copy-start.1
  12.2 0.9 %shard_map.79 = (f32[192,256]{1,0:T(8,128)S(1)}, f32[3,8,128]{2,1,0:T(8,128)S(1)}, bf16[256,1024]{1,0:T(8,128)(2,1)S(1)}) custom-call(f32[192,256]{1,0:T(8,128)S(1)} %get-tuple-element.31.field_ref, f32[192,256]{1,0:T(8,128)S(1)} %get-tuple-element.35.part_ref, bf16[232,256]{1,0:T(8,128)(2,1)S(1)} %collective-permute-done.low_ref, ...), custom_call_target="tpu_custom_call" | custom-call | tf_op jit(solution)/shard_map/pallas_call | solution.py:507
  13.1 0.0 copy-start
  13.1 4.6 %collective-permute-done.1.high_ref = bf16[232,256]{1,0:T(8,128)(2,1)S(1)} collective-permute-done((bf16[232,256]{1,0:T(8,128)(2,1)S(1)}, bf16[232,256]{1,0:T(8,128)(2,1)S(1)}, u32[]{:S(2)}, u32[]{:S(2)}) %collective-permute-start.1) | collective-permute-done | bytes 118816 | tf_op jit(solution)/shard_map/ppermute | solution.py:468
  17.7 1.0 %shard_map.80 = (f32[192,256]{1,0:T(8,128)S(1)}, bf16[32,24,128]{2,1,0:T(8,128)(2,1)S(1)}, f32[3,24,128]{2,1,0:T(8,128)S(1)}, f32[3,24,128]{2,1,0:T(8,128)S(1)},...) custom-call(f32[192,256]{1,0:T(8,128)S(1)} %get-tuple-element.31.field_ref, ...), custom_call_target="tpu_custom_call" | custom-call | tf_op jit(solution)/shard_map/pallas_call | solution.py:510
  18.7 22.3 %all_to_all.10.got_ref = bf16[32,24,128]{2,1,0:T(8,128)(2,1)S(1)} all-to-all(bf16[32,24,128]{2,1,0:T(8,128)(2,1)S(1)} %get-tuple-element.44), channel_id=1, replica_groups=mesh['px'=32,'pz'=16] {'px'}, dimensions={0} | all-to-all | bytes 393216 | tf_op jit(solution)/shard_map/all_to_all | solution.py:472
  41.1 0.0 copy-done.1
  41.1 0.0 copy-done
  41.1 0.9 %shard_map.81 = bf16[32,24,128]{2,1,0:T(8,128)(2,1)S(1)} custom-call(bf16[32,24,128]{2,1,0:T(8,128)(2,1)S(1)} %all_to_all.10.got_ref, bf16[512,512]{1,0:T(8,128)(2,1)S(1)} %copy-done, bf16[512,512]{1,0:T(8,128)(2,1)S(1)} %copy-done.1), custom_call_target="tpu_custom_call" | custom-call | tf_op jit(solution)/shard_map/pallas_call | solution.py:514
  42.0 13.9 %all_to_all.11.wall_ref = bf16[32,24,128]{2,1,0:T(8,128)(2,1)S(1)} all-to-all(bf16[32,24,128]{2,1,0:T(8,128)(2,1)S(1)} %shard_map.81), channel_id=1, replica_groups=mesh['px'=32,'pz'=16] {'px'}, dimensions={0} | all-to-all | bytes 393216 | tf_op jit(solution)/shard_map/all_to_all | solution.py:472
  55.9 0.5 shard_map.82
  56.4 1.9 %collective-permute-start.2 = (bf16[88,256]{1,0:T(8,128)(2,1)S(1)}, bf16[88,256]{1,0:T(8,128)(2,1)S(1)}, u32[]{:S(2)}, u32[]{:S(2)}) collective-permute-start(bf16[88,256]{1,0:T(8,128)(2,1)S(1)} %get-tuple-element.54), channel_id=1, source_target_pairs={{0,1},{1,2},{2,3},{3,4},{4,5},{5,6},{6,7},{7,8},{8,9},{9,10},{10,1... | collective-permute-start | bytes 135176 | tf_op jit(solution)/shard_map/ppermute | solution.py:468
  58.3 4.8 %collective-permute-start.3 = (bf16[88,256]{1,0:T(8,128)(2,1)S(1)}, bf16[88,256]{1,0:T(8,128)(2,1)S(1)}, u32[]{:S(2)}, u32[]{:S(2)}) collective-permute-start(bf16[88,256]{1,0:T(8,128)(2,1)S(1)} %get-tuple-element.55), channel_id=1, source_target_pairs={{0,15},{1,0},{2,1},{3,2},{4,3},{5,4},{6,5},{7,6},{8,7},{9,8},{10,9... | collective-permute-start | bytes 135176 | tf_op jit(solution)/shard_map/ppermute | solution.py:468
  63.2 1.9 %shard_map.83 = (f32[192,256]{1,0:T(8,128)S(1)}, f32[3,24,128]{2,1,0:T(8,128)S(1)}, f32[24,16]{1,0:T(8,128)S(1)}) custom-call(bf16[32,24,128]{2,1,0:T(8,128)(2,1)S(1)} %all_to_all.11.wall_ref, f32[192,256]{1,0:T(8,128)S(1)} %get-tuple-element.49.field_ref, f32[192,256]{1,0:T(8,128)S(1)} %get-tuple-element.50.tend_ref, ...), custom_call_target="tpu_custom_call" | custom-call | tf_op jit(solution)/shard_map/pallas_call | solution.py:521
  65.1 0.0 collective-permute-done.2.low2_ref
  65.1 0.5 shard_map.84.base_ref
  65.6 2.9 %collective-permute-done.3.high2_ref = bf16[88,256]{1,0:T(8,128)(2,1)S(1)} collective-permute-done((bf16[88,256]{1,0:T(8,128)(2,1)S(1)}, bf16[88,256]{1,0:T(8,128)(2,1)S(1)}, u32[]{:S(2)}, u32[]{:S(2)}) %collective-permute-start.3) | collective-permute-done | bytes 45088 | tf_op jit(solution)/shard_map/ppermute | solution.py:468
  68.5 1.2 %shard_map.85 = (f32[192,256]{1,0:T(8,128)}, f32[3,24,128]{2,1,0:T(8,128)}) custom-call(f32[192,256]{1,0:T(8,128)S(1)} %shard_map.84.base_ref, f32[192,256]{1,0:T(8,128)S(1)} %get-tuple-element.49.field_ref, bf16[232,256]{1,0:T(8,128)(2,1)S(1)} %collective-permute-done.1.high_ref, bf16[88,256]{1,0:T(8,128)(2,1)S(1)} %collective-permute-done.2.low2_ref, ...), custom_call_target="tpu_custom_call" | custom-call | tf_op jit(solution)/shard_map/pallas_call | solution.py:525
Async XLA Ops:
  1.9 10.3 %collective-permute-start = (bf16[232,256]{1,0:T(8,128)(2,1)S(1)}, bf16[232,256]{1,0:T(8,128)(2,1)S(1)}, u32[]{:S(2)}, u32[]{:S(2)}) collective-permute-start(bf16[232,256]{1,0:T(8,128)(2,1)S(1)} %get-tuple-element.36), channel_id=1, source_target_pairs={{0,1},{1,2},{2,3},{3,4},{4,5},{5,6},{6,7},{7,8},{8,9},{9,10},{10,1... | collective-permute-start | bytes 356360 | tf_op jit(solution)/shard_map/ppermute | solution.py:468
  4.5 13.3 %collective-permute-start.1 = (bf16[232,256]{1,0:T(8,128)(2,1)S(1)}, bf16[232,256]{1,0:T(8,128)(2,1)S(1)}, u32[]{:S(2)}, u32[]{:S(2)}) collective-permute-start(bf16[232,256]{1,0:T(8,128)(2,1)S(1)} %get-tuple-element.39), channel_id=1, source_target_pairs={{0,15},{1,0},{2,1},{3,2},{4,3},{5,4},{6,5},{7,6},{8,7},{9,8},{10,9... | collective-permute-start | bytes 356360 | tf_op jit(solution)/shard_map/ppermute | solution.py:468
  12.2 28.9 %copy-start.1 = (bf16[512,512]{1,0:T(8,128)(2,1)S(1)}, bf16[512,512]{1,0:T(8,128)(2,1)}, u32[]{:S(2)}) copy-start(bf16[512,512]{1,0:T(8,128)(2,1)} %second_ref.1) | copy-start | bytes 1572868
  13.1 28.0 %copy-start = (bf16[512,512]{1,0:T(8,128)(2,1)S(1)}, bf16[512,512]{1,0:T(8,128)(2,1)}, u32[]{:S(2)}) copy-start(bf16[512,512]{1,0:T(8,128)(2,1)} %first_ref.1) | copy-start | bytes 1572868
  56.4 8.7 %collective-permute-start.2 = (bf16[88,256]{1,0:T(8,128)(2,1)S(1)}, bf16[88,256]{1,0:T(8,128)(2,1)S(1)}, u32[]{:S(2)}, u32[]{:S(2)}) collective-permute-start(bf16[88,256]{1,0:T(8,128)(2,1)S(1)} %get-tuple-element.54), channel_id=1, source_target_pairs={{0,1},{1,2},{2,3},{3,4},{4,5},{5,6},{6,7},{7,8},{8,9},{9,10},{10,1... | collective-permute-start | bytes 135176 | tf_op jit(solution)/shard_map/ppermute | solution.py:468
  58.3 10.2 %collective-permute-start.3 = (bf16[88,256]{1,0:T(8,128)(2,1)S(1)}, bf16[88,256]{1,0:T(8,128)(2,1)S(1)}, u32[]{:S(2)}, u32[]{:S(2)}) collective-permute-start(bf16[88,256]{1,0:T(8,128)(2,1)S(1)} %get-tuple-element.55), channel_id=1, source_target_pairs={{0,15},{1,0},{2,1},{3,2},{4,3},{5,4},{6,5},{7,6},{8,7},{9,8},{10,9... | collective-permute-start | bytes 135176 | tf_op jit(solution)/shard_map/ppermute | solution.py:468

commit v10 on v9

--- a/solution.py
+++ b/solution.py
@@ -399,7 +399,7 @@
 def home_second(wall_ref, field_ref, tend_ref, bubble_ref, rate_ref, owner_ref, dest_ref,
                 base_ref, late_ref, put_ref, table_ref, hot_ref, load_ref):
     field = field_ref[...]
-    split_table(field, table_ref)
+    table_ref[0:FIELD_ROWS] = field.astype(BF16)
     put_ref[...] = put_matrix(dest_ref[1:2])
     row, col = home_cells(owner_ref[1], dest_ref[1:2])
 
@@ -412,7 +412,7 @@
         fill_values(row[rows], [p[0] for p in pairs], [p[1] for p in pairs], load)
         got = scatter(load_ref.at[i], hot_ref.at[i])
         sums = got if sums is None else sums + got
-        seen = gather(table_ref[...], row[rows], hot_ref.at[i])
+        seen = gather(table_ref[0:FIELD_ROWS], row[rows], hot_ref.at[i])
         for a in range(3):
             here = bubble_ref[a, rows]
             rate = (seen[a] - here) / relax_time

time: 70 us -> 70 us (level)
  no operation moved by 1% of the time
where the time goes in v10:
time: 70 us; the launch traced here: 69.7 us
  blocking collectives  36.3 us (52%)
  starting transfers between devices  13.5 us (19%)
  Pallas kernels  9.67 us (14%)
  waiting for transfers between devices  9.52 us (14%)
  between operations  0.73 us (1%)
    all_to_all x2, blocking collectives, exchange(): return lax.all_to_all(x, 'px', split_axis=0, concat_axis=0, tiled=True)  36.3 us
    ppermute x4, starting transfers between devices, shifted(): lax.ppermute(x, 'pz', [(i, (i + by) % length) for i in range(length)])  13.5 us
    ppermute x4, waiting for transfers between devices, shifted(): lax.ppermute(x, 'pz', [(i, (i + by) % length) for i in range(length)])  9.52 us
    pallas_call x1, Pallas kernels, on_device(): call(home_first, (block, rows, ((24, 16), F32), ((16, 24), F32)), (table,...  1.76 us
    pallas_call x1, Pallas kernels, on_device(): call(home_second, (block, rows, ((24, 16), F32)), (table, hots, loads))  1.75 us
  transfers between devices with their start and end apart: 4, of which 3 were waited for; matrix products, arithmetic and copies ran while one was open for 0% of the time, Pallas kernels for 7%

profile of v10, /device:TPU:62, one launch (start us, length us, event | category | flops | bytes accessed | tf_op | source)
XLA Modules:
  0.0 69.7 jit_solution(18075869095334538715)
XLA Ops:
  0.6 1.2 %shard_map.77 = (bf16[232,256]{1,0:T(8,128)(2,1)S(1)}, bf16[232,256]{1,0:T(8,128)(2,1)S(1)}, f32[16,256]{1,0:T(8,128)S(1)}, f32[192,256]{1,0:T(8,128)S(1)}, f32[...) custom-call(f32[192,256]{1,0:T(8,128)} %bitcast.2, f32[3,24,128]{2,1,0:T(8,128)} %bubble_hbm.1, ...), custom_call_target="tpu_custom_call" | custom-call | tf_op jit(solution)/shard_map/pallas_call | solution.py:488
  1.9 2.6 %collective-permute-start = (bf16[232,256]{1,0:T(8,128)(2,1)S(1)}, bf16[232,256]{1,0:T(8,128)(2,1)S(1)}, u32[]{:S(2)}, u32[]{:S(2)}) collective-permute-start(bf16[232,256]{1,0:T(8,128)(2,1)S(1)} %get-tuple-element.36), channel_id=1, source_target_pairs={{0,1},{1,2},{2,3},{3,4},{4,5},{5,6},{6,7},{7,8},{8,9},{9,10},{10,1... | collective-permute-start | bytes 356360 | tf_op jit(solution)/shard_map/ppermute | solution.py:468
  4.5 4.1 %collective-permute-start.1 = (bf16[232,256]{1,0:T(8,128)(2,1)S(1)}, bf16[232,256]{1,0:T(8,128)(2,1)S(1)}, u32[]{:S(2)}, u32[]{:S(2)}) collective-permute-start(bf16[232,256]{1,0:T(8,128)(2,1)S(1)} %get-tuple-element.39), channel_id=1, source_target_pairs={{0,15},{1,0},{2,1},{3,2},{4,3},{5,4},{6,5},{7,6},{8,7},{9,8},{10,9... | collective-permute-start | bytes 356360 | tf_op jit(solution)/shard_map/ppermute | solution.py:468
  8.6 1.8 %shard_map.78 = (f32[192,256]{1,0:T(8,128)S(1)}, f32[3,24,128]{2,1,0:T(8,128)S(1)}, f32[24,16]{1,0:T(8,128)S(1)}, f32[16,24]{1,0:T(8,128)S(1)}) custom-call(f32[192,256]{1,0:T(8,128)S(1)} %get-tuple-element.31.field_ref, f32[3,24,128]{2,1,0:T(8,128)S(1)} %get-tuple-element.32.bubble_ref, s32[2,24,128]{2,1,0:T(8,128)S(1)} %get-tuple-element.33.owner_ref, ...), custom_call_target="tpu_custom_call" | custom-call | tf_op jit(solution)/shard_map/pallas_call | solution.py:503
  10.4 1.8 %collective-permute-done.low_ref = bf16[232,256]{1,0:T(8,128)(2,1)S(1)} collective-permute-done((bf16[232,256]{1,0:T(8,128)(2,1)S(1)}, bf16[232,256]{1,0:T(8,128)(2,1)S(1)}, u32[]{:S(2)}, u32[]{:S(2)}) %collective-permute-start) | collective-permute-done | bytes 118816 | tf_op jit(solution)/shard_map/ppermute | solution.py:468
  12.2 0.0 copy-start.1
  12.2 0.9 %shard_map.79 = (f32[192,256]{1,0:T(8,128)S(1)}, f32[3,8,128]{2,1,0:T(8,128)S(1)}, bf16[256,1024]{1,0:T(8,128)(2,1)S(1)}) custom-call(f32[192,256]{1,0:T(8,128)S(1)} %get-tuple-element.31.field_ref, f32[192,256]{1,0:T(8,128)S(1)} %get-tuple-element.35.part_ref, bf16[232,256]{1,0:T(8,128)(2,1)S(1)} %collective-permute-done.low_ref, ...), custom_call_target="tpu_custom_call" | custom-call | tf_op jit(solution)/shard_map/pallas_call | solution.py:507
  13.1 0.0 copy-start
  13.1 4.6 %collective-permute-done.1.high_ref = bf16[232,256]{1,0:T(8,128)(2,1)S(1)} collective-permute-done((bf16[232,256]{1,0:T(8,128)(2,1)S(1)}, bf16[232,256]{1,0:T(8,128)(2,1)S(1)}, u32[]{:S(2)}, u32[]{:S(2)}) %collective-permute-start.1) | collective-permute-done | bytes 118816 | tf_op jit(solution)/shard_map/ppermute | solution.py:468
  17.7 1.0 %shard_map.80 = (f32[192,256]{1,0:T(8,128)S(1)}, bf16[32,24,128]{2,1,0:T(8,128)(2,1)S(1)}, f32[3,24,128]{2,1,0:T(8,128)S(1)}, f32[3,24,128]{2,1,0:T(8,128)S(1)},...) custom-call(f32[192,256]{1,0:T(8,128)S(1)} %get-tuple-element.31.field_ref, ...), custom_call_target="tpu_custom_call" | custom-call | tf_op jit(solution)/shard_map/pallas_call | solution.py:510
  18.7 22.3 %all_to_all.10.got_ref = bf16[32,24,128]{2,1,0:T(8,128)(2,1)S(1)} all-to-all(bf16[32,24,128]{2,1,0:T(8,128)(2,1)S(1)} %get-tuple-element.44), channel_id=1, replica_groups=mesh['px'=32,'pz'=16] {'px'}, dimensions={0} | all-to-all | bytes 393216 | tf_op jit(solution)/shard_map/all_to_all | solution.py:472
  41.1 0.0 copy-done.1
  41.1 0.0 copy-done
  41.1 0.9 %shard_map.81 = bf16[32,24,128]{2,1,0:T(8,128)(2,1)S(1)} custom-call(bf16[32,24,128]{2,1,0:T(8,128)(2,1)S(1)} %all_to_all.10.got_ref, bf16[512,512]{1,0:T(8,128)(2,1)S(1)} %copy-done, bf16[512,512]{1,0:T(8,128)(2,1)S(1)} %copy-done.1), custom_call_target="tpu_custom_call" | custom-call | tf_op jit(solution)/shard_map/pallas_call | solution.py:514
  42.0 13.9 %all_to_all.11.wall_ref = bf16[32,24,128]{2,1,0:T(8,128)(2,1)S(1)} all-to-all(bf16[32,24,128]{2,1,0:T(8,128)(2,1)S(1)} %shard_map.81), channel_id=1, replica_groups=mesh['px'=32,'pz'=16] {'px'}, dimensions={0} | all-to-all | bytes 393216 | tf_op jit(solution)/shard_map/all_to_all | solution.py:472
  55.9 0.5 shard_map.82
  56.4 1.9 %collective-permute-start.2 = (bf16[88,256]{1,0:T(8,128)(2,1)S(1)}, bf16[88,256]{1,0:T(8,128)(2,1)S(1)}, u32[]{:S(2)}, u32[]{:S(2)}) collective-permute-start(bf16[88,256]{1,0:T(8,128)(2,1)S(1)} %get-tuple-element.54), channel_id=1, source_target_pairs={{0,1},{1,2},{2,3},{3,4},{4,5},{5,6},{6,7},{7,8},{8,9},{9,10},{10,1... | collective-permute-start | bytes 135176 | tf_op jit(solution)/shard_map/ppermute | solution.py:468
  58.3 4.8 %collective-permute-start.3 = (bf16[88,256]{1,0:T(8,128)(2,1)S(1)}, bf16[88,256]{1,0:T(8,128)(2,1)S(1)}, u32[]{:S(2)}, u32[]{:S(2)}) collective-permute-start(bf16[88,256]{1,0:T(8,128)(2,1)S(1)} %get-tuple-element.55), channel_id=1, source_target_pairs={{0,15},{1,0},{2,1},{3,2},{4,3},{5,4},{6,5},{7,6},{8,7},{9,8},{10,9... | collective-permute-start | bytes 135176 | tf_op jit(solution)/shard_map/ppermute | solution.py:468
  63.2 1.8 %shard_map.83 = (f32[192,256]{1,0:T(8,128)S(1)}, f32[3,24,128]{2,1,0:T(8,128)S(1)}, f32[24,16]{1,0:T(8,128)S(1)}) custom-call(bf16[32,24,128]{2,1,0:T(8,128)(2,1)S(1)} %all_to_all.11.wall_ref, f32[192,256]{1,0:T(8,128)S(1)} %get-tuple-element.49.field_ref, f32[192,256]{1,0:T(8,128)S(1)} %get-tuple-element.50.tend_ref, ...), custom_call_target="tpu_custom_call" | custom-call | tf_op jit(solution)/shard_map/pallas_call | solution.py:521
  64.9 0.0 collective-permute-done.2.low2_ref
  64.9 0.5 shard_map.84.base_ref
  65.4 3.1 %collective-permute-done.3.high2_ref = bf16[88,256]{1,0:T(8,128)(2,1)S(1)} collective-permute-done((bf16[88,256]{1,0:T(8,128)(2,1)S(1)}, bf16[88,256]{1,0:T(8,128)(2,1)S(1)}, u32[]{:S(2)}, u32[]{:S(2)}) %collective-permute-start.3) | collective-permute-done | bytes 45088 | tf_op jit(solution)/shard_map/ppermute | solution.py:468
  68.5 1.2 %shard_map.85 = (f32[192,256]{1,0:T(8,128)}, f32[3,24,128]{2,1,0:T(8,128)}) custom-call(f32[192,256]{1,0:T(8,128)S(1)} %shard_map.84.base_ref, f32[192,256]{1,0:T(8,128)S(1)} %get-tuple-element.49.field_ref, bf16[232,256]{1,0:T(8,128)(2,1)S(1)} %collective-permute-done.1.high_ref, bf16[88,256]{1,0:T(8,128)(2,1)S(1)} %collective-permute-done.2.low2_ref, ...), custom_call_target="tpu_custom_call" | custom-call | tf_op jit(solution)/shard_map/pallas_call | solution.py:525
Async XLA Ops:
  1.9 10.3 %collective-permute-start = (bf16[232,256]{1,0:T(8,128)(2,1)S(1)}, bf16[232,256]{1,0:T(8,128)(2,1)S(1)}, u32[]{:S(2)}, u32[]{:S(2)}) collective-permute-start(bf16[232,256]{1,0:T(8,128)(2,1)S(1)} %get-tuple-element.36), channel_id=1, source_target_pairs={{0,1},{1,2},{2,3},{3,4},{4,5},{5,6},{6,7},{7,8},{8,9},{9,10},{10,1... | collective-permute-start | bytes 356360 | tf_op jit(solution)/shard_map/ppermute | solution.py:468
  4.5 13.3 %collective-permute-start.1 = (bf16[232,256]{1,0:T(8,128)(2,1)S(1)}, bf16[232,256]{1,0:T(8,128)(2,1)S(1)}, u32[]{:S(2)}, u32[]{:S(2)}) collective-permute-start(bf16[232,256]{1,0:T(8,128)(2,1)S(1)} %get-tuple-element.39), channel_id=1, source_target_pairs={{0,15},{1,0},{2,1},{3,2},{4,3},{5,4},{6,5},{7,6},{8,7},{9,8},{10,9... | collective-permute-start | bytes 356360 | tf_op jit(solution)/shard_map/ppermute | solution.py:468
  12.2 28.9 %copy-start.1 = (bf16[512,512]{1,0:T(8,128)(2,1)S(1)}, bf16[512,512]{1,0:T(8,128)(2,1)}, u32[]{:S(2)}) copy-start(bf16[512,512]{1,0:T(8,128)(2,1)} %second_ref.1) | copy-start | bytes 1572868
  13.1 28.0 %copy-start = (bf16[512,512]{1,0:T(8,128)(2,1)S(1)}, bf16[512,512]{1,0:T(8,128)(2,1)}, u32[]{:S(2)}) copy-start(bf16[512,512]{1,0:T(8,128)(2,1)} %first_ref.1) | copy-start | bytes 1572868
  56.4 8.5 %collective-permute-start.2 = (bf16[88,256]{1,0:T(8,128)(2,1)S(1)}, bf16[88,256]{1,0:T(8,128)(2,1)S(1)}, u32[]{:S(2)}, u32[]{:S(2)}) collective-permute-start(bf16[88,256]{1,0:T(8,128)(2,1)S(1)} %get-tuple-element.54), channel_id=1, source_target_pairs={{0,1},{1,2},{2,3},{3,4},{4,5},{5,6},{6,7},{7,8},{8,9},{9,10},{10,1... | collective-permute-start | bytes 135176 | tf_op jit(solution)/shard_map/ppermute | solution.py:468
  58.3 10.2 %collective-permute-start.3 = (bf16[88,256]{1,0:T(8,128)(2,1)S(1)}, bf16[88,256]{1,0:T(8,128)(2,1)S(1)}, u32[]{:S(2)}, u32[]{:S(2)}) collective-permute-start(bf16[88,256]{1,0:T(8,128)(2,1)S(1)} %get-tuple-element.55), channel_id=1, source_target_pairs={{0,15},{1,0},{2,1},{3,2},{4,3},{5,4},{6,5},{7,6},{8,7},{9,8},{10,9... | collective-permute-start | bytes 135176 | tf_op jit(solution)/shard_map/ppermute | solution.py:468
